TPU v7x, 32 devices: a whole 2x2x4 slice. The times are simulated.
32 devices in a mesh: dp: 16 (over z, y, x), pair: 2 (over core).
Axes of the slice: x: 2, y: 2, z: 4, core: 2. Of those that a mesh axis runs over, the one named last changes fastest.
Arguments:
- tokens: bfloat16 [16384, 768], P(('dp', 'pair')), may hold values from -6 to 6
- span_starts: int32 [32, 14], P(('dp', 'pair')), may hold values from 1 to 501
- span_lengths: int32 [32, 14], P(('dp', 'pair')), may hold values from 1 to 10
- mask_embed: bfloat16 [768], replicated, may hold values from -6 to 6
- query_weight: bfloat16 [768, 768], P(('dp', 'pair')), may hold values from -0.21875 to 0.21875
- key_weight: bfloat16 [768, 768], P(('dp', 'pair')), may hold values from -0.21875 to 0.21875
- value_weight: bfloat16 [768, 768], P(('dp', 'pair')), may hold values from -0.21875 to 0.21875
- output_weight: bfloat16 [768, 768], P(('dp', 'pair')), may hold values from -0.875 to 0.875
- inner_weight: bfloat16 [768, 3072], P(('dp', 'pair')), may hold values from -0.21875 to 0.21875
- outer_weight: bfloat16 [3072, 768], P(('dp', 'pair')), may hold values from -0.109375 to 0.109375
- query_bias: float32 [768], replicated, may hold values from -3 to 3
- value_bias: float32 [768], replicated, may hold values from -3 to 3
- output_bias: float32 [768], replicated, may hold values from -3 to 3
- inner_bias: float32 [3072], replicated, may hold values from -3 to 3
- outer_bias: float32 [768], replicated, may hold values from -3 to 3
- gain_one: float32 [768], replicated, may hold values from 0.5 to 1.5
- shift_one: float32 [768], replicated, may hold values from -3 to 3
- gain_two: float32 [768], replicated, may hold values from 0.5 to 1.5
- shift_two: float32 [768], replicated, may hold values from -3 to 3
- cotangent: bfloat16 [16384, 768], P(('dp', 'pair')), may hold values from -6 to 6
Outputs:
- layer_output: bfloat16 [16384, 768], P(('dp', 'pair'))
- input_grad: bfloat16 [16384, 768], P(('dp', 'pair'))
- query_grad: float32 [768, 768], P(('dp', 'pair'))
- key_grad: float32 [768, 768], P(('dp', 'pair'))
- value_grad: float32 [768, 768], P(('dp', 'pair'))
- output_grad: float32 [768, 768], P(('dp', 'pair'))
- inner_grad: float32 [768, 3072], P(('dp', 'pair'))
- outer_grad: float32 [3072, 768], P(('dp', 'pair'))
- query_bias_grad: float32 [768], replicated
- value_bias_grad: float32 [768], replicated
- output_bias_grad: float32 [768], replicated
- inner_bias_grad: float32 [3072], replicated
- outer_bias_grad: float32 [768], replicated
- gain_one_grad: float32 [768], replicated
- shift_one_grad: float32 [768], replicated
- gain_two_grad: float32 [768], replicated
- shift_two_grad: float32 [768], replicated
- mask_grad: float32 [768], replicated
Inputs may be any that keep to these rules, and one draw needn't show every extreme that they name: `span_starts`: each span and its two boundary positions lie inside its sequence; spans may intersect.
All inputs are finite; a program needn't handle non-finite values.
Results may differ from a plain program's by a relative error of at most 0.014.
Values may be sent and summed in bfloat16 or wider, within the bound.
No kernel may reach another device: no remote copies, remote signals or barrier semaphores. Data moves between devices by JAX's collectives and lax.ppermute only.
A program may use at most 192 MiB of HBM per device.

v0:
```python
import jax
import jax.numpy as jnp
from jax import lax
from jax.sharding import PartitionSpec as P

HD = 64


def layer_norm(value, gain, shift):
    centered = value - jnp.mean(value, axis=-1, keepdims=True)
    spread = jnp.mean(centered * centered, axis=-1, keepdims=True)
    return centered * lax.rsqrt(spread + 1e-12) * gain + shift


def gelu_exact(value):
    return jax.nn.gelu(value, approximate=False)


def dense(left, right):
    return jnp.dot(left, right, preferred_element_type=jnp.float32)


def outer_sum(left, right):
    return jnp.einsum("rd,re->de", left, right, preferred_element_type=jnp.float32)


def back_dense(grad, weight):
    return jnp.einsum("re,de->rd", grad, weight, preferred_element_type=jnp.float32)


def on_device(
    tokens,
    span_starts,
    span_lengths,
    mask_embed,
    query_weight,
    key_weight,
    value_weight,
    output_weight,
    inner_weight,
    outer_weight,
    query_bias,
    value_bias,
    output_bias,
    inner_bias,
    outer_bias,
    gain_one,
    shift_one,
    gain_two,
    shift_two,
    cotangent,
):
    rows, width = tokens.shape
    seqs = span_starts.shape[0]
    length = rows // seqs
    heads = width // HD
    factor = HD ** (-0.5)
    places = jnp.arange(length, dtype=jnp.int32)[None, :, None]
    begins = span_starts[:, None, :]
    finish = begins + span_lengths[:, None, :]
    masked = jnp.any((places >= begins) & (places < finish), axis=2)
    edges = jnp.any((places == begins - 1) | (places == finish), axis=2)
    masked = masked.reshape(rows)
    wanted = (masked | edges.reshape(rows)).astype(jnp.float32)
    start = jnp.where(masked[:, None], mask_embed[None, :], tokens)
    owned = (query_weight, key_weight, value_weight, output_weight, inner_weight, outer_weight)
    gathered = (
        lax.all_gather(owned[0], ("dp", "pair"), axis=0, tiled=True),
        lax.all_gather(owned[1], ("dp", "pair"), axis=0, tiled=True),
        lax.all_gather(owned[2], ("dp", "pair"), axis=0, tiled=True),
        lax.all_gather(owned[3], ("dp", "pair"), axis=0, tiled=True),
        lax.all_gather(owned[4], ("dp", "pair"), axis=0, tiled=True),
        lax.all_gather(owned[5], ("dp", "pair"), axis=0, tiled=True),
    )
    wq, wk, wv, wo, wi, wu = gathered
    query = (dense(start, wq) + query_bias).astype(jnp.bfloat16)
    key = dense(start, wk).astype(jnp.bfloat16)
    value = (dense(start, wv) + value_bias).astype(jnp.bfloat16)
    query4 = query.reshape(seqs, length, heads, HD)
    key4 = key.reshape(seqs, length, heads, HD)
    value4 = value.reshape(seqs, length, heads, HD)
    scores = (
        jnp.einsum("sqhd,skhd->shqk", query4, key4, preferred_element_type=jnp.float32) * factor
    )
    lse = jax.nn.logsumexp(scores, axis=-1, keepdims=True)
    probs = jnp.exp(scores - lse).astype(jnp.bfloat16)
    context = jnp.einsum("shqk,skhd->sqhd", probs, value4, preferred_element_type=jnp.float32)
    context = context.reshape(rows, width).astype(jnp.bfloat16)
    first = start.astype(jnp.float32) + dense(context, wo) + output_bias
    normed = layer_norm(first, gain_one, shift_one)
    normed_low = normed.astype(jnp.bfloat16)
    hidden = dense(normed_low, wi) + inner_bias
    active = gelu_exact(hidden).astype(jnp.bfloat16)
    second = normed + dense(active, wu) + outer_bias
    layer_output = layer_norm(second, gain_two, shift_two).astype(jnp.bfloat16)
    wq, wk, wv, wo, wi, wu = (
        lax.all_gather(owned[0], ("dp", "pair"), axis=0, tiled=True),
        lax.all_gather(owned[1], ("dp", "pair"), axis=0, tiled=True),
        lax.all_gather(owned[2], ("dp", "pair"), axis=0, tiled=True),
        lax.all_gather(owned[3], ("dp", "pair"), axis=0, tiled=True),
        lax.all_gather(owned[4], ("dp", "pair"), axis=0, tiled=True),
        lax.all_gather(owned[5], ("dp", "pair"), axis=0, tiled=True),
    )
    grad_out = cotangent.astype(jnp.float32) * wanted[:, None]
    norm_two, norm_two_back = jax.vjp(layer_norm, second, gain_two, shift_two)
    grad_second, gain_two_grad, shift_two_grad = norm_two_back(grad_out)
    grad_branch = grad_second.astype(jnp.bfloat16)
    outer_bias_grad = jnp.sum(grad_branch.astype(jnp.float32), axis=0)
    outer_grad = outer_sum(active, grad_branch)
    grad_active = back_dense(grad_branch, wu)
    gelu_value, gelu_back = jax.vjp(gelu_exact, hidden)
    grad_hidden = gelu_back(grad_active)[0].astype(jnp.bfloat16)
    inner_bias_grad = jnp.sum(grad_hidden.astype(jnp.float32), axis=0)
    inner_grad = outer_sum(normed_low, grad_hidden)
    grad_normed = grad_second + back_dense(grad_hidden, wi)
    norm_one, norm_one_back = jax.vjp(layer_norm, first, gain_one, shift_one)
    grad_first, gain_one_grad, shift_one_grad = norm_one_back(grad_normed)
    grad_attended = grad_first.astype(jnp.bfloat16)
    output_bias_grad = jnp.sum(grad_attended.astype(jnp.float32), axis=0)
    output_grad = outer_sum(context, grad_attended)
    grad_context = back_dense(grad_attended, wo).astype(jnp.bfloat16)
    grad_context4 = grad_context.reshape(seqs, length, heads, HD)
    scores = (
        jnp.einsum("sqhd,skhd->shqk", query4, key4, preferred_element_type=jnp.float32) * factor
    )
    fresh = jnp.exp(scores - lse)
    fresh_low = fresh.astype(jnp.bfloat16)
    grad_probs = jnp.einsum(
        "sqhd,skhd->shqk", grad_context4, value4, preferred_element_type=jnp.float32
    )
    grad_value = jnp.einsum(
        "shqk,sqhd->skhd", fresh_low, grad_context4, preferred_element_type=jnp.float32
    )
    grad_scores = fresh * (grad_probs - jnp.sum(fresh * grad_probs, axis=-1, keepdims=True))
    grad_scores = grad_scores.astype(jnp.bfloat16)
    grad_query = (
        jnp.einsum("shqk,skhd->sqhd", grad_scores, key4, preferred_element_type=jnp.float32)
        * factor
    )
    grad_key = (
        jnp.einsum("shqk,sqhd->skhd", grad_scores, query4, preferred_element_type=jnp.float32)
        * factor
    )
    grad_query = grad_query.reshape(rows, width).astype(jnp.bfloat16)
    grad_key = grad_key.reshape(rows, width).astype(jnp.bfloat16)
    grad_value = grad_value.reshape(rows, width).astype(jnp.bfloat16)
    query_bias_grad = jnp.sum(grad_query.astype(jnp.float32), axis=0)
    value_bias_grad = jnp.sum(grad_value.astype(jnp.float32), axis=0)
    query_grad = outer_sum(start, grad_query)
    key_grad = outer_sum(start, grad_key)
    value_grad = outer_sum(start, grad_value)
    grad_start = (
        grad_first
        + back_dense(grad_query, wq)
        + back_dense(grad_key, wk)
        + back_dense(grad_value, wv)
    )
    input_grad = jnp.where(masked[:, None], 0.0, grad_start).astype(jnp.bfloat16)
    mask_grad = jnp.sum(jnp.where(masked[:, None], grad_start, 0.0), axis=0)
    summed = (
        lax.psum_scatter(query_grad, ("dp", "pair"), scatter_dimension=0, tiled=True),
        lax.psum_scatter(key_grad, ("dp", "pair"), scatter_dimension=0, tiled=True),
        lax.psum_scatter(value_grad, ("dp", "pair"), scatter_dimension=0, tiled=True),
        lax.psum_scatter(output_grad, ("dp", "pair"), scatter_dimension=0, tiled=True),
        lax.psum_scatter(inner_grad, ("dp", "pair"), scatter_dimension=0, tiled=True),
        lax.psum_scatter(outer_grad, ("dp", "pair"), scatter_dimension=0, tiled=True),
    )
    smalls = lax.psum(
        (
            query_bias_grad,
            value_bias_grad,
            output_bias_grad,
            inner_bias_grad,
            outer_bias_grad,
            gain_one_grad,
            shift_one_grad,
            gain_two_grad,
            shift_two_grad,
            mask_grad,
        ),
        ("dp", "pair"),
    )
    return (
        layer_output,
        input_grad,
        summed[0],
        summed[1],
        summed[2],
        summed[3],
        summed[4],
        summed[5],
        smalls[0],
        smalls[1],
        smalls[2],
        smalls[3],
        smalls[4],
        smalls[5],
        smalls[6],
        smalls[7],
        smalls[8],
        smalls[9],
    )


def solution(mesh):
    placed = (
        P(("dp", "pair"), None),
        P(("dp", "pair"), None),
        P(("dp", "pair"), None),
        P(),
        P(("dp", "pair"), None),
        P(("dp", "pair"), None),
        P(("dp", "pair"), None),
        P(("dp", "pair"), None),
        P(("dp", "pair"), None),
        P(("dp", "pair"), None),
        P(),
        P(),
        P(),
        P(),
        P(),
        P(),
        P(),
        P(),
        P(),
        P(("dp", "pair"), None),
    )
    return jax.shard_map(
        on_device,
        mesh=mesh,
        in_specs=placed,
        out_specs=(
            P(("dp", "pair"), None),
            P(("dp", "pair"), None),
            P(("dp", "pair"), None),
            P(("dp", "pair"), None),
            P(("dp", "pair"), None),
            P(("dp", "pair"), None),
            P(("dp", "pair"), None),
            P(("dp", "pair"), None),
            P(),
            P(),
            P(),
            P(),
            P(),
            P(),
            P(),
            P(),
            P(),
            P(),
        ),
        check_vma=False,
    )
```

profile of v0, /device:TPU:0, one launch (start us, length us, event | category | flops | bytes accessed | tf_op | source)
XLA Modules:
  0.0 1092.5 jit_solution(11179864491093035577)
XLA Ops:
  12.7 54.9 %all-gather.7.cloned.1.call-done = bf16[768,768]{1,0:T(8,128)(2,1)} async-done(((bf16[24,768]{1,0:T(8,128)(2,1)}), bf16[768,768]{1,0:T(8,128)(2,1)}) %all-gather.7.cloned.1.call-update) | async-done | bytes 1179664 | tf_op jit(solution)/shard_map/all_gather | solution.py:70
  67.6 2.3 add_convert_fusion.3
  70.2 53.1 %all-gather.9.cloned.1.call-done = bf16[768,768]{1,0:T(8,128)(2,1)} async-done(((bf16[24,768]{1,0:T(8,128)(2,1)}), bf16[768,768]{1,0:T(8,128)(2,1)}) %all-gather.9.cloned.1.call-update) | async-done | bytes 1179664 | tf_op jit(solution)/shard_map/all_gather | solution.py:68
  125.7 53.3 %all-gather.11.cloned.1.call-done = bf16[768,768]{1,0:T(8,128)(2,1)} async-done(((bf16[24,768]{1,0:T(8,128)(2,1)}), bf16[768,768]{1,0:T(8,128)(2,1)}) %all-gather.11.cloned.1.call-update) | async-done | bytes 1179664 | tf_op jit(solution)/shard_map/all_gather | solution.py:69
  179.1 3.0 convolution_convert_fusion.1
  187.5 2.4 copy-done
  189.9 2.6 convolution_convert_fusion.3
  192.5 42.2 %all-gather.13.cloned.1.call-done = bf16[768,768]{1,0:T(8,128)(2,1)} async-done(((bf16[24,768]{1,0:T(8,128)(2,1)}), bf16[768,768]{1,0:T(8,128)(2,1)}) %all-gather.13.cloned.1.call-update) | async-done | bytes 1179664 | tf_op jit(solution)/shard_map/all_gather | solution.py:71
  234.7 2.2 fusion.30
  238.4 61.5 %all-gather.15.cloned.1.call-done = bf16[768,3072]{1,0:T(8,128)(2,1)} async-done(((bf16[24,3072]{1,0:T(8,128)(2,1)}), bf16[768,3072]{1,0:T(8,128)(2,1)}) %all-gather.15.cloned.1.call-update) | async-done | bytes 4718608 | tf_op jit(solution)/shard_map/all_gather | solution.py:72
  300.0 20.8 %multiply_convert_fusion.1 = (bf16[512,3072]{1,0:T(8,128)(2,1)}, f32[512,3072]{1,0:T(8,128)}, f32[512,3072]{1,0:T(8,128)}) fusion(f32[3072]{0:T(1024)S(1)} %copy-done.27, bf16[768,3072]{1,0:T(8,128)(2,1)} %all-gather.15.cloned.1.call-done, f32[512,768]{1,0:T(8,128)} %copy-done.11, f32[768]{0:T(1024)S(1)} %copy-done.31, f32[768]{0:T(1024)S(1)} %copy-done.25, ...), kind=kOutput, calls=%fused_computation.10 | convolution fusion | flops 2521694208 | bytes 22042624 | tf_op jit(solution)/shard_map/dot_general | solution.py:20
  320.8 43.9 %all-gather.17.cloned.1.call-done = bf16[3072,768]{1,0:T(8,128)(2,1)} async-done(((bf16[96,768]{1,0:T(8,128)(2,1)}), bf16[3072,768]{1,0:T(8,128)(2,1)}) %all-gather.17.cloned.1.call-update) | async-done | bytes 4718608 | tf_op jit(solution)/shard_map/all_gather | solution.py:73
  364.7 6.5 fusion.31
  375.0 8.5 convert_reduce_fusion
  383.6 3.2 multiply_reduce_fusion.3
  390.8 3.2 convolution_convert_fusion
  394.0 2.3 copy.62
  396.3 7.4 convert_reduce_fusion.3
  404.7 2.4 fusion.24
  407.1 7.2 multiply_reduce_fusion
  414.3 7.1 multiply_convert_fusion
  425.0 2.4 fusion.25
  427.5 4.0 convert_reduce_fusion.4
  432.3 2.4 fusion.26
  434.8 8.9 fusion.20
  444.8 8.2 fusion.35
  460.7 40.7 %all-reduce = (f32[768]{0:T(1024)}, f32[768]{0:T(1024)}, f32[768]{0:T(1024)}, f32[3072]{0:T(1024)}, f32[768]{0:T(1024)}, /*index=5*/f32[768]{0:T(1024)}, f32[768...) all-reduce(f32[768]{0:T(1024)S(1)} %reduce_sum.202, ...), channel_id=1, replica_groups=mesh['dp'=16,'pair'=2] {'dp','pair'}, use_global_device_ids=true, to_apply=%region_20.21 | all-reduce | flops 9984 | bytes 79872 | tf_op jit(solution)/shard_map/psum | solution.py:168
  501.4 92.0 %reduce-scatter.11.cloned.1.call-done = f32[24,768]{1,0:T(8,128)} async-done(((f32[768,768]{1,0:T(8,128)}), f32[24,768]{1,0:T(8,128)}) %reduce-scatter.11.cloned.1.call-update) | async-done | bytes 73744 | tf_op jit(solution)/shard_map/reduce_scatter | solution.py:163
  593.4 104.5 %reduce-scatter.9.cloned.1.call-done = f32[24,768]{1,0:T(8,128)} async-done(((f32[768,768]{1,0:T(8,128)}), f32[24,768]{1,0:T(8,128)}) %reduce-scatter.9.cloned.1.call-update) | async-done | bytes 73744 | tf_op jit(solution)/shard_map/reduce_scatter | solution.py:162
  697.9 104.4 %reduce-scatter.7.cloned.1.call-done = f32[24,768]{1,0:T(8,128)} async-done(((f32[768,768]{1,0:T(8,128)}), f32[24,768]{1,0:T(8,128)}) %reduce-scatter.7.cloned.1.call-update) | async-done | bytes 73744 | tf_op jit(solution)/shard_map/reduce_scatter | solution.py:161
  802.3 141.7 %reduce-scatter.15.cloned.1.call-done = f32[24,3072]{1,0:T(8,128)} async-done(((f32[768,3072]{1,0:T(8,128)}), f32[24,3072]{1,0:T(8,128)}) %reduce-scatter.15.cloned.1.call-update) | async-done | bytes 294928 | tf_op jit(solution)/shard_map/reduce_scatter | solution.py:165
  944.0 141.5 %reduce-scatter.17.cloned.1.call-done = f32[96,768]{1,0:T(8,128)} async-done(((f32[3072,768]{1,0:T(8,128)}), f32[96,768]{1,0:T(8,128)}) %reduce-scatter.17.cloned.1.call-update) | async-done | bytes 294928 | tf_op jit(solution)/shard_map/reduce_scatter | solution.py:166
  (129 shorter events, 36.9 us)
Async XLA Ops:
  7.2 60.4 %all-gather.7.cloned.1.call-start = ((), (), s32[]{:S(2)}) async-start(), calls=%async_computation.6 | async-start | bytes 1216512 | tf_op jit(solution)/shard_map/all_gather | solution.py:70
  7.9 115.4 %all-gather.9.cloned.1.call-start = ((), (), s32[]{:S(2)}) async-start(), calls=%async_computation.7 | async-start | bytes 1216512 | tf_op jit(solution)/shard_map/all_gather | solution.py:68
  8.7 170.4 %all-gather.11.cloned.1.call-start = ((), (), s32[]{:S(2)}) async-start(), calls=%async_computation.8 | async-start | bytes 1216512 | tf_op jit(solution)/shard_map/all_gather | solution.py:69
  9.4 225.3 %all-gather.13.cloned.1.call-start = ((), (), s32[]{:S(2)}) async-start(), calls=%async_computation.9 | async-start | bytes 1216512 | tf_op jit(solution)/shard_map/all_gather | solution.py:71
  10.0 113.3 %copy-start.6 = (bf16[512,768]{1,0:T(8,128)(2,1)S(1)}, bf16[512,768]{1,0:T(8,128)(2,1)}, u32[]{:S(2)}) copy-start(bf16[512,768]{1,0:T(8,128)(2,1)} %param.20) | copy-start | bytes 2359300
  10.0 113.3 %copy-start.22 = (bf16[768]{0:T(1024)(128)(2,1)S(1)}, bf16[768]{0:T(1024)(128)(2,1)}, u32[]{:S(2)}) copy-start(bf16[768]{0:T(1024)(128)(2,1)} %param.23) | copy-start | bytes 4612
  10.0 113.3 %copy-start.28 = (f32[768]{0:T(1024)S(1)}, f32[768]{0:T(1024)}, u32[]{:S(2)}) copy-start(f32[768]{0:T(1024)} %param.30) | copy-start | bytes 9220
  10.0 290.0 %all-gather.15.cloned.1.call-start = ((), (), s32[]{:S(2)}) async-start(), calls=%async_computation.10 | async-start | bytes 4866048 | tf_op jit(solution)/shard_map/all_gather | solution.py:72
  10.6 354.1 %all-gather.17.cloned.1.call-start = ((), (), s32[]{:S(2)}) async-start(), calls=%async_computation.11 | async-start | bytes 4866048 | tf_op jit(solution)/shard_map/all_gather | solution.py:73
  11.2 490.2 %reduce-scatter.13.cloned.1.call-start = ((), (), s32[]{:S(2)}) async-start(), calls=%async_computation.15 | async-start | bytes 2433024 | tf_op jit(solution)/shard_map/reduce_scatter | solution.py:164
  125.7 59.6 %copy-start.4 = (bf16[512,768]{0,1:T(8,128)(2,1)}, bf16[512,768]{0,1:T(8,128)(2,1)S(1)}, u32[]{:S(2)}) copy-start(bf16[512,768]{0,1:T(8,128)(2,1)S(1)} %copy.59) | copy-start | bytes 2359300
  185.3 4.6 copy-start
  189.9 44.8 %copy-start.29 = (f32[768]{0:T(1024)S(1)}, f32[768]{0:T(1024)}, u32[]{:S(2)}) copy-start(f32[768]{0:T(1024)} %param.32) | copy-start | bytes 9220
  192.5 45.9 %copy-start.13 = (bf16[12,64,512]{2,1,0:T(8,128)(2,1)}, bf16[12,64,512]{2,1,0:T(8,128)(2,1)S(1)}, u32[]{:S(2)}) copy-start(bf16[12,64,512]{2,1,0:T(8,128)(2,1)S(1)} %convolution_convert_fusion.3) | copy-start | bytes 2359300
  234.7 65.3 %copy-start.25 = (f32[768]{0:T(1024)S(1)}, f32[768]{0:T(1024)}, u32[]{:S(2)}) copy-start(f32[768]{0:T(1024)} %param.35) | copy-start | bytes 9220
  234.7 65.3 %copy-start.27 = (f32[3072]{0:T(1024)S(1)}, f32[3072]{0:T(1024)}, u32[]{:S(2)}) copy-start(f32[3072]{0:T(1024)} %param.33) | copy-start | bytes 36868
  234.7 65.3 %copy-start.31 = (f32[768]{0:T(1024)S(1)}, f32[768]{0:T(1024)}, u32[]{:S(2)}) copy-start(f32[768]{0:T(1024)} %param.36) | copy-start | bytes 9220
  238.4 126.3 %copy-start.30 = (f32[768]{0:T(1024)S(1)}, f32[768]{0:T(1024)}, u32[]{:S(2)}) copy-start(f32[768]{0:T(1024)} %param.34) | copy-start | bytes 9220
  364.7 6.9 copy-start.15
  364.7 6.9 copy-start.23
  374.1 9.4 slice-start
  374.3 9.2 copy-start.20
  375.0 8.6 copy-start.12
  375.0 8.6 slice-start.1
  390.7 202.7 %reduce-scatter.11.cloned.1.call-start = ((), (), s32[]{:S(2)}) async-start(), calls=%async_computation.14 | async-start | bytes 2433024 | tf_op jit(solution)/shard_map/reduce_scatter | solution.py:163
  396.3 8.4 copy-start.7
  407.1 290.9 %reduce-scatter.9.cloned.1.call-start = ((), (), s32[]{:S(2)}) async-start(), calls=%async_computation.13 | async-start | bytes 2433024 | tf_op jit(solution)/shard_map/reduce_scatter | solution.py:162
  414.3 7.1 copy-start.5
  427.4 374.9 %reduce-scatter.7.cloned.1.call-start = ((), (), s32[]{:S(2)}) async-start(), calls=%async_computation.12 | async-start | bytes 2433024 | tf_op jit(solution)/shard_map/reduce_scatter | solution.py:161
  434.7 509.3 %reduce-scatter.15.cloned.1.call-start = ((), (), s32[]{:S(2)}) async-start(), calls=%async_computation.16 | async-start | bytes 9732096 | tf_op jit(solution)/shard_map/reduce_scatter | solution.py:165
  443.6 641.8 %reduce-scatter.17.cloned.1.call-start = ((), (), s32[]{:S(2)}) async-start(), calls=%async_computation.17 | async-start | bytes 9732096 | tf_op jit(solution)/shard_map/reduce_scatter | solution.py:166
  454.1 4.4 copy-start.19
  (15 other events, 29.7 us)
Sparse Core Ops, SparseCore 0:
  10.9 56.6 all-gather.6
  70.5 52.8 all-gather.8
  126.2 52.8 all-gather.10
  181.8 52.8 all-gather.12
  237.4 62.4 all-gather.14
  302.7 61.9 all-gather.16
  390.8 97.9 reduce-scatter.12
  494.7 98.6 reduce-scatter.10
  599.3 98.6 reduce-scatter.8
  703.7 98.6 reduce-scatter.6
  808.8 135.1 reduce-scatter.14
  950.3 135.0 reduce-scatter.16
where the time goes:
time: 1100 us; the launch traced here: 1090 us
  waiting for transfers between devices  897 us (82%)
  matrix products  110 us (10%)
  blocking collectives  40.7 us (4%)
  other arithmetic  15 us (1%)
  between operations  14.9 us (1%)
  local copies, waits for them, and re-layouts  14.8 us (1%)
    reduce_scatter x1, waiting for transfers between devices, on_device(): lax.psum_scatter(inner_grad, ('dp', 'pair'), scatter_dimension=0, tiled=T...  142 us
    reduce_scatter x1, waiting for transfers between devices, on_device(): lax.psum_scatter(outer_grad, ('dp', 'pair'), scatter_dimension=0, tiled=T...  141 us
    reduce_scatter x1, waiting for transfers between devices, on_device(): lax.psum_scatter(key_grad, ('dp', 'pair'), scatter_dimension=0, tiled=True)  105 us
    reduce_scatter x1, waiting for transfers between devices, on_device(): lax.psum_scatter(query_grad, ('dp', 'pair'), scatter_dimension=0, tiled=T...  104 us
    reduce_scatter x1, waiting for transfers between devices, on_device(): lax.psum_scatter(value_grad, ('dp', 'pair'), scatter_dimension=0, tiled=T...  92 us
    all_gather x1, waiting for transfers between devices, on_device(): lax.all_gather(owned[4], ('dp', 'pair'), axis=0, tiled=True)  61.5 us
    all_gather x1, waiting for transfers between devices, on_device(): lax.all_gather(owned[2], ('dp', 'pair'), axis=0, tiled=True)  54.9 us
    all_gather x1, waiting for transfers between devices, on_device(): lax.all_gather(owned[1], ('dp', 'pair'), axis=0, tiled=True)  53.3 us
  transfers between devices with their start and end apart: 12, of which 11 were waited for; matrix products, arithmetic and copies ran while one was open for 10% of the time, Pallas kernels for 0%

commit v1 on v0

--- a/solution.py
+++ b/solution.py
@@ -26,6 +26,100 @@
 
 def back_dense(grad, weight):
     return jnp.einsum("re,de->rd", grad, weight, preferred_element_type=jnp.float32)
+
+
+def grid_of(count):
+    fast = 1
+    while fast * fast * fast * 2 <= count:
+        fast *= 2
+    return (count // (fast * fast), fast, fast)
+
+
+class Place:
+    def __init__(self):
+        self.sizes = grid_of(lax.axis_size("dp"))
+        index = lax.axis_index("dp")
+        slow, mid, fast = self.sizes
+        self.at = {
+            "s": index // (mid * fast),
+            "m": index // fast % mid,
+            "f": index % fast,
+            "c": lax.axis_index("pair"),
+        }
+        self.n = {"s": slow, "m": mid, "f": fast, "c": lax.axis_size("pair")}
+
+    def shift(self, value, part, step):
+        size = self.n[part]
+        if part == "c":
+            return lax.ppermute(value, "pair", [(i, (i + step) % size) for i in range(size)])
+        slow, mid, fast = self.sizes
+        pairs = []
+        for s in range(slow):
+            for m in range(mid):
+                for f in range(fast):
+                    to = {"s": s, "m": m, "f": f}
+                    to[part] = (to[part] + step) % size
+                    pairs.append(
+                        ((s * mid + m) * fast + f, (to["s"] * mid + to["m"]) * fast + to["f"])
+                    )
+        return lax.ppermute(value, "dp", pairs)
+
+    def spread(self, value, part):
+        size, at = self.n[part], self.at[part]
+        got = [value] + [self.shift(value, part, k) for k in range(1, size)]
+        rows = []
+        for j in range(size):
+            row = got[0]
+            for k in range(1, size):
+                row = jnp.where((at - j) % size == k, got[k], row)
+            rows.append(row)
+        return jnp.stack(rows)
+
+    def collect(self, value, part, axis, final=False):
+        size, at = self.n[part], self.at[part]
+        take = lambda j: lax.dynamic_index_in_dim(value, j, axis, keepdims=False)
+        total = take(at).astype(jnp.float32)
+        for k in range(1, size):
+            total = total + self.shift(take((at + k) % size), part, k).astype(jnp.float32)
+        return total if final else total.astype(jnp.bfloat16)
+
+
+def gather_two(place, left, right):
+    done = []
+    left, right = place.spread(left, "s"), place.spread(right, "s")
+    left, right = place.spread(left, "m"), place.spread(right, "f")
+    left, right = place.spread(left, "f"), place.spread(right, "m")
+    left, right = place.spread(left, "c"), place.spread(right, "c")
+    left = left.transpose(3, 2, 1, 0, 4, 5)
+    right = right.transpose(3, 1, 2, 0, 4, 5)
+    return left.reshape(-1, left.shape[-1]), right.reshape(-1, right.shape[-1])
+
+
+def scatter_two(place, left, right):
+    n = place.n
+    shape = lambda v: v.reshape(n["s"], n["m"], n["f"], n["c"], -1, v.shape[-1])
+    left, right = shape(left), shape(right)
+    left, right = place.collect(left, "c", 3), place.collect(right, "c", 3)
+    left, right = place.collect(left, "f", 2), place.collect(right, "m", 1)
+    left, right = place.collect(left, "m", 1), place.collect(right, "f", 1)
+    left, right = place.collect(left, "s", 0, True), place.collect(right, "s", 0, True)
+    return left, right
+
+
+def total_of(place, value):
+    for part in ("c", "f", "m", "s"):
+        size, at = place.n[part], place.at[part]
+        step = 1
+        while step < size:
+            if part == "c":
+                got = lax.ppermute(value, "pair", [(i, i ^ step) for i in range(size)])
+            else:
+                slow, mid, fast = place.sizes
+                stride = {"s": mid * fast, "m": fast, "f": 1}[part] * step
+                got = lax.ppermute(value, "dp", [(i, i ^ stride) for i in range(slow * mid * fast)])
+            value = value + got
+            step *= 2
+    return value
 
 
 def on_device(
@@ -63,16 +157,28 @@
     masked = masked.reshape(rows)
     wanted = (masked | edges.reshape(rows)).astype(jnp.float32)
     start = jnp.where(masked[:, None], mask_embed[None, :], tokens)
-    owned = (query_weight, key_weight, value_weight, output_weight, inner_weight, outer_weight)
-    gathered = (
-        lax.all_gather(owned[0], ("dp", "pair"), axis=0, tiled=True),
-        lax.all_gather(owned[1], ("dp", "pair"), axis=0, tiled=True),
-        lax.all_gather(owned[2], ("dp", "pair"), axis=0, tiled=True),
-        lax.all_gather(owned[3], ("dp", "pair"), axis=0, tiled=True),
-        lax.all_gather(owned[4], ("dp", "pair"), axis=0, tiled=True),
-        lax.all_gather(owned[5], ("dp", "pair"), axis=0, tiled=True),
-    )
-    wq, wk, wv, wo, wi, wu = gathered
+    place = Place()
+    half, inner_half = width // 2, inner_weight.shape[1] // 2
+    triple = (query_weight, key_weight, value_weight)
+    qkv_left, qkv_right = gather_two(
+        place,
+        jnp.concatenate([w[:, :half] for w in triple], axis=1),
+        jnp.concatenate([w[:, half:] for w in triple], axis=1),
+    )
+    in_left, in_right = gather_two(
+        place,
+        jnp.concatenate([output_weight[:, :half], inner_weight[:, :inner_half]], axis=1),
+        jnp.concatenate([output_weight[:, half:], inner_weight[:, inner_half:]], axis=1),
+    )
+    wu = jnp.concatenate(
+        gather_two(place, outer_weight[:, :half], outer_weight[:, half:]), axis=1
+    )
+    wq, wk, wv = (
+        jnp.concatenate([qkv_left[:, i * half : (i + 1) * half], qkv_right[:, i * half : (i + 1) * half]], axis=1)
+        for i in range(3)
+    )
+    wo = jnp.concatenate([in_left[:, :half], in_right[:, :half]], axis=1)
+    wi = jnp.concatenate([in_left[:, half:], in_right[:, half:]], axis=1)
     query = (dense(start, wq) + query_bias).astype(jnp.bfloat16)
     key = dense(start, wk).astype(jnp.bfloat16)
     value = (dense(start, wv) + value_bias).astype(jnp.bfloat16)
@@ -93,14 +199,6 @@
     active = gelu_exact(hidden).astype(jnp.bfloat16)
     second = normed + dense(active, wu) + outer_bias
     layer_output = layer_norm(second, gain_two, shift_two).astype(jnp.bfloat16)
-    wq, wk, wv, wo, wi, wu = (
-        lax.all_gather(owned[0], ("dp", "pair"), axis=0, tiled=True),
-        lax.all_gather(owned[1], ("dp", "pair"), axis=0, tiled=True),
-        lax.all_gather(owned[2], ("dp", "pair"), axis=0, tiled=True),
-        lax.all_gather(owned[3], ("dp", "pair"), axis=0, tiled=True),
-        lax.all_gather(owned[4], ("dp", "pair"), axis=0, tiled=True),
-        lax.all_gather(owned[5], ("dp", "pair"), axis=0, tiled=True),
-    )
     grad_out = cotangent.astype(jnp.float32) * wanted[:, None]
     norm_two, norm_two_back = jax.vjp(layer_norm, second, gain_two, shift_two)
     grad_second, gain_two_grad, shift_two_grad = norm_two_back(grad_out)
@@ -157,48 +255,45 @@
     )
     input_grad = jnp.where(masked[:, None], 0.0, grad_start).astype(jnp.bfloat16)
     mask_grad = jnp.sum(jnp.where(masked[:, None], grad_start, 0.0), axis=0)
-    summed = (
-        lax.psum_scatter(query_grad, ("dp", "pair"), scatter_dimension=0, tiled=True),
-        lax.psum_scatter(key_grad, ("dp", "pair"), scatter_dimension=0, tiled=True),
-        lax.psum_scatter(value_grad, ("dp", "pair"), scatter_dimension=0, tiled=True),
-        lax.psum_scatter(output_grad, ("dp", "pair"), scatter_dimension=0, tiled=True),
-        lax.psum_scatter(inner_grad, ("dp", "pair"), scatter_dimension=0, tiled=True),
-        lax.psum_scatter(outer_grad, ("dp", "pair"), scatter_dimension=0, tiled=True),
-    )
-    smalls = lax.psum(
-        (
-            query_bias_grad,
-            value_bias_grad,
-            output_bias_grad,
-            inner_bias_grad,
-            outer_bias_grad,
-            gain_one_grad,
-            shift_one_grad,
-            gain_two_grad,
-            shift_two_grad,
-            mask_grad,
-        ),
-        ("dp", "pair"),
-    )
+    low = jnp.bfloat16
+    outer_rows = scatter_two(
+        place, outer_grad[:, :half].astype(low), outer_grad[:, half:].astype(low)
+    )
+    inner_rows = scatter_two(
+        place, inner_grad[:, :inner_half].astype(low), inner_grad[:, inner_half:].astype(low)
+    )
+    four = [g.astype(low) for g in (query_grad, key_grad, value_grad, output_grad)]
+    four_rows = scatter_two(
+        place,
+        jnp.concatenate(four[:2], axis=1),
+        jnp.concatenate(four[2:], axis=1),
+    )
+    smalls = (
+        query_bias_grad,
+        value_bias_grad,
+        output_bias_grad,
+        inner_bias_grad,
+        outer_bias_grad,
+        gain_one_grad,
+        shift_one_grad,
+        gain_two_grad,
+        shift_two_grad,
+        mask_grad,
+    )
+    packed = total_of(place, jnp.concatenate(smalls).reshape(-1, 128)).reshape(-1)
+    ends = [0]
+    for value in smalls:
+        ends.append(ends[-1] + value.shape[0])
     return (
         layer_output,
         input_grad,
-        summed[0],
-        summed[1],
-        summed[2],
-        summed[3],
-        summed[4],
-        summed[5],
-        smalls[0],
-        smalls[1],
-        smalls[2],
-        smalls[3],
-        smalls[4],
-        smalls[5],
-        smalls[6],
-        smalls[7],
-        smalls[8],
-        smalls[9],
+        four_rows[0][:, :width],
+        four_rows[0][:, width:],
+        four_rows[1][:, :width],
+        four_rows[1][:, width:],
+        jnp.concatenate(inner_rows, axis=1),
+        jnp.concatenate(outer_rows, axis=1),
+        *(packed[a:b] for a, b in zip(ends[:-1], ends[1:])),
     )
 
 

time: 1100 us -> 434 us (0.39)
  waiting for transfers between devices: 897 us -> 136 us
  starting transfers between devices: 0.65 us -> 103 us
  blocking collectives: 40.7 us -> 0 us
  local copies, waits for them, and re-layouts: 14.8 us -> 47.7 us
  other arithmetic: 15 us -> 44.2 us
  matrix products: 110 us -> 93.6 us
  between operations: 14.9 us -> 3.45 us
    reduce_scatter x6 -> x0, waiting for transfers between devices: 584 us -> none  [the longest x1 142 us: on_device(): lax.psum_scatter(inner_grad, ('dp', 'pair'), scatter_dimension=0, tiled=T...]
    all_gather x6 -> x0, waiting for transfers between devices: 309 us -> none  [the longest x1 61.5 us: on_device(): lax.all_gather(owned[4], ('dp', 'pair'), axis=0, tiled=True)]
    ppermute x0 -> x89, waiting for transfers between devices: none -> 136 us  [the longest x72 126 us: shift(): return lax.ppermute(value, 'dp', pairs)]
    ppermute x0 -> x89, starting transfers between devices: none -> 103 us  [the longest x72 92.9 us: shift(): return lax.ppermute(value, 'dp', pairs)]
    psum x1 -> x0, blocking collectives: 40.7 us -> none  [on_device(): lax.psum((query_bias_grad, value_bias_grad, output_bias_grad, inner_bias_...]
    another operation x0 -> x47, other arithmetic: none -> 16.3 us  [spread(): return jnp.stack(rows)]
    slice x0 -> x16, local copies, waits for them, and re-layouts: none -> 13.8 us  [the longest x1 4.82 us: on_device(): inner_grad[:, :inner_half].astype(low)]
    dot_general x6, matrix products: 26.4 us -> 12.7 us  [outer_sum(): jnp.einsum('rd,re->de', left, right, preferred_element_type=jnp.float32)]
  transfers between devices with their start and end apart: 12 -> 89, of which waited for: 11 -> 29; matrix products, arithmetic and copies ran while one was open for 10% -> 17% of each run, Pallas kernels for 0% -> 0%
where the time goes in v1:
time: 434 us; the launch traced here: 428 us
  waiting for transfers between devices  136 us (31%)
  starting transfers between devices  103 us (24%)
  matrix products  93.6 us (22%)
  local copies, waits for them, and re-layouts  47.7 us (11%)
  other arithmetic  44.2 us (10%)
    ppermute x72, waiting for transfers between devices, shift(): return lax.ppermute(value, 'dp', pairs)  126 us
    ppermute x72, starting transfers between devices, shift(): return lax.ppermute(value, 'dp', pairs)  92.9 us
    dot_general x6, matrix products, dense(): return jnp.dot(left, right, preferred_element_type=jnp.float32)  29.5 us
    dot_general x6, matrix products, back_dense(): jnp.einsum('re,de->rd', grad, weight, preferred_element_type=jnp.float32)  22 us
    another operation x47, other arithmetic, spread(): return jnp.stack(rows)  16.3 us
    dot_general x6, matrix products, outer_sum(): jnp.einsum('rd,re->de', left, right, preferred_element_type=jnp.float32)  12.7 us
    unnamed x215, local copies, waits for them, and re-layouts  10.7 us
    ppermute x4, waiting for transfers between devices, total_of(): lax.ppermute(value, 'dp', [(i, i ^ stride) for i in range(slow * mid * fa...  9.55 us
  transfers between devices with their start and end apart: 89, of which 29 were waited for; matrix products, arithmetic and copies ran while one was open for 17% of the time, Pallas kernels for 0%

profile of v1, /device:TPU:0, one launch (start us, length us, event | category | flops | bytes accessed | tf_op | source)
XLA Modules:
  0.0 427.5 jit_solution(10337157023632256525)
XLA Ops:
  2.3 4.0 collective-permute-start.21
  14.8 3.7 collective-permute-start
  25.7 3.2 collective-permute-start.28
  32.4 3.9 collective-permute-done.29
  36.3 3.2 collective-permute-start.14
  39.5 6.2 %collective-permute-start.15 = (bf16[1,24,1920]{2,1,0:T(8,128)(2,1)S(1)}, bf16[1,24,1920]{2,1,0:T(8,128)(2,1)S(1)}, u32[]{:S(2)}, u32[]{:S(2)}) collective-permute-start(bf16[1,24,1920]{2,1,0:T(8,128)(2,1)S(1)} %maximum_bitcast_fusion.3), channel_id=1, source_target_pairs={{0,16},{2,18},{4,20},{6,22},{8,24},{10,26},{12,28},{14,30},{16,0},... | collective-permute-start | bytes 276488 | tf_op jit(solution)/shard_map/ppermute | solution.py:65
  45.9 3.8 collective-permute-start.10
  56.4 14.9 %collective-permute-done.11 = bf16[4,1,24,1152]{3,2,0,1:T(8,128)(2,1)S(1)} collective-permute-done((bf16[4,1,24,1152]{3,2,0,1:T(8,128)(2,1)S(1)}, bf16[4,1,24,1152]{3,2,0,1:T(8,128)(2,1)S(1)}, u32[]{:S(2)}, u32[]{:S(2)}) %collective-permute-start.11) | collective-permute-done | bytes 221216 | tf_op jit(solution)/shard_map/ppermute | solution.py:65
  79.8 18.9 %collective-permute-done.39 = bf16[4,1,96,384]{3,2,0,1:T(8,128)(2,1)S(1)} collective-permute-done((bf16[4,1,96,384]{3,2,0,1:T(8,128)(2,1)S(1)}, bf16[4,1,96,384]{3,2,0,1:T(8,128)(2,1)S(1)}, u32[]{:S(2)}, u32[]{:S(2)}) %collective-permute-start.39) | collective-permute-done | bytes 294944 | tf_op jit(solution)/shard_map/ppermute | solution.py:65
  98.8 3.7 collective-permute-start.25
  108.7 9.2 %collective-permute-done.25 = bf16[4,1,24,1920]{3,2,0,1:T(8,128)(2,1)S(1)} collective-permute-done((bf16[4,1,24,1920]{3,2,0,1:T(8,128)(2,1)S(1)}, bf16[4,1,24,1920]{3,2,0,1:T(8,128)(2,1)S(1)}, u32[]{:S(2)}, u32[]{:S(2)}) %collective-permute-start.25) | collective-permute-done | bytes 368672 | tf_op jit(solution)/shard_map/ppermute | solution.py:65
  128.4 3.5 convolution_convert_fusion.7
  143.0 7.1 %convolution_convert_fusion.9 = bf16[12,64,512]{2,1,0:T(8,128)(2,1)S(1)} fusion(bf16[512,12,64]{0,2,1:T(8,128)(2,1)S(1)} %bitcast.545, f32[12,512,512]{1,2,0:T(8,128)} %copy-done, f32[12,512]{1,0:T(8,128)S(1)} %log_add_fusion), kind=kOutput, calls=%fused_computation.94 | convolution fusion | flops 412483584 | bytes 14180352 | tf_op jit(solution)/shard_map/shqk,skhd->sqhd/dot_general | solution.py:193
  164.7 19.6 %multiply_convert_fusion.1 = (bf16[512,3072]{1,0:T(8,128)(2,1)S(1)}, f32[512,3072]{1,0:T(8,128)}, f32[512,3072]{1,0:T(8,128)}) fusion(f32[3072]{0:T(1024)S(1)} %copy-done.84, bf16[768,1536]{1,0:T(8,128)(2,1)S(1)} %slice.213, bf16[768,1536]{1,0:T(8,128)(2,1)S(1)} %slice.212, f32[512,768]{1,0:T(8,128)S(1)} %get-tuple-element.175, f32[768]{0:T(1024)S(1)} %copy-done.89, ...), kind=kOutput, calls=%fused_computation.10 | convolution fusion | flops 2531131392 | bytes 22042624 | tf_op jit(solution)/shard_map/dot_general | solution.py:20
  192.2 8.7 %convert_reduce_fusion = (f32[3072]{0:T(1024)}, bf16[512,3072]{1,0:T(8,128)(2,1)S(1)}) fusion(f32[512,3072]{1,0:T(8,128)} %get-tuple-element.35, bf16[512,768]{1,0:T(8,128)(2,1)S(1)} %get-tuple-element.27, bf16[3072,384]{1,0:T(8,128)(2,1)S(1)} %bitcast.560, bf16[3072,384]{1,0:T(8,128)(2,1)S(1)} %bitcast.562, f32[512,3072]{1,0:T(8,128)} %get-tuple-element.176, ...), kind=kOutput, calls=%fused_computation.8 | convolution fusion | flops 2452091904 | bytes 21258240 | tf_op jit(solution)/shard_map/re,de->rd/dot_general | solution.py:28
  200.9 3.6 multiply_reduce_fusion.3
  210.9 8.2 %convert_reduce_fusion.3 = (f32[12,64]{1,0:T(8,128)S(1)}, bf16[12,64,512]{2,1,0:T(8,128)(2,1)}) fusion(bf16[512,12,64]{0,2,1:T(8,128)(2,1)} %bitcast.547, f32[12,512,512]{1,2,0:T(8,128)} %copy-done, f32[12,512]{1,0:T(8,128)S(1)} %log_add_fusion), kind=kOutput, calls=%fused_computation.59 | convolution fusion | flops 413269248 | bytes 14183424 | tf_op jit(solution)/shard_map/shqk,sqhd->skhd/dot_general | solution.py:229
  219.0 9.1 %multiply_reduce_fusion = (f32[12,512]{1,0:T(8,128)S(1)}, f32[12,512,512]{1,2,0:T(8,128)}) fusion(f32[12,512,512]{1,2,0:T(8,128)} %copy-done, f32[12,512]{1,0:T(8,128)S(1)} %log_add_fusion, bf16[512,12,64]{0,2,1:T(8,128)(2,1)S(1)} %bitcast.548, bf16[512,12,64]{0,2,1:T(8,128)(2,1)S(1)} %bitcast.546), kind=kOutput, calls=%fused_computation.1 | convolution fusion | flops 415229952 | bytes 26787840 | tf_op jit(solution)/shard_map/sqhd,skhd->shqk/dot_general | solution.py:226
  228.2 7.1 %multiply_convert_fusion = bf16[12,512,512]{1,2,0:T(8,128)(2,1)S(1)} fusion(f32[12,512,512]{1,2,0:T(8,128)} %get-tuple-element.181, f32[12,512,512]{1,2,0:T(8,128)S(1)} %bitcast.528, f32[12,512]{1,0:T(8,128)S(1)} %get-tuple-element.180, f32[12,512]{1,0:T(8,128)S(1)} %log_add_fusion), kind=kLoop, calls=%fused_computation | loop fusion | flops 15728640 | bytes 31506432 | tf_op jit(solution)/shard_map/convert_element_type | solution.py:233
  247.0 4.9 %convolution_convert_fusion.1 = bf16[768,3072]{1,0:T(8,128)(2,1)} fusion(bf16[512,3072]{1,0:T(8,128)(2,1)S(1)} %copy-done.95, f32[512,768]{1,0:T(8,128)S(1)} %copy-done.9, f32[768]{0:T(1024)S(1)} %copy-done.90, f32[768]{0:T(1024)S(1)} %copy-done.78, f32[512]{0:T(512)S(1)} %copy-done.69, f32[512]{0:T(512)S(1)} %copy-done.59), kind=kOutput, calls=%fused_computation.25 | convolution fusion | flops 2420244480 | bytes 9447424 | tf_op jit(solution)/shard_map/rd,re->de/dot_general | solution.py:24
  251.9 4.3 %convolution_convert_fusion = bf16[3072,768]{1,0:T(8,128)(2,1)} fusion(bf16[512,3072]{1,0:T(8,128)(2,1)S(1)} %copy-done.97, bf16[512,768]{1,0:T(8,128)(2,1)S(1)} %copy-done.47), kind=kOutput, calls=%fused_computation.24 | convolution fusion | flops 2418278400 | bytes 8650752 | tf_op jit(solution)/shard_map/rd,re->de/dot_general | solution.py:24
  257.7 4.3 %copy.225 = bf16[768,1536]{1,0:T(8,128)(2,1)} copy(bf16[768,1536]{0,1:T(8,128)(2,1)} %pad_maximum_fusion.8) | data formatting | bytes 4718592 | tf_op jit(solution)/shard_map/concatenate | solution.py:268
  267.1 4.5 %copy.226 = bf16[768,1536]{1,0:T(8,128)(2,1)} copy(bf16[768,1536]{0,1:T(8,128)(2,1)} %pad_maximum_fusion.9) | data formatting | bytes 4718592 | tf_op jit(solution)/shard_map/concatenate | solution.py:269
  274.4 4.8 %fusion.94 = (bf16[768,1536]{1,0:T(8,128)(2,1)}, bf16[768,1536]{1,0:T(8,128)(2,1)}) fusion(bf16[768,3072]{1,0:T(8,128)(2,1)} %convolution_convert_fusion.1), kind=kLoop, calls=%fused_computation.342 | loop fusion | bytes 9437184 | tf_op jit(solution)/shard_map/slice | solution.py:263
  280.1 4.0 select_convert_fusion
  317.4 3.4 collective-permute-done.52
  320.7 4.1 collective-permute-start.66
  324.9 25.9 %collective-permute-done.51 = bf16[1,4,24,1536]{3,2,1,0:T(8,128)(2,1)S(1)} collective-permute-done((bf16[1,4,24,1536]{3,2,1,0:T(8,128)(2,1)S(1)}, bf16[1,4,24,1536]{3,2,1,0:T(8,128)(2,1)S(1)}, u32[]{:S(2)}, u32[]{:S(2)}) %collective-permute-start.51) | collective-permute-done | bytes 294944 | tf_op jit(solution)/shard_map/ppermute | solution.py:65
  352.4 12.7 %collective-permute-done.65 = bf16[1,4,24,1536]{3,2,1,0:T(8,128)(2,1)S(1)} collective-permute-done((bf16[1,4,24,1536]{3,2,1,0:T(8,128)(2,1)S(1)}, bf16[1,4,24,1536]{3,2,1,0:T(8,128)(2,1)S(1)}, u32[]{:S(2)}, u32[]{:S(2)}) %collective-permute-start.65) | collective-permute-done | bytes 294944 | tf_op jit(solution)/shard_map/ppermute | solution.py:65
  368.9 6.1 %collective-permute-done.59 = bf16[1,4,24,1536]{3,2,1,0:T(8,128)(2,1)S(1)} collective-permute-done((bf16[1,4,24,1536]{3,2,1,0:T(8,128)(2,1)S(1)}, bf16[1,4,24,1536]{3,2,1,0:T(8,128)(2,1)S(1)}, u32[]{:S(2)}, u32[]{:S(2)}) %collective-permute-start.59) | collective-permute-done | bytes 294944 | tf_op jit(solution)/shard_map/ppermute | solution.py:65
  375.0 5.4 %collective-permute-done.58 = bf16[1,4,24,1536]{3,2,1,0:T(8,128)(2,1)S(1)} collective-permute-done((bf16[1,4,24,1536]{3,2,1,0:T(8,128)(2,1)S(1)}, bf16[1,4,24,1536]{3,2,1,0:T(8,128)(2,1)S(1)}, u32[]{:S(2)}, u32[]{:S(2)}) %collective-permute-start.58) | collective-permute-done | bytes 294944 | tf_op jit(solution)/shard_map/ppermute | solution.py:65
  383.8 11.2 %collective-permute-done.79 = bf16[1,4,96,384]{3,2,1,0:T(8,128)(2,1)S(1)} collective-permute-done((bf16[1,4,96,384]{3,2,1,0:T(8,128)(2,1)S(1)}, bf16[1,4,96,384]{3,2,1,0:T(8,128)(2,1)S(1)}, u32[]{:S(2)}, u32[]{:S(2)}) %collective-permute-start.79) | collective-permute-done | bytes 294944 | tf_op jit(solution)/shard_map/ppermute | solution.py:65
  (537 shorter events, 186.9 us)
Async XLA Ops:
  2.3 43.5 %collective-permute-start.21 = (bf16[1,24,1920]{2,1,0:T(8,128)(2,1)S(1)}, bf16[1,24,1920]{2,1,0:T(8,128)(2,1)S(1)}, u32[]{:S(2)}, u32[]{:S(2)}) collective-permute-start(bf16[1,24,1920]{2,1,0:T(8,128)(2,1)S(1)} %maximum_bitcast_fusion.4), channel_id=1, source_target_pairs={{0,6},{2,0},{4,2},{6,4},{8,14},{10,8},{12,10},{14,12},{16,22},{18,... | collective-permute-start | bytes 276488 | tf_op jit(solution)/shard_map/ppermute | solution.py:65
  6.3 39.6 %collective-permute-start.22 = (bf16[1,24,1920]{2,1,0:T(8,128)(2,1)S(1)}, bf16[1,24,1920]{2,1,0:T(8,128)(2,1)S(1)}, u32[]{:S(2)}, u32[]{:S(2)}) collective-permute-start(bf16[1,24,1920]{2,1,0:T(8,128)(2,1)S(1)} %maximum_bitcast_fusion.4), channel_id=1, source_target_pairs={{0,4},{2,6},{4,0},{6,2},{8,12},{10,14},{12,8},{14,10},{16,20},{18,... | collective-permute-start | bytes 276488 | tf_op jit(solution)/shard_map/ppermute | solution.py:65
  31.1 18.6 %collective-permute-start.23 = (bf16[1,24,1920]{2,1,0:T(8,128)(2,1)S(1)}, bf16[1,24,1920]{2,1,0:T(8,128)(2,1)S(1)}, u32[]{:S(2)}, u32[]{:S(2)}) collective-permute-start(bf16[1,24,1920]{2,1,0:T(8,128)(2,1)S(1)} %maximum_bitcast_fusion.4), channel_id=1, source_target_pairs={{0,2},{2,4},{4,6},{6,0},{8,10},{10,12},{12,14},{14,8},{16,18},{18,... | collective-permute-start | bytes 276488 | tf_op jit(solution)/shard_map/ppermute | solution.py:65
  49.7 21.6 %collective-permute-start.11 = (bf16[4,1,24,1152]{3,2,0,1:T(8,128)(2,1)S(1)}, bf16[4,1,24,1152]{3,2,0,1:T(8,128)(2,1)S(1)}, u32[]{:S(2)}, u32[]{:S(2)}) collective-permute-start(bf16[4,1,24,1152]{3,2,0,1:T(8,128)(2,1)S(1)} %pad_maximum_fusion.40), channel_id=1, source_target_pairs={{0,16},{2,18},{4,20},{6,22},{8,24},{10,26},{12,28},{14,30},{16,0},... | collective-permute-start | bytes 663560 | tf_op jit(solution)/shard_map/ppermute | solution.py:65
  49.9 21.4 %collective-permute-start.12 = (bf16[4,1,24,1152]{3,2,0,1:T(8,128)(2,1)S(1)}, bf16[4,1,24,1152]{3,2,0,1:T(8,128)(2,1)S(1)}, u32[]{:S(2)}, u32[]{:S(2)}) collective-permute-start(bf16[4,1,24,1152]{3,2,0,1:T(8,128)(2,1)S(1)} %pad_maximum_fusion.40), channel_id=1, source_target_pairs={{0,8},{2,10},{4,12},{6,14},{8,16},{10,18},{12,20},{14,22},{16,24},... | collective-permute-start | bytes 663560 | tf_op jit(solution)/shard_map/ppermute | solution.py:65
  50.6 23.5 %collective-permute-start.3 = (bf16[4,1,24,1152]{3,2,0,1:T(8,128)(2,1)S(1)}, bf16[4,1,24,1152]{3,2,0,1:T(8,128)(2,1)S(1)}, u32[]{:S(2)}, u32[]{:S(2)}) collective-permute-start(bf16[4,1,24,1152]{3,2,0,1:T(8,128)(2,1)S(1)} %pad_maximum_fusion.39), channel_id=1, source_target_pairs={{0,6},{2,0},{4,2},{6,4},{8,14},{10,8},{12,10},{14,12},{16,22},{18,... | collective-permute-start | bytes 663560 | tf_op jit(solution)/shard_map/ppermute | solution.py:65
  52.3 21.9 %collective-permute-start.4 = (bf16[4,1,24,1152]{3,2,0,1:T(8,128)(2,1)S(1)}, bf16[4,1,24,1152]{3,2,0,1:T(8,128)(2,1)S(1)}, u32[]{:S(2)}, u32[]{:S(2)}) collective-permute-start(bf16[4,1,24,1152]{3,2,0,1:T(8,128)(2,1)S(1)} %pad_maximum_fusion.39), channel_id=1, source_target_pairs={{0,4},{2,6},{4,0},{6,2},{8,12},{10,14},{12,8},{14,10},{16,20},{18,... | collective-permute-start | bytes 663560 | tf_op jit(solution)/shard_map/ppermute | solution.py:65
  55.2 20.5 %collective-permute-start.5 = (bf16[4,1,24,1152]{3,2,0,1:T(8,128)(2,1)S(1)}, bf16[4,1,24,1152]{3,2,0,1:T(8,128)(2,1)S(1)}, u32[]{:S(2)}, u32[]{:S(2)}) collective-permute-start(bf16[4,1,24,1152]{3,2,0,1:T(8,128)(2,1)S(1)} %pad_maximum_fusion.39), channel_id=1, source_target_pairs={{0,2},{2,4},{4,6},{6,0},{8,10},{10,12},{12,14},{14,8},{16,18},{18,... | collective-permute-start | bytes 663560 | tf_op jit(solution)/shard_map/ppermute | solution.py:65
  71.3 27.4 %collective-permute-start.39 = (bf16[4,1,96,384]{3,2,0,1:T(8,128)(2,1)S(1)}, bf16[4,1,96,384]{3,2,0,1:T(8,128)(2,1)S(1)}, u32[]{:S(2)}, u32[]{:S(2)}) collective-permute-start(bf16[4,1,96,384]{3,2,0,1:T(8,128)(2,1)S(1)} %pad_maximum_fusion.38), channel_id=1, source_target_pairs={{0,16},{2,18},{4,20},{6,22},{8,24},{10,26},{12,28},{14,30},{16,0},... | collective-permute-start | bytes 884744 | tf_op jit(solution)/shard_map/ppermute | solution.py:65
  74.2 24.6 %collective-permute-start.40 = (bf16[4,1,96,384]{3,2,0,1:T(8,128)(2,1)S(1)}, bf16[4,1,96,384]{3,2,0,1:T(8,128)(2,1)S(1)}, u32[]{:S(2)}, u32[]{:S(2)}) collective-permute-start(bf16[4,1,96,384]{3,2,0,1:T(8,128)(2,1)S(1)} %pad_maximum_fusion.38), channel_id=1, source_target_pairs={{0,8},{2,10},{4,12},{6,14},{8,16},{10,18},{12,20},{14,22},{16,24},... | collective-permute-start | bytes 884744 | tf_op jit(solution)/shard_map/ppermute | solution.py:65
  74.2 29.8 %collective-permute-start.31 = (bf16[4,1,96,384]{3,2,0,1:T(8,128)(2,1)S(1)}, bf16[4,1,96,384]{3,2,0,1:T(8,128)(2,1)S(1)}, u32[]{:S(2)}, u32[]{:S(2)}) collective-permute-start(bf16[4,1,96,384]{3,2,0,1:T(8,128)(2,1)S(1)} %pad_maximum_fusion.37), channel_id=1, source_target_pairs={{0,6},{2,0},{4,2},{6,4},{8,14},{10,8},{12,10},{14,12},{16,22},{18,... | collective-permute-start | bytes 884744 | tf_op jit(solution)/shard_map/ppermute | solution.py:65
  75.8 28.3 %collective-permute-start.32 = (bf16[4,1,96,384]{3,2,0,1:T(8,128)(2,1)S(1)}, bf16[4,1,96,384]{3,2,0,1:T(8,128)(2,1)S(1)}, u32[]{:S(2)}, u32[]{:S(2)}) collective-permute-start(bf16[4,1,96,384]{3,2,0,1:T(8,128)(2,1)S(1)} %pad_maximum_fusion.37), channel_id=1, source_target_pairs={{0,4},{2,6},{4,0},{6,2},{8,12},{10,14},{12,8},{14,10},{16,20},{18,... | collective-permute-start | bytes 884744 | tf_op jit(solution)/shard_map/ppermute | solution.py:65
  78.8 25.3 %collective-permute-start.33 = (bf16[4,1,96,384]{3,2,0,1:T(8,128)(2,1)S(1)}, bf16[4,1,96,384]{3,2,0,1:T(8,128)(2,1)S(1)}, u32[]{:S(2)}, u32[]{:S(2)}) collective-permute-start(bf16[4,1,96,384]{3,2,0,1:T(8,128)(2,1)S(1)} %pad_maximum_fusion.37), channel_id=1, source_target_pairs={{0,2},{2,4},{4,6},{6,0},{8,10},{10,12},{12,14},{14,8},{16,18},{18,... | collective-permute-start | bytes 884744 | tf_op jit(solution)/shard_map/ppermute | solution.py:65
  98.8 19.2 %collective-permute-start.25 = (bf16[4,1,24,1920]{3,2,0,1:T(8,128)(2,1)S(1)}, bf16[4,1,24,1920]{3,2,0,1:T(8,128)(2,1)S(1)}, u32[]{:S(2)}, u32[]{:S(2)}) collective-permute-start(bf16[4,1,24,1920]{3,2,0,1:T(8,128)(2,1)S(1)} %pad_maximum_fusion.36), channel_id=1, source_target_pairs={{0,16},{2,18},{4,20},{6,22},{8,24},{10,26},{12,28},{14,30},{16,0},... | collective-permute-start | bytes 1105928 | tf_op jit(solution)/shard_map/ppermute | solution.py:65
  120.2 30.0 %collective-permute-start.41 = (bf16[4,4,1,96,384]{4,3,0,1,2:T(8,128)(2,1)}, bf16[4,4,1,96,384]{4,3,0,1,2:T(8,128)(2,1)}, u32[]{:S(2)}, u32[]{:S(2)}) collective-permute-start(bf16[4,4,1,96,384]{4,3,0,1,2:T(8,128)(2,1)} %pad_maximum_fusion.24), channel_id=1, source_target_pairs={{0,1},{1,0},{2,3},{3,2},{4,5},{5,4},{6,7},{7,6},{8,9},{9,8},{10,11... | collective-permute-start | bytes 3538952 | tf_op jit(solution)/shard_map/ppermute | solution.py:54
  120.2 32.6 %collective-permute-start.34 = (bf16[4,4,1,96,384]{4,3,0,1,2:T(8,128)(2,1)}, bf16[4,4,1,96,384]{4,3,0,1,2:T(8,128)(2,1)}, u32[]{:S(2)}, u32[]{:S(2)}) collective-permute-start(bf16[4,4,1,96,384]{4,3,0,1,2:T(8,128)(2,1)} %pad_maximum_fusion.23), channel_id=1, source_target_pairs={{0,1},{1,0},{2,3},{3,2},{4,5},{5,4},{6,7},{7,6},{8,9},{9,8},{10,11... | collective-permute-start | bytes 3538952 | tf_op jit(solution)/shard_map/ppermute | solution.py:54
  120.7 34.8 %collective-permute-start.27 = (bf16[4,4,1,24,1920]{4,3,0,1,2:T(8,128)(2,1)}, bf16[4,4,1,24,1920]{4,3,0,1,2:T(8,128)(2,1)}, u32[]{:S(2)}, u32[]{:S(2)}) collective-permute-start(bf16[4,4,1,24,1920]{4,3,0,1,2:T(8,128)(2,1)} %pad_maximum_fusion.14), channel_id=1, source_target_pairs={{0,1},{1,0},{2,3},{3,2},{4,5},{5,4},{6,7},{7,6},{8,9},{9,8},{10,11... | collective-permute-start | bytes 4423688 | tf_op jit(solution)/shard_map/ppermute | solution.py:54
  122.5 36.5 %collective-permute-start.20 = (bf16[4,4,1,24,1920]{4,3,0,1,2:T(8,128)(2,1)}, bf16[4,4,1,24,1920]{4,3,0,1,2:T(8,128)(2,1)}, u32[]{:S(2)}, u32[]{:S(2)}) collective-permute-start(bf16[4,4,1,24,1920]{4,3,0,1,2:T(8,128)(2,1)} %pad_maximum_fusion.13), channel_id=1, source_target_pairs={{0,1},{1,0},{2,3},{3,2},{4,5},{5,4},{6,7},{7,6},{8,9},{9,8},{10,11... | collective-permute-start | bytes 4423688 | tf_op jit(solution)/shard_map/ppermute | solution.py:54
  264.5 40.0 %collective-permute-start.42 = (bf16[1,4,4,24,1536]{4,3,2,1,0:T(8,128)(2,1)}, bf16[1,4,4,24,1536]{4,3,2,1,0:T(8,128)(2,1)}, u32[]{:S(2)}, u32[]{:S(2)}) collective-permute-start(bf16[1,4,4,24,1536]{4,3,2,1,0:T(8,128)(2,1)} %dynamic-slice_bitcast_fusion.3), channel_id=1, source_target_pairs={{0,1},{1,0},{2,3},{3,2},{4,5},{5,4},{6,7},{7,6},{8,9},{9,8},{10,11... | collective-permute-start | bytes 3538952 | tf_op jit(solution)/shard_map/ppermute | solution.py:54
  274.0 32.9 %collective-permute-start.49 = (bf16[1,4,4,24,1536]{4,3,2,1,0:T(8,128)(2,1)}, bf16[1,4,4,24,1536]{4,3,2,1,0:T(8,128)(2,1)}, u32[]{:S(2)}, u32[]{:S(2)}) collective-permute-start(bf16[1,4,4,24,1536]{4,3,2,1,0:T(8,128)(2,1)} %dynamic-slice_bitcast_fusion.2), channel_id=1, source_target_pairs={{0,1},{1,0},{2,3},{3,2},{4,5},{5,4},{6,7},{7,6},{8,9},{9,8},{10,11... | collective-permute-start | bytes 3538952 | tf_op jit(solution)/shard_map/ppermute | solution.py:54
  284.9 26.6 %collective-permute-start.63 = (bf16[1,4,4,24,1536]{4,3,2,1,0:T(8,128)(2,1)S(1)}, bf16[1,4,4,24,1536]{4,3,2,1,0:T(8,128)(2,1)S(1)}, u32[]{:S(2)}, u32[]{:S(2)}) collective-permute-start(bf16[1,4,4,24,1536]{4,3,2,1,0:T(8,128)(2,1)S(1)} %dynamic-slice_bitcast_fusion.1), channel_id=1, source_target_pairs={{0,1},{1,0},{2,3},{3,2},{4,5},{5,4},{6,7},{7,6},{8,9},{9,8},{10,11... | collective-permute-start | bytes 3538952 | tf_op jit(solution)/shard_map/ppermute | solution.py:54
  287.4 26.1 %collective-permute-start.56 = (bf16[1,4,4,24,1536]{4,3,1,2,0:T(8,128)(2,1)S(1)}, bf16[1,4,4,24,1536]{4,3,1,2,0:T(8,128)(2,1)S(1)}, u32[]{:S(2)}, u32[]{:S(2)}) collective-permute-start(bf16[1,4,4,24,1536]{4,3,1,2,0:T(8,128)(2,1)S(1)} %bitcast.563), channel_id=1, source_target_pairs={{0,1},{1,0},{2,3},{3,2},{4,5},{5,4},{6,7},{7,6},{8,9},{9,8},{10,11... | collective-permute-start | bytes 3538952 | tf_op jit(solution)/shard_map/ppermute | solution.py:54
  306.9 61.1 %collective-permute-start.45 = (bf16[1,4,24,1536]{3,2,1,0:T(8,128)(2,1)S(1)}, bf16[1,4,24,1536]{3,2,1,0:T(8,128)(2,1)S(1)}, u32[]{:S(2)}, u32[]{:S(2)}) collective-permute-start(bf16[1,4,24,1536]{3,2,1,0:T(8,128)(2,1)S(1)} %get-tuple-element.87), channel_id=1, source_target_pairs={{0,6},{2,0},{4,2},{6,4},{8,14},{10,8},{12,10},{14,12},{16,22},{18,... | collective-permute-start | bytes 884744 | tf_op jit(solution)/shard_map/ppermute | solution.py:65
  310.8 57.3 %collective-permute-start.44 = (bf16[1,4,24,1536]{3,2,1,0:T(8,128)(2,1)S(1)}, bf16[1,4,24,1536]{3,2,1,0:T(8,128)(2,1)S(1)}, u32[]{:S(2)}, u32[]{:S(2)}) collective-permute-start(bf16[1,4,24,1536]{3,2,1,0:T(8,128)(2,1)S(1)} %get-tuple-element.88), channel_id=1, source_target_pairs={{0,4},{2,6},{4,0},{6,2},{8,12},{10,14},{12,8},{14,10},{16,20},{18,... | collective-permute-start | bytes 884744 | tf_op jit(solution)/shard_map/ppermute | solution.py:65
  313.5 37.3 %collective-permute-start.51 = (bf16[1,4,24,1536]{3,2,1,0:T(8,128)(2,1)S(1)}, bf16[1,4,24,1536]{3,2,1,0:T(8,128)(2,1)S(1)}, u32[]{:S(2)}, u32[]{:S(2)}) collective-permute-start(bf16[1,4,24,1536]{3,2,1,0:T(8,128)(2,1)S(1)} %get-tuple-element.85), channel_id=1, source_target_pairs={{0,16},{2,18},{4,20},{6,22},{8,24},{10,26},{12,28},{14,30},{16,0},... | collective-permute-start | bytes 884744 | tf_op jit(solution)/shard_map/ppermute | solution.py:65
  315.3 35.5 %collective-permute-start.50 = (bf16[1,4,24,1536]{3,2,1,0:T(8,128)(2,1)S(1)}, bf16[1,4,24,1536]{3,2,1,0:T(8,128)(2,1)S(1)}, u32[]{:S(2)}, u32[]{:S(2)}) collective-permute-start(bf16[1,4,24,1536]{3,2,1,0:T(8,128)(2,1)S(1)} %get-tuple-element.83), channel_id=1, source_target_pairs={{0,8},{2,10},{4,12},{6,14},{8,16},{10,18},{12,20},{14,22},{16,24},... | collective-permute-start | bytes 884744 | tf_op jit(solution)/shard_map/ppermute | solution.py:65
  320.7 30.2 %collective-permute-start.66 = (bf16[1,4,24,1536]{3,2,1,0:T(8,128)(2,1)S(1)}, bf16[1,4,24,1536]{3,2,1,0:T(8,128)(2,1)S(1)}, u32[]{:S(2)}, u32[]{:S(2)}) collective-permute-start(bf16[1,4,24,1536]{3,2,1,0:T(8,128)(2,1)S(1)} %get-tuple-element.81), channel_id=1, source_target_pairs={{0,24},{2,26},{4,28},{6,30},{8,0},{10,2},{12,4},{14,6},{16,8},{18,... | collective-permute-start | bytes 884744 | tf_op jit(solution)/shard_map/ppermute | solution.py:65
  368.2 26.7 %collective-permute-start.79 = (bf16[1,4,96,384]{3,2,1,0:T(8,128)(2,1)S(1)}, bf16[1,4,96,384]{3,2,1,0:T(8,128)(2,1)S(1)}, u32[]{:S(2)}, u32[]{:S(2)}) collective-permute-start(bf16[1,4,96,384]{3,2,1,0:T(8,128)(2,1)S(1)} %get-tuple-element.76), channel_id=1, source_target_pairs={{0,16},{2,18},{4,20},{6,22},{8,24},{10,26},{12,28},{14,30},{16,0},... | collective-permute-start | bytes 884744 | tf_op jit(solution)/shard_map/ppermute | solution.py:65
  375.0 20.0 %collective-permute-start.78 = (bf16[1,4,96,384]{3,2,1,0:T(8,128)(2,1)S(1)}, bf16[1,4,96,384]{3,2,1,0:T(8,128)(2,1)S(1)}, u32[]{:S(2)}, u32[]{:S(2)}) collective-permute-start(bf16[1,4,96,384]{3,2,1,0:T(8,128)(2,1)S(1)} %get-tuple-element.74), channel_id=1, source_target_pairs={{0,8},{2,10},{4,12},{6,14},{8,16},{10,18},{12,20},{14,22},{16,24},... | collective-permute-start | bytes 884744 | tf_op jit(solution)/shard_map/ppermute | solution.py:65
  382.4 17.3 %collective-permute-start.71 = (bf16[1,4,96,384]{3,2,1,0:T(8,128)(2,1)S(1)}, bf16[1,4,96,384]{3,2,1,0:T(8,128)(2,1)S(1)}, u32[]{:S(2)}, u32[]{:S(2)}) collective-permute-start(bf16[1,4,96,384]{3,2,1,0:T(8,128)(2,1)S(1)} %get-tuple-element.71), channel_id=1, source_target_pairs={{0,2},{2,4},{4,6},{6,0},{8,10},{10,12},{12,14},{14,8},{16,18},{18,... | collective-permute-start | bytes 884744 | tf_op jit(solution)/shard_map/ppermute | solution.py:65
  397.3 19.5 %collective-permute-start.55 = (bf16[1,24,1536]{2,1,0:T(8,128)(2,1)S(1)}, bf16[1,24,1536]{2,1,0:T(8,128)(2,1)S(1)}, u32[]{:S(2)}, u32[]{:S(2)}) collective-permute-start(bf16[1,24,1536]{2,1,0:T(8,128)(2,1)S(1)} %get-tuple-element.132), channel_id=1, source_target_pairs={{0,6},{2,0},{4,2},{6,4},{8,14},{10,8},{12,10},{14,12},{16,22},{18,... | collective-permute-start | bytes 221192 | tf_op jit(solution)/shard_map/ppermute | solution.py:65
  399.7 18.5 %collective-permute-start.54 = (bf16[1,24,1536]{2,1,0:T(8,128)(2,1)S(1)}, bf16[1,24,1536]{2,1,0:T(8,128)(2,1)S(1)}, u32[]{:S(2)}, u32[]{:S(2)}) collective-permute-start(bf16[1,24,1536]{2,1,0:T(8,128)(2,1)S(1)} %get-tuple-element.133), channel_id=1, source_target_pairs={{0,4},{2,6},{4,0},{6,2},{8,12},{10,14},{12,8},{14,10},{16,20},{18,... | collective-permute-start | bytes 221192 | tf_op jit(solution)/shard_map/ppermute | solution.py:65
  (160 other events, 1155.9 us)

commit v2 on v0

v2 whole, which is shorter than its diff:
```python
import jax
import jax.numpy as jnp
from jax import lax
from jax.experimental import pallas as pl
from jax.experimental.pallas import tpu as pltpu
from jax.sharding import PartitionSpec as P

HD = 64
BOTH = ("dp", "pair")
LOW = jnp.bfloat16


def hold(value, *others):
    others = [o for o in others if o is not None]
    return lax.optimization_barrier((value, *others))[0] if others else value


class Place:
    def __init__(self):
        self.chips = lax.axis_size("dp")
        fast = 1
        while (2 * fast) ** 3 <= self.chips:
            fast *= 2
        strides = []
        while (1 << len(strides)) < self.chips:
            strides.insert(0, self.chips >> (len(strides) + 1))
        strides = sorted(strides, reverse=True)
        self.fast = [b for b in strides if b < fast]
        self.mid = [b for b in strides if fast <= b < fast * fast]
        self.slow = [b for b in strides if b >= fast * fast]
        self.chip = lax.axis_index("dp")
        self.core = lax.axis_index("pair")
        self.where = jnp.stack([self.chip, self.core]).astype(jnp.int32)

    def swap(self, value, stride):
        return lax.ppermute(value, "dp", [(i, i ^ stride) for i in range(self.chips)])

    def swap_core(self, value):
        return lax.ppermute(value, "pair", [(0, 1), (1, 0)])


def kernel_call(body, grid, in_specs, out_specs, out_shape, cost, scratch=(), limit=None):
    flops, moved, special = cost
    return pl.pallas_call(
        body,
        grid_spec=pltpu.PrefetchScalarGridSpec(
            num_scalar_prefetch=1,
            grid=grid,
            in_specs=in_specs,
            out_specs=out_specs,
            scratch_shapes=scratch,
        ),
        out_shape=out_shape,
        cost_estimate=pl.CostEstimate(
            flops=flops, bytes_accessed=moved, transcendentals=special
        ),
        compiler_params=pltpu.CompilerParams(vmem_limit_bytes=limit or 32 * 2**20),
    )


def pack(place, arrays, spots, shape):
    def body(at, *refs):
        out = refs[-1]
        for i, begin, width, row, column in spots:
            value = refs[i][:, begin : begin + width]
            out[row : row + value.shape[0], column : column + width] = value

    moved = 2 * sum(a.size * a.dtype.itemsize for a in arrays)
    return kernel_call(
        body,
        (1,),
        [pl.BlockSpec(a.shape, lambda i, at: (0, 0)) for a in arrays],
        pl.BlockSpec(shape, lambda i, at: (0, 0)),
        jax.ShapeDtypeStruct(shape, arrays[0].dtype),
        (0, moved, 0),
    )(place.where, *arrays)


class Gather:
    def __init__(self, place, rows):
        self.place = place
        self.slots = rows[None]
        self.left = place.slow + place.mid + place.fast
        self.right = place.slow + place.fast + place.mid
        self.stage = 0
        self.halves = None

    def step(self, before=(), during=()):
        place, stage = self.place, self.stage
        self.stage += 1
        if stage < len(place.slow):
            value = hold(self.slots, *before)
            got = hold(place.swap(value, self.left[stage]), *during)
            self.slots = jnp.concatenate([value, got])
            return got
        if stage < len(self.left):
            if self.halves is None:
                half = self.slots.shape[-1] // 2
                self.halves = (self.slots[..., :half], self.slots[..., half:])
            l, r = (hold(v, *before) for v in self.halves)
            gl = hold(place.swap(l, self.left[stage]), *during)
            gr = hold(place.swap(r, self.right[stage]), *during)
            self.halves = (jnp.concatenate([l, gl]), jnp.concatenate([r, gr]))
            return gr
        self.own = hold(jnp.stack(self.halves), *before)
        self.other = hold(place.swap_core(self.own), *during)
        return self.other

    def done(self, parts):
        place = self.place
        _, chips, rows, half = self.own.shape
        orders = (self.left, self.right)

        def body(at, own, other, *outs):
            chip, core = at[0], at[1]
            for side in range(2):

                def put(j, carry):
                    to = chip
                    for i, stride in enumerate(orders[side]):
                        to = to ^ (((j >> i) & 1) * stride)
                    begin = 0
                    for out, width in zip(outs, parts):
                        cols = slice(side * width, (side + 1) * width)
                        out[2 * to + core, :, cols] = own[side, j, :, begin : begin + width]
                        out[2 * to + 1 - core, :, cols] = other[side, j, :, begin : begin + width]
                        begin += width
                    return carry

                lax.fori_loop(0, chips, put, 0)

        moved = 8 * chips * rows * half * 2
        whole = pl.BlockSpec((2, chips, rows, half), lambda i, at: (0, 0, 0, 0))
        outs = kernel_call(
            body,
            (1,),
            [whole, whole],
            [pl.BlockSpec((2 * chips, rows, 2 * w), lambda i, at: (0, 0, 0)) for w in parts],
            [jax.ShapeDtypeStruct((2 * chips, rows, 2 * w), LOW) for w in parts],
            (0, moved, 0),
        )(place.where, self.own, self.other)
        return [o.reshape(-1, o.shape[-1]) for o in outs]


def fold(place, keeps, gots, bits, join):
    sides = len(bits)
    deep = keeps[0].ndim == 4
    chips, rows, cols = keeps[0].shape[-3:]
    steps = next(s for s in (3, 2, 1) if rows % (8 * s) == 0)
    part = rows // steps

    def body(at, *refs):
        ins, outs = refs[: 2 * len(keeps)], refs[2 * len(keeps) :]
        for side in range(sides):
            for j in range(chips):
                if deep:
                    a, b = ins[0][side, j], ins[1][side, j]
                else:
                    a, b = ins[side][j], ins[len(keeps) + side][j]
                total = (a.astype(jnp.float32) + b.astype(jnp.float32)).astype(LOW)
                low = bits[side]
                to = (j // (2 * low)) * low + j % low
                goes = (j // low) % 2
                if join:
                    outs[goes][to, :, side * cols : (side + 1) * cols] = total
                else:
                    outs[goes * sides + side][to] = total

    if deep:
        ins = pl.BlockSpec((2, chips, part, cols), lambda i, at: (0, 0, i, 0))
    else:
        ins = pl.BlockSpec((chips, part, cols), lambda i, at: (0, i, 0))
    wide = cols * sides if join else cols
    count = 2 if join else 2 * sides
    outs = kernel_call(
        body,
        (steps,),
        [ins] * (2 * len(keeps)),
        [pl.BlockSpec((chips // 2, part, wide), lambda i, at: (0, i, 0))] * count,
        [jax.ShapeDtypeStruct((chips // 2, rows, wide), LOW)] * count,
        (0, 6 * sides * chips * rows * cols, 0),
    )(place.where, *keeps, *gots)
    return list(outs[: count // 2]), list(outs[count // 2 :])


class Scatter:
    def __init__(self, place, keep, send):
        self.place = place
        self.keeps, self.sends = [keep], [send]
        self.left = (place.slow + place.mid + place.fast)[::-1]
        self.right = (place.slow + place.fast + place.mid)[::-1]
        self.held = [sorted(self.left), sorted(self.right)]
        self.stage = -1
        self.result = None
        self.gots = None

    def step(self, before=(), during=()):
        place = self.place
        if self.gots is not None:
            orders = (self.left, self.right)
            crossing = len(self.left) - len(place.slow)
            sides = 2 if self.stage <= crossing else 1
            bits = []
            for side in range(sides):
                stride = orders[side][self.stage]
                bits.append(1 << self.held[side].index(stride))
                self.held[side].remove(stride)
            join = self.stage == crossing
            self.keeps, self.sends = fold(place, self.keeps, self.gots, bits, join)
        swaps = (
            [place.swap_core]
            if self.stage < 0
            else [lambda v, b=o[self.stage]: place.swap(v, b) for o in (self.left, self.right)]
        )
        self.gots = [
            hold(swap(hold(v, *before)), *during) for v, swap in zip(self.sends, swaps)
        ]
        self.stage += 1
        if self.stage == len(self.left):
            self.result = self.keeps[0][0].astype(jnp.float32) + self.gots[0][0].astype(jnp.float32)
        return self.gots[-1]


def weight_terms(place, lefts, rights, rows):
    chips = place.chips
    count = len(lefts)
    length, features = lefts[0].shape
    joined = not isinstance(rights, list)
    width = rights.shape[1] // count if joined else rights[0].shape[1]
    per = count // 2
    unique = []
    for l in lefts:
        if not any(l is u for u in unique):
            unique.append(l)
    which = [next(i for i, u in enumerate(unique) if u is l) for l in lefts]
    rights = [rights] if joined else rights

    def body(at, *refs):
        ins, (keep, send) = refs[:-2], refs[-2:]
        t = pl.program_id(0)
        chip, core = at[0], at[1]

        def one(left, right):
            total = lax.dot_general(
                left[...], right[...], (((0,), (0,)), ((), ())), preferred_element_type=jnp.float32
            )
            for c in range(chips):
                to = c ^ chip
                a = total[2 * c * rows : (2 * c + 1) * rows].astype(LOW)
                b = total[(2 * c + 1) * rows : (2 * c + 2) * rows].astype(LOW)
                keep[0, to] = jnp.where(core == 0, a, b)
                send[0, to] = jnp.where(core == 0, b, a)

        if joined:
            one(ins[0], ins[1])
        else:
            for k in range(count):
                pl.when(t == k)(lambda k=k: one(ins[which[k]], ins[len(unique) + k]))

    block = pl.BlockSpec((1, chips, rows, width), lambda t, at: (t // per, 0, 0, t % per))
    shape = jax.ShapeDtypeStruct((2, chips, rows, width * per), LOW)
    fixed = pl.BlockSpec((length, width), lambda t, at: (0, 0))
    return kernel_call(
        body,
        (count,),
        [pl.BlockSpec((length, features), lambda t, at: (0, 0)) for _ in unique]
        + ([pl.BlockSpec((length, width), lambda t, at: (0, t))] if joined else [fixed] * count),
        [block, block],
        [shape, shape],
        (2 * count * length * features * width, 4 * count * features * width, 0),
    )(place.where, *unique, *rights)


def weight_terms_tall(place, left, right, rows):
    chips = place.chips
    length, features = left.shape
    width = right.shape[1]
    tiles = 4
    group = chips // tiles

    def body(at, left_ref, right_ref, keep, send):
        chip, core = at[0], at[1]
        total = lax.dot_general(
            left_ref[...], right_ref[...], (((0,), (0,)), ((), ())), preferred_element_type=jnp.float32
        )
        for c in range(group):
            to = c ^ (chip % group)
            a = total[2 * c * rows : (2 * c + 1) * rows].astype(LOW)
            b = total[(2 * c + 1) * rows : (2 * c + 2) * rows].astype(LOW)
            own, other = jnp.where(core == 0, a, b), jnp.where(core == 0, b, a)
            for side in range(2):
                cols = slice(side * (width // 2), (side + 1) * (width // 2))
                keep[side, to] = own[:, cols]
                send[side, to] = other[:, cols]

    block = pl.BlockSpec((2, group, rows, width // 2), lambda t, at: (0, t, 0, 0))
    shape = jax.ShapeDtypeStruct((2, chips, rows, width // 2), LOW)
    return kernel_call(
        body,
        (tiles,),
        [
            pl.BlockSpec((length, features // tiles), lambda t, at: (0, t ^ (at[0] // group))),
            pl.BlockSpec((length, width), lambda t, at: (0, 0)),
        ],
        [block, block],
        [shape, shape],
        (2 * length * features * width, 4 * features * width, 0),
    )(place.where, left, right)


class Total:
    def __init__(self, place, value):
        self.place, self.value = place, value
        self.strides = [0] + place.fast + place.mid + place.slow

    def step(self, before=(), during=()):
        value = hold(self.value, *before)
        stride = self.strides.pop(0)
        got = hold(self.place.swap(value, stride) if stride else self.place.swap_core(value), *during)
        self.value = value + got
        return got


def attention_forward(place, start, weights, query_bias, value_bias, seqs):
    rows, width = start.shape
    length = rows // seqs
    cols = 4 * HD
    groups = width // cols

    def body(at, start, wq, wk, wv, qb, vb, query, key, value, context, lse):
        x = start[...]
        dot = lambda l, r: jnp.dot(l, r, preferred_element_type=jnp.float32)
        query[...] = (dot(x, wq[...]) + qb[...]).astype(LOW)
        key[...] = dot(x, wk[...]).astype(LOW)
        value[...] = (dot(x, wv[...]) + vb[...]).astype(LOW)
        lane = lax.broadcasted_iota(jnp.int32, (length, 2 * HD), 1)
        for pair in range(2):
            at_cols = slice(pair * 2 * HD, (pair + 1) * 2 * HD)
            q, k = query[:, at_cols], key[:, at_cols]
            v_across = value[:, at_cols].T
            mixed = []
            for h in range(2):
                mine = (lane < HD) if h == 0 else (lane >= HD)
                q_mine = jnp.where(mine, q * jnp.asarray(HD**-0.5, LOW), jnp.zeros_like(q))
                scores = lax.dot_general(
                    k, q_mine, (((1,), (1,)), ((), ())), preferred_element_type=jnp.float32
                )
                most = jnp.max(scores, axis=0, keepdims=True)
                raised = jnp.exp(scores - most)
                total = jnp.sum(raised, axis=0, keepdims=True)
                probs = (raised * (1.0 / total)).astype(LOW)
                mixed.append(dot(v_across[h * HD : (h + 1) * HD], probs))
                lse[0, 0, 2 * pair + h : 2 * pair + h + 1, :] = most + jnp.log(total)
            context[:, at_cols] = jnp.concatenate(mixed, axis=0).T.astype(LOW)

    block = pl.BlockSpec((length, cols), lambda s, g, at: (s, g))
    weight = pl.BlockSpec((width, cols), lambda s, g, at: (0, g))
    bias = pl.BlockSpec((1, cols), lambda s, g, at: (0, g))
    table = jax.ShapeDtypeStruct((rows, width), LOW)
    return kernel_call(
        body,
        (seqs, groups),
        [pl.BlockSpec((length, width), lambda s, g, at: (s, 0)), weight, weight, weight, bias, bias],
        [block] * 4 + [pl.BlockSpec((1, 1, 4, length), lambda s, g, at: (s, g, 0, 0))],
        [table] * 4 + [jax.ShapeDtypeStruct((seqs, groups, 4, length), jnp.float32)],
        (6 * rows * width * width, 6 * width * width, seqs * groups * 4 * length * length),
    )(place.where, start, *weights, query_bias, value_bias)


def attention_backward(place, query, key, value, grad_context, lse):
    rows, width = query.shape
    seqs, groups, _, length = lse.shape
    cols = 4 * HD

    def body(at, query, key, value, grad, lse, dq, dk, dv, dq_sum, dv_sum):
        dot = lambda l, r: jnp.dot(l, r, preferred_element_type=jnp.float32)
        dot_t = lambda l, r: lax.dot_general(
            l, r, (((1,), (1,)), ((), ())), preferred_element_type=jnp.float32
        )
        lane = lax.broadcasted_iota(jnp.int32, (length, 2 * HD), 1)
        for pair in range(2):
            at_cols = slice(pair * 2 * HD, (pair + 1) * 2 * HD)
            q, k, v, g = query[:, at_cols], key[:, at_cols], value[:, at_cols], grad[:, at_cols]
            k_across = k.T
            dqs, dks, dvs = [], [], []
            for h in range(2):
                mine = (lane < HD) if h == 0 else (lane >= HD)
                none = jnp.zeros_like(q)
                scaled = jnp.where(mine, q * jnp.asarray(HD**-0.5, LOW), none)
                scores = dot_t(k, scaled)
                probs = jnp.exp(scores - lse[0, 0, 2 * pair + h : 2 * pair + h + 1, :])
                grad_probs = dot_t(v, jnp.where(mine, g, none))
                dvs.append(dot(probs.astype(LOW), g))
                inner = jnp.sum(probs * grad_probs, axis=0, keepdims=True)
                grad_scores = (probs * (grad_probs - inner)).astype(LOW)
                dks.append(dot(grad_scores, q))
                dqs.append(dot(k_across[h * HD : (h + 1) * HD], grad_scores))
            scale = HD**-0.5
            dq_low = (jnp.concatenate(dqs, axis=0).T * scale).astype(LOW)
            dk_low = (jnp.where(lane < HD, dks[0], dks[1]) * scale).astype(LOW)
            dv_low = jnp.where(lane < HD, dvs[0], dvs[1]).astype(LOW)
            dq[:, at_cols], dk[:, at_cols], dv[:, at_cols] = dq_low, dk_low, dv_low
            for total, term in ((dq_sum, dq_low), (dv_sum, dv_low)):
                term = jnp.sum(term.astype(jnp.float32), axis=0, keepdims=True)

                @pl.when(pl.program_id(1) == 0)
                def _(total=total, term=term):
                    total[:, at_cols] = term

                @pl.when(pl.program_id(1) > 0)
                def _(total=total, term=term):
                    total[:, at_cols] += term

    block = pl.BlockSpec((length, cols), lambda g, s, at: (s, g))
    total = pl.BlockSpec((1, cols), lambda g, s, at: (0, g))
    table = jax.ShapeDtypeStruct((rows, width), LOW)
    sums = jax.ShapeDtypeStruct((1, width), jnp.float32)
    return kernel_call(
        body,
        (groups, seqs),
        [block] * 4 + [pl.BlockSpec((1, 1, 4, length), lambda g, s, at: (s, g, 0, 0))],
        [block] * 3 + [total] * 2,
        [table] * 3 + [sums] * 2,
        (10 * rows * length * width, 14 * rows * width, rows * length * width // HD),
    )(place.where, query, key, value, grad_context, lse)


def normalised(value):
    centered = value - jnp.mean(value, axis=-1, keepdims=True)
    inverse = lax.rsqrt(jnp.mean(centered * centered, axis=-1, keepdims=True) + 1e-12)
    return centered * inverse, inverse


def normalised_back(grad, unit, inverse, gain):
    inner = grad * gain
    mean = jnp.mean(inner, axis=-1, keepdims=True)
    along = jnp.mean(inner * unit, axis=-1, keepdims=True)
    return (
        inverse * (inner - mean - unit * along),
        jnp.sum(grad * unit, axis=0, keepdims=True),
        jnp.sum(grad, axis=0, keepdims=True),
    )


def feed_in(place, start, context, wo, output_bias, gain, shift, wi, inner_bias):
    rows, width = start.shape
    inner = wi.shape[1]
    tile = width

    def body(at, start, context, wo, ob, gain, shift, wi, ib, unit, inverse, normed_low, active, slope):
        @pl.when(pl.program_id(0) == 0)
        def _():
            first = (
                start[...].astype(jnp.float32)
                + jnp.dot(context[...], wo[...], preferred_element_type=jnp.float32)
                + ob[...]
            )
            u, i = normalised(first)
            unit[...] = u
            inverse[...] = i
            normed_low[...] = (u * gain[...] + shift[...]).astype(LOW)

        for part in range(4):
            cut = slice(part * tile // 4, (part + 1) * tile // 4)
            hidden = (
                jnp.dot(normed_low[...], wi[:, cut], preferred_element_type=jnp.float32) + ib[:, cut]
            )
            below = 0.5 + 0.5 * lax.erf(hidden * 0.7071067811865476)
            active[:, cut] = (hidden * below).astype(LOW)
            bell = jnp.exp(hidden * hidden * -0.5) * 0.3989422804014327
            slope[:, cut] = (below + hidden * bell).astype(LOW)

    keep = lambda a: pl.BlockSpec(a.shape, lambda t, at: (0, 0))
    column = pl.BlockSpec((rows, tile), lambda t, at: (0, t))
    shapes = [
        jax.ShapeDtypeStruct((rows, width), jnp.float32),
        jax.ShapeDtypeStruct((rows, 1), jnp.float32),
        jax.ShapeDtypeStruct((rows, width), LOW),
        jax.ShapeDtypeStruct((rows, inner), LOW),
        jax.ShapeDtypeStruct((rows, inner), LOW),
    ]
    ins = (start, context, wo, output_bias, gain, shift)
    return kernel_call(
        body,
        (inner // tile,),
        [keep(a) for a in ins]
        + [
            pl.BlockSpec((width, tile), lambda t, at: (0, t)),
            pl.BlockSpec((1, tile), lambda t, at: (0, t)),
        ],
        [keep(s) for s in shapes[:3]] + [column, column],
        shapes,
        (2 * rows * width * (width + inner), 2 * width * inner, 2 * rows * inner),
    )(place.where, *ins, wi, inner_bias)


def feed_out(place, active, wu, outer_bias, unit, gain_one, shift_one, gain, shift, cotangent, wanted):
    rows, width = unit.shape
    inner = active.shape[1]
    tile = width
    steps = inner // tile

    def body(at, active, wu, ob, unit, g1, s1, g2, s2, cot, wanted, out, grad, branch, ob_g, g2_g, s2_g, total):
        t = pl.program_id(0)
        term = jnp.dot(active[...], wu[...], preferred_element_type=jnp.float32)

        @pl.when(t == 0)
        def _():
            total[...] = unit[...] * g1[...] + s1[...] + ob[...] + term

        @pl.when(t > 0)
        def _():
            total[...] += term

        @pl.when(t == steps - 1)
        def _():
            u, i = normalised(total[...])
            out[...] = (u * g2[...] + s2[...]).astype(LOW)
            grad_out = cot[...].astype(jnp.float32) * wanted[...]
            back, gain_grad, shift_grad = normalised_back(grad_out, u, i, g2[...])
            grad[...] = back
            low = back.astype(LOW)
            branch[...] = low
            ob_g[...] = jnp.sum(low.astype(jnp.float32), axis=0, keepdims=True)
            g2_g[...] = gain_grad
            s2_g[...] = shift_grad

    keep = lambda a: pl.BlockSpec(a.shape, lambda t, at: (0, 0))
    row = jax.ShapeDtypeStruct((1, width), jnp.float32)
    shapes = [
        jax.ShapeDtypeStruct((rows, width), LOW),
        jax.ShapeDtypeStruct((rows, width), jnp.float32),
        jax.ShapeDtypeStruct((rows, width), LOW),
        row,
        row,
        row,
    ]
    ins = (outer_bias, unit, gain_one, shift_one, gain, shift, cotangent, wanted)
    return kernel_call(
        body,
        (steps,),
        [
            pl.BlockSpec((rows, tile), lambda t, at: (0, t)),
            pl.BlockSpec((tile, width), lambda t, at: (t, 0)),
        ]
        + [keep(a) for a in ins],
        [keep(s) for s in shapes],
        shapes,
        (2 * rows * width * inner, 2 * width * inner, 0),
        [pltpu.VMEM((rows, width), jnp.float32)],
    )(place.where, active, wu, *ins)


def hidden_back(place, grad_branch, wu, slope):
    rows, width = grad_branch.shape
    inner = wu.shape[0]
    tile = width

    def body(at, grad, wu, slope, out, sums):
        back = lax.dot_general(
            grad[...], wu[...], (((1,), (1,)), ((), ())), preferred_element_type=jnp.float32
        )
        low = (back * slope[...].astype(jnp.float32)).astype(LOW)
        out[...] = low
        sums[...] = jnp.sum(low.astype(jnp.float32), axis=0, keepdims=True)

    column = pl.BlockSpec((rows, tile), lambda t, at: (0, t))
    return kernel_call(
        body,
        (inner // tile,),
        [
            pl.BlockSpec((rows, width), lambda t, at: (0, 0)),
            pl.BlockSpec((tile, width), lambda t, at: (t, 0)),
            column,
        ],
        [column, pl.BlockSpec((1, tile), lambda t, at: (0, t))],
        [jax.ShapeDtypeStruct((rows, inner), LOW), jax.ShapeDtypeStruct((1, inner), jnp.float32)],
        (2 * rows * width * inner, 2 * width * inner, 0),
    )(place.where, grad_branch, wu, slope)


def first_back(place, grad_hidden, wi, grad_second, unit, inverse, gain, wo):
    rows, width = grad_second.shape
    inner = wi.shape[1]
    tile = width
    steps = inner // tile

    def body(at, gh, wi, second, unit, inverse, gain, wo, first, low_out, context, ob_g, g_g, s_g, total):
        t = pl.program_id(0)
        term = lax.dot_general(
            gh[...], wi[...], (((1,), (1,)), ((), ())), preferred_element_type=jnp.float32
        )

        @pl.when(t == 0)
        def _():
            total[...] = second[...] + term

        @pl.when(t > 0)
        def _():
            total[...] += term

        @pl.when(t == steps - 1)
        def _():
            back, gain_grad, shift_grad = normalised_back(
                total[...], unit[...], inverse[...], gain[...]
            )
            first[...] = back
            low = back.astype(LOW)
            low_out[...] = low
            ob_g[...] = jnp.sum(low.astype(jnp.float32), axis=0, keepdims=True)
            g_g[...] = gain_grad
            s_g[...] = shift_grad
            context[...] = lax.dot_general(
                low, wo[...], (((1,), (1,)), ((), ())), preferred_element_type=jnp.float32
            ).astype(LOW)

    keep = lambda a: pl.BlockSpec(a.shape, lambda t, at: (0, 0))
    row = jax.ShapeDtypeStruct((1, width), jnp.float32)
    shapes = [
        jax.ShapeDtypeStruct((rows, width), jnp.float32),
        jax.ShapeDtypeStruct((rows, width), LOW),
        jax.ShapeDtypeStruct((rows, width), LOW),
        row,
        row,
        row,
    ]
    ins = (grad_second, unit, inverse, gain, wo)
    return kernel_call(
        body,
        (steps,),
        [
            pl.BlockSpec((rows, tile), lambda t, at: (0, t)),
            pl.BlockSpec((width, tile), lambda t, at: (0, t)),
        ]
        + [keep(a) for a in ins],
        [keep(s) for s in shapes],
        shapes,
        (2 * rows * width * (inner + width), 2 * width * inner, 0),
        [pltpu.VMEM((rows, width), jnp.float32)],
    )(place.where, grad_hidden, wi, *ins)


def start_back(place, grad_first, grads, weights, masked):
    rows, width = grad_first.shape

    def body(at, first, dq, dk, dv, wq, wk, wv, masked, out, sums):
        total = first[...]
        for grad, weight in ((dq, wq), (dk, wk), (dv, wv)):
            total += lax.dot_general(
                grad[...], weight[...], (((1,), (1,)), ((), ())), preferred_element_type=jnp.float32
            )
        hidden = masked[...] > 0.0
        out[...] = jnp.where(hidden, 0.0, total).astype(LOW)
        sums[...] = jnp.sum(jnp.where(hidden, total, 0.0), axis=0, keepdims=True)

    ins = (grad_first, *grads, *weights, masked)
    shapes = [jax.ShapeDtypeStruct((rows, width), LOW), jax.ShapeDtypeStruct((1, width), jnp.float32)]
    return kernel_call(
        body,
        (1,),
        [pl.BlockSpec(a.shape, lambda t, at: (0, 0)) for a in ins],
        [pl.BlockSpec(s.shape, lambda t, at: (0, 0)) for s in shapes],
        shapes,
        (6 * rows * width * width, 6 * width * width, 0),
    )(place.where, *ins)


class PlainGather:
    def __init__(self, rows):
        self.rows = rows

    def step(self, before=(), during=()):
        return None

    def done(self, parts):
        whole = lax.all_gather(self.rows, BOTH, axis=0, tiled=True)
        half = whole.shape[1] // 2
        outs, begin = [], 0
        for width in parts:
            outs.append(
                jnp.concatenate(
                    [whole[:, s * half + begin : s * half + begin + width] for s in range(2)], axis=1
                )
            )
            begin += width
        return outs


class PlainScatter:
    def __init__(self, term):
        self.result = lax.psum_scatter(term, BOTH, scatter_dimension=0, tiled=True)

    def step(self, before=(), during=()):
        return None


class PlainTotal:
    def __init__(self, value):
        self.value = lax.psum(value, BOTH)
        self.strides = [0]

    def step(self, before=(), during=()):
        self.strides.pop(0)


def outer_sum(left, right):
    return jnp.einsum("rd,re->de", left, right, preferred_element_type=jnp.float32)


def halves(place, arrays):
    spots, column = [], 0
    for side in range(2):
        for i, a in enumerate(arrays):
            half = a.shape[1] // 2
            spots.append((i, side * half, half, 0, column))
            column += half
    return pack(place, arrays, spots, (arrays[0].shape[0], column))


def on_device(
    tokens,
    span_starts,
    span_lengths,
    mask_embed,
    query_weight,
    key_weight,
    value_weight,
    output_weight,
    inner_weight,
    outer_weight,
    query_bias,
    value_bias,
    output_bias,
    inner_bias,
    outer_bias,
    gain_one,
    shift_one,
    gain_two,
    shift_two,
    cotangent,
):
    rows, width = tokens.shape
    seqs = span_starts.shape[0]
    length = rows // seqs
    inner = inner_weight.shape[1]
    own_rows, own_tall = query_weight.shape[0], outer_weight.shape[0]
    place = Place()
    staged = own_rows % 8 == 0 and place.chips & (place.chips - 1) == 0
    gather = (lambda piece: Gather(place, piece)) if staged else PlainGather

    first_gather = gather(halves(place, (query_weight, key_weight, value_weight)))
    inner_gather = gather(halves(place, (output_weight, inner_weight)))
    outer_gather = gather(outer_weight)
    first_gather.step()
    places = jnp.arange(length, dtype=jnp.int32)[None, :, None]
    begins = span_starts[:, None, :]
    finish = begins + span_lengths[:, None, :]
    masked = jnp.any((places >= begins) & (places < finish), axis=2)
    edges = jnp.any((places == begins - 1) | (places == finish), axis=2)
    masked = masked.reshape(rows)
    wanted = (masked | edges.reshape(rows)).astype(jnp.float32)[:, None]
    start = jnp.where(masked[:, None], mask_embed[None, :], tokens)
    masked = masked.astype(jnp.float32)[:, None]
    vectors = (
        query_bias,
        value_bias,
        output_bias,
        inner_bias,
        outer_bias,
        gain_one,
        shift_one,
        gain_two,
        shift_two,
    )
    vectors = tuple(v[None] for v in vectors)
    query_row, value_row, output_row, inner_row, outer_row, gain_1, shift_1, gain_2, shift_2 = vectors
    got = first_gather.step(during=(*vectors, start, masked, wanted))
    inner_gather.step((got,))
    got = first_gather.step()
    inner_gather.step((got,))
    got = first_gather.step()
    outer_gather.step((got,))
    inner_gather.step((got,))
    got = first_gather.step()
    weights = first_gather.done((width // 2,) * 3)
    query, key, value, context, lse = attention_forward(
        place, start, weights, query_row, value_row, seqs
    )
    inner_gather.step((got,), (context,))
    outer_gather.step((got,), (context,))
    got = outer_gather.step((context,))
    inner_gather.step((context,))
    wo, wi = inner_gather.done((width // 2, inner // 2))
    unit, inverse, normed_low, active, slope = feed_in(
        place, start, hold(context, got), wo, output_row, gain_1, shift_1, wi, inner_row
    )
    outer_gather.step((), (active,))
    outer_gather.step()
    (wu,) = outer_gather.done((width // 2,))
    layer_output, grad_second, grad_branch, outer_bias_grad, gain_two_grad, shift_two_grad = feed_out(
        place, active, wu, outer_row, unit, gain_1, shift_1, gain_2, shift_2, cotangent, wanted
    )
    if staged:
        outer_sums = Scatter(place, *weight_terms_tall(place, active, grad_branch, own_tall))
        grad_branch = hold(grad_branch, *outer_sums.sends)
    else:
        outer_sums = PlainScatter(outer_sum(active, grad_branch))
    grad_hidden, inner_bias_grad = hidden_back(place, grad_branch, wu, slope)
    got = outer_sums.step((), (grad_hidden,))
    if staged:
        tiles = inner // width
        inner_sums = Scatter(
            place, *weight_terms(place, [normed_low] * tiles, hold(grad_hidden, got), own_rows)
        )
        grad_hidden = hold(grad_hidden, *inner_sums.sends)
    else:
        inner_sums = PlainScatter(outer_sum(normed_low, grad_hidden))
    grad_first, grad_attended, grad_context, output_bias_grad, gain_one_grad, shift_one_grad = first_back(
        place, grad_hidden, wi, grad_second, unit, inverse, gain_1, wo
    )
    got = outer_sums.step((), (grad_context,))
    grad_query, grad_key, grad_value, query_bias_grad, value_bias_grad = attention_backward(
        place, query, key, value, hold(grad_context, got), lse
    )
    got = outer_sums.step((), (grad_query,))
    inner_sums.step((grad_context,), (grad_query,))
    lefts = [start, start, start, context]
    rights = [hold(grad_query, got), grad_key, grad_value, grad_attended]
    if staged:
        first_sums = Scatter(place, *weight_terms(place, lefts, rights, own_rows))
        grad_query = hold(grad_query, *first_sums.sends)
    else:
        first_sums = PlainScatter(
            jnp.concatenate([outer_sum(l, r) for l, r in zip(lefts, rights)], axis=1)
        )
    input_grad, mask_grad = start_back(
        place, grad_first, (grad_query, grad_key, grad_value), weights, masked
    )
    got_outer = outer_sums.step((), (mask_grad,))
    got = inner_sums.step((), (mask_grad,))
    first_sums.step((), (mask_grad,))
    smalls = (
        query_bias_grad,
        value_bias_grad,
        output_bias_grad,
        outer_bias_grad,
        gain_one_grad,
        shift_one_grad,
        gain_two_grad,
        shift_two_grad,
        mask_grad,
        inner_bias_grad,
    )
    spots = [(i, 0, width, i, 0) for i in range(9)]
    spots += [(9, i * width, width, 9 + i, 0) for i in range(inner // width)]
    high = -(-(9 + inner // width) // 8) * 8
    packed = pack(place, smalls, spots, (high, width))
    total = Total(place, packed) if staged else PlainTotal(packed)
    got = inner_sums.step((got,))
    got = first_sums.step((got_outer,))
    outer_sums.step((got_outer,))
    if staged:
        total.step((got_outer,))
        inner_sums.step((got,))
        got = first_sums.step((got,))
        total.step()
        got = first_sums.step()
        inner_sums.step((got,))
        total.step()
        got = first_sums.step()
        total.step()
        total.step()
    else:
        total.step()
    packed = total.value
    order = (0, 1, 2, 9, 3, 4, 5, 6, 7, 8)
    firsts = first_sums.result
    return (
        layer_output,
        input_grad,
        *(firsts[:, i * width : (i + 1) * width] for i in range(4)),
        inner_sums.result,
        outer_sums.result,
        *(packed[9:9 + inner // width].reshape(-1) if i == 9 else packed[i] for i in order),
    )


def solution(mesh):
    placed = (
        P(("dp", "pair"), None),
        P(("dp", "pair"), None),
        P(("dp", "pair"), None),
        P(),
        P(("dp", "pair"), None),
        P(("dp", "pair"), None),
        P(("dp", "pair"), None),
        P(("dp", "pair"), None),
        P(("dp", "pair"), None),
        P(("dp", "pair"), None),
        P(),
        P(),
        P(),
        P(),
        P(),
        P(),
        P(),
        P(),
        P(),
        P(("dp", "pair"), None),
    )
    return jax.shard_map(
        on_device,
        mesh=mesh,
        in_specs=placed,
        out_specs=(
            P(("dp", "pair"), None),
            P(("dp", "pair"), None),
            P(("dp", "pair"), None),
            P(("dp", "pair"), None),
            P(("dp", "pair"), None),
            P(("dp", "pair"), None),
            P(("dp", "pair"), None),
            P(("dp", "pair"), None),
            P(),
            P(),
            P(),
            P(),
            P(),
            P(),
            P(),
            P(),
            P(),
            P(),
        ),
        check_vma=False,
    )
```

time: 1100 us -> 293 us (0.27)
  waiting for transfers between devices: 897 us -> 116 us
  matrix products: 110 us -> 0 us
  Pallas kernels: 0 us -> 93.9 us
  starting transfers between devices: 0.65 us -> 48 us
  blocking collectives: 40.7 us -> 0 us
  between operations: 14.9 us -> 1.94 us
  local copies, waits for them, and re-layouts: 14.8 us -> 25.8 us
    reduce_scatter x6 -> x0, waiting for transfers between devices: 584 us -> none  [the longest x1 142 us: on_device(): lax.psum_scatter(inner_grad, ('dp', 'pair'), scatter_dimension=0, tiled=T...]
    all_gather x6 -> x0, waiting for transfers between devices: 309 us -> none  [the longest x1 61.5 us: on_device(): lax.all_gather(owned[4], ('dp', 'pair'), axis=0, tiled=True)]
    ppermute x0 -> x47, waiting for transfers between devices: none -> 116 us  [the longest x40 111 us: swap(): lax.ppermute(value, 'dp', [(i, i ^ stride) for i in range(self.chips)])]
    dot_general x24 -> x0, matrix products: 110 us -> none  [the longest x6 37 us: dense(): return jnp.dot(left, right, preferred_element_type=jnp.float32)]
    pallas_call x0 -> x28, Pallas kernels: none -> 93.9 us  [the longest x12 20.1 us: fold(): kernel_call(body, (steps,), [ins] * (2 * len(keeps)), [pl.BlockSpec((chip...]
    ppermute x0 -> x47, starting transfers between devices: none -> 48 us  [the longest x40 47 us: swap(): lax.ppermute(value, 'dp', [(i, i ^ stride) for i in range(self.chips)])]
    psum x1 -> x0, blocking collectives: 40.7 us -> none  [on_device(): lax.psum((query_bias_grad, value_bias_grad, output_bias_grad, inner_bias_...]
  transfers between devices with their start and end apart: 12 -> 47, of which waited for: 11 -> 27; matrix products, arithmetic and copies ran while one was open for 10% -> 4% of each run, Pallas kernels for 0% -> 24%
where the time goes in v2:
time: 293 us; the launch traced here: 292 us
  waiting for transfers between devices  116 us (40%)
  Pallas kernels  93.9 us (32%)
  starting transfers between devices  48 us (16%)
  local copies, waits for them, and re-layouts  25.8 us (9%)
  other arithmetic  7.01 us (2%)
    ppermute x40, waiting for transfers between devices, swap(): lax.ppermute(value, 'dp', [(i, i ^ stride) for i in range(self.chips)])  111 us
    ppermute x40, starting transfers between devices, swap(): lax.ppermute(value, 'dp', [(i, i ^ stride) for i in range(self.chips)])  47 us
    pallas_call x12, Pallas kernels, fold(): kernel_call(body, (steps,), [ins] * (2 * len(keeps)), [pl.BlockSpec((chip...  20.1 us
    unnamed x162, local copies, waits for them, and re-layouts  19.9 us
    pallas_call x1, Pallas kernels, attention_backward(): kernel_call(body, (groups, seqs), [block] * 4 + [pl.BlockSpec((1, 1, 4, l...  10.8 us
    pallas_call x2, Pallas kernels, weight_terms(): kernel_call(body, (count,), [pl.BlockSpec((length, features), lambda t, a...  10.4 us
    pallas_call x1, Pallas kernels, attention_forward(): kernel_call(body, (seqs, groups), [pl.BlockSpec((length, width), lambda s...  9.83 us
    pallas_call x1, Pallas kernels, feed_in(): kernel_call(body, (inner // tile,), [keep(a) for a in ins] + [pl.BlockSpe...  9.04 us
  transfers between devices with their start and end apart: 47, of which 27 were waited for; matrix products, arithmetic and copies ran while one was open for 4% of the time, Pallas kernels for 24%

profile of v2, /device:TPU:0, one launch (start us, length us, event | category | flops | bytes accessed | tf_op | source)
XLA Modules:
  0.0 292.3 jit_solution(3079990816773338942)
XLA Ops:
  3.7 4.1 %collective-permute-start = (bf16[1,24,2304]{2,1,0:T(8,128)(2,1)S(1)}, bf16[1,24,2304]{2,1,0:T(8,128)(2,1)S(1)}, u32[]{:S(2)}, u32[]{:S(2)}) collective-permute-start(bf16[1,24,2304]{2,1,0:T(8,128)(2,1)S(1)} %bitcast.51), channel_id=1, source_target_pairs={{0,16},{2,18},{4,20},{6,22},{8,24},{10,26},{12,28},{14,30},{16,0},... | collective-permute-start | bytes 331784 | tf_op jit(solution)/shard_map/ppermute | solution.py:36
  14.8 5.1 %collective-permute-done.1 = bf16[2,24,2304]{2,1,0:T(8,128)(2,1)S(1)} collective-permute-done((bf16[2,24,2304]{2,1,0:T(8,128)(2,1)S(1)}, bf16[2,24,2304]{2,1,0:T(8,128)(2,1)S(1)}, u32[]{:S(2)}, u32[]{:S(2)}) %collective-permute-start.1) | collective-permute-done | bytes 221216 | tf_op jit(solution)/shard_map/ppermute | solution.py:36
  19.9 3.1 %collective-permute-start.10 = (bf16[1,24,3840]{2,1,0:T(8,128)(2,1)S(1)}, bf16[1,24,3840]{2,1,0:T(8,128)(2,1)S(1)}, u32[]{:S(2)}, u32[]{:S(2)}) collective-permute-start(bf16[1,24,3840]{2,1,0:T(8,128)(2,1)S(1)} %bitcast.54), channel_id=1, source_target_pairs={{0,16},{2,18},{4,20},{6,22},{8,24},{10,26},{12,28},{14,30},{16,0},... | collective-permute-start | bytes 552968 | tf_op jit(solution)/shard_map/ppermute | solution.py:36
  26.2 5.0 %collective-permute-done.10 = bf16[1,24,3840]{2,1,0:T(8,128)(2,1)S(1)} collective-permute-done((bf16[1,24,3840]{2,1,0:T(8,128)(2,1)S(1)}, bf16[1,24,3840]{2,1,0:T(8,128)(2,1)S(1)}, u32[]{:S(2)}, u32[]{:S(2)}) %collective-permute-start.10) | collective-permute-done | bytes 184352 | tf_op jit(solution)/shard_map/ppermute | solution.py:36
  35.4 7.2 %collective-permute-done.3 = bf16[8,24,1152]{2,1,0:T(8,128)(2,1)S(1)} collective-permute-done((bf16[8,24,1152]{2,1,0:T(8,128)(2,1)S(1)}, bf16[8,24,1152]{2,1,0:T(8,128)(2,1)S(1)}, u32[]{:S(2)}, u32[]{:S(2)}) %collective-permute-start.3) | collective-permute-done | bytes 442400 | tf_op jit(solution)/shard_map/ppermute | solution.py:36
  46.5 8.9 %collective-permute-done.14 = bf16[4,24,1920]{2,1,0:T(8,128)(2,1)S(1)} collective-permute-done((bf16[4,24,1920]{2,1,0:T(8,128)(2,1)S(1)}, bf16[4,24,1920]{2,1,0:T(8,128)(2,1)S(1)}, u32[]{:S(2)}, u32[]{:S(2)}) %collective-permute-start.14) | collective-permute-done | bytes 368672 | tf_op jit(solution)/shard_map/ppermute | solution.py:36
  60.2 9.8 %shard_map.333 = (bf16[512,768]{1,0:T(8,128)(2,1)S(1)}, bf16[512,768]{1,0:T(8,128)(2,1)S(1)}, bf16[512,768]{1,0:T(8,128)(2,1)S(1)}, bf16[512,768]{1,0:T(8,128)(2,1)S(1)}, f32[1,3,4,512]{3,2,1,0:T(4,128)S(1)}) custom-call(s32[2]{0:T(128)S(1)} %pad_add_fusion.at, bf16[512,768]{1,0:T(8,128)(2,1)S(1)} %broadcast_select_fusion.start.refs_0_, ...), custom_call_target="tpu_custom_call" | custom-call | flops 1811939328 | bytes 3538944 | tf_op jit(solution)/shard_map/pallas_call | solution.py:360
  70.1 3.7 %collective-permute-done.15 = bf16[8,24,1920]{2,1,0:T(8,128)(2,1)S(1)} collective-permute-done((bf16[8,24,1920]{2,1,0:T(8,128)(2,1)S(1)}, bf16[8,24,1920]{2,1,0:T(8,128)(2,1)S(1)}, u32[]{:S(2)}, u32[]{:S(2)}) %collective-permute-start.15) | collective-permute-done | bytes 737312 | tf_op jit(solution)/shard_map/ppermute | solution.py:36
  76.2 9.8 %collective-permute-done.7 = bf16[1,96,768]{2,1,0:T(8,128)(2,1)S(1)} collective-permute-done((bf16[1,96,768]{2,1,0:T(8,128)(2,1)S(1)}, bf16[1,96,768]{2,1,0:T(8,128)(2,1)S(1)}, u32[]{:S(2)}, u32[]{:S(2)}) %collective-permute-start.7) | collective-permute-done | bytes 147488 | tf_op jit(solution)/shard_map/ppermute | solution.py:36
  86.2 8.0 %collective-permute-done.8 = bf16[2,96,768]{2,1,0:T(8,128)(2,1)S(1)} collective-permute-done((bf16[2,96,768]{2,1,0:T(8,128)(2,1)S(1)}, bf16[2,96,768]{2,1,0:T(8,128)(2,1)S(1)}, u32[]{:S(2)}, u32[]{:S(2)}) %collective-permute-start.8) | collective-permute-done | bytes 294944 | tf_op jit(solution)/shard_map/ppermute | solution.py:36
  96.2 5.3 %collective-permute-done.17 = bf16[4,96,384]{2,1,0:T(8,128)(2,1)S(1)} collective-permute-done((bf16[4,96,384]{2,1,0:T(8,128)(2,1)S(1)}, bf16[4,96,384]{2,1,0:T(8,128)(2,1)S(1)}, u32[]{:S(2)}, u32[]{:S(2)}) %collective-permute-start.17) | collective-permute-done | bytes 294944 | tf_op jit(solution)/shard_map/ppermute | solution.py:36
  105.7 9.0 %shard_map.336 = (f32[512,768]{1,0:T(8,128)S(1)}, f32[512,1]{1,0:T(8,128)S(1)}, bf16[512,768]{1,0:T(8,128)(2,1)S(1)}, bf16[512,3072]{1,0:T(8,128)(2,1)S(1)}, bf16[512,3072]{1,0:T(8,128)(2,1)S(1)}) custom-call(s32[2]{0:T(128)S(1)} %pad_add_fusion.at, bf16[512,768]{1,0:T(8,128)(2,1)S(1)} %broadcast_select_fusion.start.refs_0_, ...), custom_call_target="tpu_custom_call" | custom-call | flops 3019898880 | bytes 4718592 | tf_op jit(solution)/shard_map/pallas_call | solution.py:483
  122.2 3.1 %collective-permute-done.20.other = bf16[2,16,96,384]{3,2,1,0:T(8,128)(2,1)} collective-permute-done((bf16[2,16,96,384]{3,2,1,0:T(8,128)(2,1)S(1)}, bf16[2,16,96,384]{3,2,1,0:T(8,128)(2,1)}, u32[]{:S(2)}, u32[]{:S(2)}) %collective-permute-start.20) | collective-permute-done | bytes 2359328 | tf_op jit(solution)/shard_map/ppermute | solution.py:39
  125.2 2.9 shard_map.337
  128.2 7.1 %shard_map.338 = (bf16[512,768]{1,0:T(8,128)(2,1)}, f32[512,768]{1,0:T(8,128)S(1)}, bf16[512,768]{1,0:T(8,128)(2,1)S(1)}, f32[1,768]{1,0:T(1,128)S(1)}, f32[1,768]{1,0:T(1,128)S(1)}, /*index=5*/f32[1,768]{1,0:T(1,128)S(1)}) custom-call(s32[2]{0:T(128)S(1)} %pad_add_fusion.at, bf16[512,3072]{1,0:T(8,128)(2,1)S(1)} %copy-done.4, ...), custom_call_target="tpu_custom_call" | custom-call | flops 2415919104 | bytes 4718592 | tf_op jit(solution)/shard_map/pallas_call | solution.py:539
  136.4 4.7 %shard_map.339 = (bf16[2,16,96,384]{3,2,1,0:T(8,128)(2,1)S(1)}, bf16[2,16,96,384]{3,2,1,0:T(8,128)(2,1)S(1)}) custom-call(s32[2]{0:T(128)S(1)} %pad_add_fusion.at, bf16[512,3072]{1,0:T(8,128)(2,1)S(1)} %copy-done.4, bf16[512,768]{1,0:T(8,128)(2,1)S(1)} %get-tuple-element.170.right_ref.grad), custom_call_target="tpu_custom_call" | custom-call | flops 2415919104 | bytes 9437184 | tf_op jit(solution)/shard_map/pallas_call | solution.py:298
  141.4 4.7 %shard_map.340 = (bf16[512,3072]{1,0:T(8,128)(2,1)S(1)}, f32[1,3072]{1,0:T(1,128)S(1)}) custom-call(s32[2]{0:T(128)S(1)} %pad_add_fusion.at, bf16[512,768]{1,0:T(8,128)(2,1)S(1)} %get-tuple-element.170.right_ref.grad, bf16[3072,768]{1,0:T(8,128)(2,1)S(1)} %bitcast.38, bf16[512,3072]{1,0:T(8,128)(2,1)S(1)} %copy-done.55), custom_call_target="tpu_custom_call" | custom-call | flops 2415919104 | bytes 4718592 | tf_op jit(solution)/shard_map/pallas_call | solution.py:568
  149.5 5.3 %shard_map.341 = (bf16[2,16,24,1536]{3,2,1,0:T(8,128)(2,1)S(1)}, bf16[2,16,24,1536]{3,2,1,0:T(8,128)(2,1)}) custom-call(s32[2]{0:T(128)S(1)} %pad_add_fusion.at, bf16[512,768]{1,0:T(8,128)(2,1)S(1)} %copy-done.65, bf16[512,3072]{1,0:T(8,128)(2,1)S(1)} %get-tuple-element.177.refs_1_.gh), custom_call_target="tpu_custom_call" | custom-call | flops 2415919104 | bytes 9437184 | tf_op jit(solution)/shard_map/pallas_call | solution.py:263
  154.8 6.6 %shard_map.342 = (f32[512,768]{1,0:T(8,128)S(1)}, bf16[512,768]{1,0:T(8,128)(2,1)S(1)}, bf16[512,768]{1,0:T(8,128)(2,1)S(1)}, f32[1,768]{1,0:T(1,128)S(1)}, f32[1,768]{1,0:T(1,128)S(1)}, /*index=5*/f32[1,768]{1,0:T(1,128)S(1)}) custom-call(s32[2]{0:T(128)S(1)} %pad_add_fusion.at, bf16[512,3072]{1,0:T(8,128)(2,1)S(1)} %get-tuple-element.177.refs_1_.gh, ...), custom_call_target="tpu_custom_call" | custom-call | flops 3019898880 | bytes 4718592 | tf_op jit(solution)/shard_map/pallas_call | solution.py:628
  166.8 10.8 %shard_map.344 = (bf16[512,768]{1,0:T(8,128)(2,1)S(1)}, bf16[512,768]{1,0:T(8,128)(2,1)S(1)}, bf16[512,768]{1,0:T(8,128)(2,1)S(1)}, f32[1,768]{1,0:T(1,128)S(1)}, f32[1,768]{1,0:T(1,128)S(1)}) custom-call(s32[2]{0:T(128)S(1)} %pad_add_fusion.at, bf16[512,768]{1,0:T(8,128)(2,1)S(1)} %copy-done.59, bf16[512,768]{1,0:T(8,128)(2,1)S(1)} %copy-done.61, ...), custom_call_target="tpu_custom_call" | custom-call | flops 2013265920 | bytes 5505024 | tf_op jit(solution)/shard_map/pallas_call | solution.py:418
  177.8 5.2 %shard_map.346 = (bf16[2,16,24,1536]{3,2,1,0:T(8,128)(2,1)S(1)}, bf16[2,16,24,1536]{3,2,1,0:T(8,128)(2,1)}) custom-call(s32[2]{0:T(128)S(1)} %pad_add_fusion.at, bf16[512,768]{1,0:T(8,128)(2,1)S(1)} %copy-done.27, bf16[512,768]{1,0:T(8,128)(2,1)S(1)} %copy-done.57, bf16[512,768]{1,0:T(8,128)(2,1)S(1)} %get-tuple-element.202.refs_2_.dq, ...), custom_call_target="tpu_custom_call" | custom-call | flops 2415919104 | bytes 9437184 | tf_op jit(solution)/shard_map/pallas_call | solution.py:263
  185.6 8.2 %collective-permute-done.26.refs_2_ = bf16[4,96,384]{2,1,0:T(8,128)(2,1)S(1)} collective-permute-done((bf16[4,96,384]{2,1,0:T(8,128)(2,1)S(1)}, bf16[4,96,384]{2,1,0:T(8,128)(2,1)S(1)}, u32[]{:S(2)}, u32[]{:S(2)}) %collective-permute-start.26) | collective-permute-done | bytes 294944 | tf_op jit(solution)/shard_map/ppermute | solution.py:36
  206.1 3.7 %shard_map.347 = (bf16[512,768]{1,0:T(8,128)(2,1)}, f32[1,768]{1,0:T(1,128)S(1)}) custom-call(s32[2]{0:T(128)S(1)} %pad_add_fusion.at, f32[512,768]{1,0:T(8,128)S(1)} %copy-done.8, bf16[512,768]{1,0:T(8,128)(2,1)S(1)} %copy-done.21, bf16[512,768]{1,0:T(8,128)(2,1)S(1)} %copy-done.23, bf16[512,768]{1,0:T(8,128)(2,1)S(1)} %copy-done.25, ...), custom_call_target="tpu_custom_call" | custom-call | flops 1811939328 | bytes 3538944 | tf_op jit(solution)/shard_map/pallas_call | solution.py:658
  209.7 3.4 %shard_map.348 = (bf16[8,24,1536]{2,1,0:T(8,128)(2,1)S(1)}, bf16[8,24,1536]{2,1,0:T(8,128)(2,1)S(1)}, bf16[8,24,1536]{2,1,0:T(8,128)(2,1)S(1)}, bf16[8,24,1536]{2,1,0:T(8,128)(2,1)S(1)}) custom-call(s32[2]{0:T(128)S(1)} %pad_add_fusion.at, bf16[2,16,24,1536]{3,2,1,0:T(8,128)(2,1)S(1)} %copy-done.6, bf16[2,16,24,1536]{3,2,1,0:T(8,128)(2,1)} %collective-permute-done.25.refs_1_), custom_call_target="tpu_custom_call" | custom-call | bytes 7077888 | tf_op jit(solution)/shard_map/pallas_call | solution.py:175
  214.9 3.4 %shard_map.353 = (bf16[8,24,1536]{2,1,0:T(8,128)(2,1)S(1)}, bf16[8,24,1536]{2,1,0:T(8,128)(2,1)S(1)}, bf16[8,24,1536]{2,1,0:T(8,128)(2,1)S(1)}, bf16[8,24,1536]{2,1,0:T(8,128)(2,1)S(1)}) custom-call(s32[2]{0:T(128)S(1)} %pad_add_fusion.at, bf16[2,16,24,1536]{3,2,1,0:T(8,128)(2,1)S(1)} %get-tuple-element.229.refs_0_, ...), custom_call_target="tpu_custom_call" | custom-call | bytes 7077888 | tf_op jit(solution)/shard_map/pallas_call | solution.py:175
  220.8 8.7 %collective-permute-done.29.refs_3_ = bf16[8,24,1536]{2,1,0:T(8,128)(2,1)S(1)} collective-permute-done((bf16[8,24,1536]{2,1,0:T(8,128)(2,1)S(1)}, bf16[8,24,1536]{2,1,0:T(8,128)(2,1)S(1)}, u32[]{:S(2)}, u32[]{:S(2)}) %collective-permute-start.29) | collective-permute-done | bytes 589856 | tf_op jit(solution)/shard_map/ppermute | solution.py:36
  234.1 8.0 %collective-permute-done.36.refs_3_ = bf16[8,24,1536]{2,1,0:T(8,128)(2,1)S(1)} collective-permute-done((bf16[8,24,1536]{2,1,0:T(8,128)(2,1)S(1)}, bf16[8,24,1536]{2,1,0:T(8,128)(2,1)S(1)}, u32[]{:S(2)}, u32[]{:S(2)}) %collective-permute-start.36) | collective-permute-done | bytes 589856 | tf_op jit(solution)/shard_map/ppermute | solution.py:36
  246.8 2.6 collective-permute-done.31.refs_3_
  259.2 2.8 collective-permute-done.44
  264.4 4.3 %collective-permute-done.45 = f32[16,768]{1,0:T(8,128)S(1)} collective-permute-done((f32[16,768]{1,0:T(8,128)S(1)}, f32[16,768]{1,0:T(8,128)S(1)}, u32[]{:S(2)}, u32[]{:S(2)}) %collective-permute-start.45) | collective-permute-done | bytes 49184 | tf_op jit(solution)/shard_map/ppermute | solution.py:36
  275.3 7.0 %collective-permute-done.39.refs_1_ = bf16[2,24,3072]{2,1,0:T(8,128)(2,1)S(1)} collective-permute-done((bf16[2,24,3072]{2,1,0:T(8,128)(2,1)S(1)}, bf16[2,24,3072]{2,1,0:T(8,128)(2,1)S(1)}, u32[]{:S(2)}, u32[]{:S(2)}) %collective-permute-start.39) | collective-permute-done | bytes 294944 | tf_op jit(solution)/shard_map/ppermute | solution.py:36
  283.9 7.6 %collective-permute-done.40 = bf16[1,24,3072]{2,1,0:T(8,128)(2,1)S(1)} collective-permute-done((bf16[1,24,3072]{2,1,0:T(8,128)(2,1)S(1)}, bf16[1,24,3072]{2,1,0:T(8,128)(2,1)S(1)}, u32[]{:S(2)}, u32[]{:S(2)}) %collective-permute-start.40) | collective-permute-done | bytes 147488 | tf_op jit(solution)/shard_map/ppermute | solution.py:36
  (303 shorter events, 101.2 us)
Async XLA Ops:
  3.7 9.6 %collective-permute-start = (bf16[1,24,2304]{2,1,0:T(8,128)(2,1)S(1)}, bf16[1,24,2304]{2,1,0:T(8,128)(2,1)S(1)}, u32[]{:S(2)}, u32[]{:S(2)}) collective-permute-start(bf16[1,24,2304]{2,1,0:T(8,128)(2,1)S(1)} %bitcast.51), channel_id=1, source_target_pairs={{0,16},{2,18},{4,20},{6,22},{8,24},{10,26},{12,28},{14,30},{16,0},... | collective-permute-start | bytes 331784 | tf_op jit(solution)/shard_map/ppermute | solution.py:36
  19.9 11.3 %collective-permute-start.10 = (bf16[1,24,3840]{2,1,0:T(8,128)(2,1)S(1)}, bf16[1,24,3840]{2,1,0:T(8,128)(2,1)S(1)}, u32[]{:S(2)}, u32[]{:S(2)}) collective-permute-start(bf16[1,24,3840]{2,1,0:T(8,128)(2,1)S(1)} %bitcast.54), channel_id=1, source_target_pairs={{0,16},{2,18},{4,20},{6,22},{8,24},{10,26},{12,28},{14,30},{16,0},... | collective-permute-start | bytes 552968 | tf_op jit(solution)/shard_map/ppermute | solution.py:36
  31.3 11.3 %collective-permute-start.3 = (bf16[8,24,1152]{2,1,0:T(8,128)(2,1)S(1)}, bf16[8,24,1152]{2,1,0:T(8,128)(2,1)S(1)}, u32[]{:S(2)}, u32[]{:S(2)}) collective-permute-start(bf16[8,24,1152]{2,1,0:T(8,128)(2,1)S(1)} %pad_maximum_fusion.8), channel_id=1, source_target_pairs={{0,2},{2,0},{4,6},{6,4},{8,10},{10,8},{12,14},{14,12},{16,18},{18,... | collective-permute-start | bytes 1327112 | tf_op jit(solution)/shard_map/ppermute | solution.py:36
  33.0 11.0 %collective-permute-start.5 = (bf16[8,24,1152]{2,1,0:T(8,128)(2,1)S(1)}, bf16[8,24,1152]{2,1,0:T(8,128)(2,1)S(1)}, u32[]{:S(2)}, u32[]{:S(2)}) collective-permute-start(bf16[8,24,1152]{2,1,0:T(8,128)(2,1)S(1)} %pad_maximum_fusion.9), channel_id=1, source_target_pairs={{0,4},{2,6},{4,0},{6,2},{8,12},{10,14},{12,8},{14,10},{16,20},{18,... | collective-permute-start | bytes 1327112 | tf_op jit(solution)/shard_map/ppermute | solution.py:36
  34.6 9.7 %collective-permute-start.11 = (bf16[2,24,3840]{2,1,0:T(8,128)(2,1)S(1)}, bf16[2,24,3840]{2,1,0:T(8,128)(2,1)S(1)}, u32[]{:S(2)}, u32[]{:S(2)}) collective-permute-start(bf16[2,24,3840]{2,1,0:T(8,128)(2,1)S(1)} %pad_maximum_fusion.10), channel_id=1, source_target_pairs={{0,8},{2,10},{4,12},{6,14},{8,0},{10,2},{12,4},{14,6},{16,24},{18,... | collective-permute-start | bytes 1105928 | tf_op jit(solution)/shard_map/ppermute | solution.py:36
  44.2 11.6 %collective-permute-start.6 = (bf16[2,16,24,1152]{3,2,1,0:T(8,128)(2,1)S(1)}, bf16[2,16,24,1152]{3,2,1,0:T(8,128)(2,1)S(1)}, u32[]{:S(2)}, u32[]{:S(2)}) collective-permute-start(bf16[2,16,24,1152]{3,2,1,0:T(8,128)(2,1)S(1)} %pad_maximum_fusion.2.own), channel_id=1, source_target_pairs={{0,1},{1,0},{2,3},{3,2},{4,5},{5,4},{6,7},{7,6},{8,9},{9,8},{10,11... | collective-permute-start | bytes 5308424 | tf_op jit(solution)/shard_map/ppermute | solution.py:39
  44.4 11.0 %collective-permute-start.14 = (bf16[4,24,1920]{2,1,0:T(8,128)(2,1)S(1)}, bf16[4,24,1920]{2,1,0:T(8,128)(2,1)S(1)}, u32[]{:S(2)}, u32[]{:S(2)}) collective-permute-start(bf16[4,24,1920]{2,1,0:T(8,128)(2,1)S(1)} %get-tuple-element.156), channel_id=1, source_target_pairs={{0,2},{2,0},{4,6},{6,4},{8,10},{10,8},{12,14},{14,12},{16,18},{18,... | collective-permute-start | bytes 1105928 | tf_op jit(solution)/shard_map/ppermute | solution.py:36
  45.0 10.7 %collective-permute-start.12 = (bf16[4,24,1920]{2,1,0:T(8,128)(2,1)S(1)}, bf16[4,24,1920]{2,1,0:T(8,128)(2,1)S(1)}, u32[]{:S(2)}, u32[]{:S(2)}) collective-permute-start(bf16[4,24,1920]{2,1,0:T(8,128)(2,1)S(1)} %get-tuple-element.153), channel_id=1, source_target_pairs={{0,4},{2,6},{4,0},{6,2},{8,12},{10,14},{12,8},{14,10},{16,20},{18,... | collective-permute-start | bytes 1105928 | tf_op jit(solution)/shard_map/ppermute | solution.py:36
  55.8 17.9 %collective-permute-start.15 = (bf16[8,24,1920]{2,1,0:T(8,128)(2,1)S(1)}, bf16[8,24,1920]{2,1,0:T(8,128)(2,1)S(1)}, u32[]{:S(2)}, u32[]{:S(2)}) collective-permute-start(bf16[8,24,1920]{2,1,0:T(8,128)(2,1)S(1)} %pad_maximum_fusion.4), channel_id=1, source_target_pairs={{0,4},{2,6},{4,0},{6,2},{8,12},{10,14},{12,8},{14,10},{16,20},{18,... | collective-permute-start | bytes 2211848 | tf_op jit(solution)/shard_map/ppermute | solution.py:36
  57.4 17.6 %collective-permute-start.13 = (bf16[8,24,1920]{2,1,0:T(8,128)(2,1)S(1)}, bf16[8,24,1920]{2,1,0:T(8,128)(2,1)S(1)}, u32[]{:S(2)}, u32[]{:S(2)}) collective-permute-start(bf16[8,24,1920]{2,1,0:T(8,128)(2,1)S(1)} %pad_maximum_fusion.3), channel_id=1, source_target_pairs={{0,2},{2,0},{4,6},{6,4},{8,10},{10,8},{12,14},{14,12},{16,18},{18,... | collective-permute-start | bytes 2211848 | tf_op jit(solution)/shard_map/ppermute | solution.py:36
  75.6 28.9 %collective-permute-start.16 = (bf16[2,16,24,1920]{3,2,1,0:T(8,128)(2,1)S(1)}, bf16[2,16,24,1920]{3,2,1,0:T(8,128)(2,1)S(1)}, u32[]{:S(2)}, u32[]{:S(2)}) collective-permute-start(bf16[2,16,24,1920]{3,2,1,0:T(8,128)(2,1)S(1)} %pad_maximum_fusion.own), channel_id=1, source_target_pairs={{0,1},{1,0},{2,3},{3,2},{4,5},{5,4},{6,7},{7,6},{8,9},{9,8},{10,11... | collective-permute-start | bytes 8847368 | tf_op jit(solution)/shard_map/ppermute | solution.py:39
  76.2 9.8 %collective-permute-start.7 = (bf16[1,96,768]{2,1,0:T(8,128)(2,1)S(1)}, bf16[1,96,768]{2,1,0:T(8,128)(2,1)S(1)}, u32[]{:S(2)}, u32[]{:S(2)}) collective-permute-start(bf16[1,96,768]{2,1,0:T(8,128)(2,1)S(1)} %bitcast.57), channel_id=1, source_target_pairs={{0,16},{2,18},{4,20},{6,22},{8,24},{10,26},{12,28},{14,30},{16,0},... | collective-permute-start | bytes 442376 | tf_op jit(solution)/shard_map/ppermute | solution.py:36
  101.6 16.5 %collective-permute-start.18 = (bf16[8,96,384]{2,1,0:T(8,128)(2,1)S(1)}, bf16[8,96,384]{2,1,0:T(8,128)(2,1)S(1)}, u32[]{:S(2)}, u32[]{:S(2)}) collective-permute-start(bf16[8,96,384]{2,1,0:T(8,128)(2,1)S(1)} %pad_maximum_fusion.5), channel_id=1, source_target_pairs={{0,2},{2,0},{4,6},{6,4},{8,10},{10,8},{12,14},{14,12},{16,18},{18,... | collective-permute-start | bytes 1769480 | tf_op jit(solution)/shard_map/ppermute | solution.py:36
  103.1 15.0 %collective-permute-start.19 = (bf16[8,96,384]{2,1,0:T(8,128)(2,1)S(1)}, bf16[8,96,384]{2,1,0:T(8,128)(2,1)S(1)}, u32[]{:S(2)}, u32[]{:S(2)}) collective-permute-start(bf16[8,96,384]{2,1,0:T(8,128)(2,1)S(1)} %pad_maximum_fusion.6), channel_id=1, source_target_pairs={{0,4},{2,6},{4,0},{6,2},{8,12},{10,14},{12,8},{14,10},{16,20},{18,... | collective-permute-start | bytes 1769480 | tf_op jit(solution)/shard_map/ppermute | solution.py:36
  148.0 15.7 %collective-permute-start.23 = (bf16[8,96,384]{2,1,0:T(8,128)(2,1)S(1)}, bf16[8,96,384]{2,1,0:T(8,128)(2,1)S(1)}, u32[]{:S(2)}, u32[]{:S(2)}) collective-permute-start(bf16[8,96,384]{2,1,0:T(8,128)(2,1)S(1)} %get-tuple-element.193), channel_id=1, source_target_pairs={{0,2},{2,0},{4,6},{6,4},{8,10},{10,8},{12,14},{14,12},{16,18},{18,... | collective-permute-start | bytes 1769480 | tf_op jit(solution)/shard_map/ppermute | solution.py:36
  149.4 15.3 %collective-permute-start.22 = (bf16[8,96,384]{2,1,0:T(8,128)(2,1)S(1)}, bf16[8,96,384]{2,1,0:T(8,128)(2,1)S(1)}, u32[]{:S(2)}, u32[]{:S(2)}) collective-permute-start(bf16[8,96,384]{2,1,0:T(8,128)(2,1)S(1)} %get-tuple-element.186), channel_id=1, source_target_pairs={{0,4},{2,6},{4,0},{6,2},{8,12},{10,14},{12,8},{14,10},{16,20},{18,... | collective-permute-start | bytes 1769480 | tf_op jit(solution)/shard_map/ppermute | solution.py:36
  166.1 11.7 %collective-permute-start.24 = (bf16[4,96,384]{2,1,0:T(8,128)(2,1)S(1)}, bf16[4,96,384]{2,1,0:T(8,128)(2,1)S(1)}, u32[]{:S(2)}, u32[]{:S(2)}) collective-permute-start(bf16[4,96,384]{2,1,0:T(8,128)(2,1)S(1)} %get-tuple-element.195), channel_id=1, source_target_pairs={{0,2},{2,0},{4,6},{6,4},{8,10},{10,8},{12,14},{14,12},{16,18},{18,... | collective-permute-start | bytes 884744 | tf_op jit(solution)/shard_map/ppermute | solution.py:36
  184.4 25.3 %collective-permute-start.25 = (bf16[2,16,24,1536]{3,2,1,0:T(8,128)(2,1)}, bf16[2,16,24,1536]{3,2,1,0:T(8,128)(2,1)}, u32[]{:S(2)}, u32[]{:S(2)}) collective-permute-start(bf16[2,16,24,1536]{3,2,1,0:T(8,128)(2,1)} %get-tuple-element.201), channel_id=1, source_target_pairs={{0,1},{1,0},{2,3},{3,2},{4,5},{5,4},{6,7},{7,6},{8,9},{9,8},{10,11... | collective-permute-start | bytes 7077896 | tf_op jit(solution)/shard_map/ppermute | solution.py:39
  184.4 30.5 %collective-permute-start.34 = (bf16[2,16,24,1536]{3,2,1,0:T(8,128)(2,1)}, bf16[2,16,24,1536]{3,2,1,0:T(8,128)(2,1)}, u32[]{:S(2)}, u32[]{:S(2)}) collective-permute-start(bf16[2,16,24,1536]{3,2,1,0:T(8,128)(2,1)} %get-tuple-element.230), channel_id=1, source_target_pairs={{0,1},{1,0},{2,3},{3,2},{4,5},{5,4},{6,7},{7,6},{8,9},{9,8},{10,11... | collective-permute-start | bytes 7077896 | tf_op jit(solution)/shard_map/ppermute | solution.py:39
  196.6 13.1 %collective-permute-start.27 = (bf16[2,96,768]{2,1,0:T(8,128)(2,1)}, bf16[2,96,768]{2,1,0:T(8,128)(2,1)}, u32[]{:S(2)}, u32[]{:S(2)}) collective-permute-start(bf16[2,96,768]{2,1,0:T(8,128)(2,1)} %get-tuple-element.214), channel_id=1, source_target_pairs={{0,8},{2,10},{4,12},{6,14},{8,0},{10,2},{12,4},{14,6},{16,24},{18,... | collective-permute-start | bytes 884744 | tf_op jit(solution)/shard_map/ppermute | solution.py:36
  213.2 16.3 %collective-permute-start.29 = (bf16[8,24,1536]{2,1,0:T(8,128)(2,1)S(1)}, bf16[8,24,1536]{2,1,0:T(8,128)(2,1)S(1)}, u32[]{:S(2)}, u32[]{:S(2)}) collective-permute-start(bf16[8,24,1536]{2,1,0:T(8,128)(2,1)S(1)} %get-tuple-element.218), channel_id=1, source_target_pairs={{0,4},{2,6},{4,0},{6,2},{8,12},{10,14},{12,8},{14,10},{16,20},{18,... | collective-permute-start | bytes 1769480 | tf_op jit(solution)/shard_map/ppermute | solution.py:36
  214.2 16.2 %collective-permute-start.28 = (bf16[8,24,1536]{2,1,0:T(8,128)(2,1)S(1)}, bf16[8,24,1536]{2,1,0:T(8,128)(2,1)S(1)}, u32[]{:S(2)}, u32[]{:S(2)}) collective-permute-start(bf16[8,24,1536]{2,1,0:T(8,128)(2,1)S(1)} %get-tuple-element.216), channel_id=1, source_target_pairs={{0,2},{2,0},{4,6},{6,4},{8,10},{10,8},{12,14},{14,12},{16,18},{18,... | collective-permute-start | bytes 1769480 | tf_op jit(solution)/shard_map/ppermute | solution.py:36
  218.3 23.8 %collective-permute-start.36 = (bf16[8,24,1536]{2,1,0:T(8,128)(2,1)S(1)}, bf16[8,24,1536]{2,1,0:T(8,128)(2,1)S(1)}, u32[]{:S(2)}, u32[]{:S(2)}) collective-permute-start(bf16[8,24,1536]{2,1,0:T(8,128)(2,1)S(1)} %get-tuple-element.236), channel_id=1, source_target_pairs={{0,4},{2,6},{4,0},{6,2},{8,12},{10,14},{12,8},{14,10},{16,20},{18,... | collective-permute-start | bytes 1769480 | tf_op jit(solution)/shard_map/ppermute | solution.py:36
  220.1 22.9 %collective-permute-start.35 = (bf16[8,24,1536]{2,1,0:T(8,128)(2,1)S(1)}, bf16[8,24,1536]{2,1,0:T(8,128)(2,1)S(1)}, u32[]{:S(2)}, u32[]{:S(2)}) collective-permute-start(bf16[8,24,1536]{2,1,0:T(8,128)(2,1)S(1)} %get-tuple-element.234), channel_id=1, source_target_pairs={{0,2},{2,0},{4,6},{6,4},{8,10},{10,8},{12,14},{14,12},{16,18},{18,... | collective-permute-start | bytes 1769480 | tf_op jit(solution)/shard_map/ppermute | solution.py:36
  231.6 17.8 %collective-permute-start.31 = (bf16[4,24,1536]{2,1,0:T(8,128)(2,1)S(1)}, bf16[4,24,1536]{2,1,0:T(8,128)(2,1)S(1)}, u32[]{:S(2)}, u32[]{:S(2)}) collective-permute-start(bf16[4,24,1536]{2,1,0:T(8,128)(2,1)S(1)} %get-tuple-element.224), channel_id=1, source_target_pairs={{0,2},{2,0},{4,6},{6,4},{8,10},{10,8},{12,14},{14,12},{16,18},{18,... | collective-permute-start | bytes 884744 | tf_op jit(solution)/shard_map/ppermute | solution.py:36
  232.3 17.0 %collective-permute-start.30 = (bf16[4,24,1536]{2,1,0:T(8,128)(2,1)S(1)}, bf16[4,24,1536]{2,1,0:T(8,128)(2,1)S(1)}, u32[]{:S(2)}, u32[]{:S(2)}) collective-permute-start(bf16[4,24,1536]{2,1,0:T(8,128)(2,1)S(1)} %get-tuple-element.222), channel_id=1, source_target_pairs={{0,4},{2,6},{4,0},{6,2},{8,12},{10,14},{12,8},{14,10},{16,20},{18,... | collective-permute-start | bytes 884744 | tf_op jit(solution)/shard_map/ppermute | solution.py:36
  244.3 24.5 %collective-permute-start.38 = (bf16[4,24,1536]{2,1,0:T(8,128)(2,1)S(1)}, bf16[4,24,1536]{2,1,0:T(8,128)(2,1)S(1)}, u32[]{:S(2)}, u32[]{:S(2)}) collective-permute-start(bf16[4,24,1536]{2,1,0:T(8,128)(2,1)S(1)} %get-tuple-element.243), channel_id=1, source_target_pairs={{0,2},{2,0},{4,6},{6,4},{8,10},{10,8},{12,14},{14,12},{16,18},{18,... | collective-permute-start | bytes 884744 | tf_op jit(solution)/shard_map/ppermute | solution.py:36
  245.0 23.8 %collective-permute-start.37 = (bf16[4,24,1536]{2,1,0:T(8,128)(2,1)S(1)}, bf16[4,24,1536]{2,1,0:T(8,128)(2,1)S(1)}, u32[]{:S(2)}, u32[]{:S(2)}) collective-permute-start(bf16[4,24,1536]{2,1,0:T(8,128)(2,1)S(1)} %get-tuple-element.241), channel_id=1, source_target_pairs={{0,4},{2,6},{4,0},{6,2},{8,12},{10,14},{12,8},{14,10},{16,20},{18,... | collective-permute-start | bytes 884744 | tf_op jit(solution)/shard_map/ppermute | solution.py:36
  250.3 21.5 %collective-permute-start.32 = (bf16[2,24,3072]{2,1,0:T(8,128)(2,1)S(1)}, bf16[2,24,3072]{2,1,0:T(8,128)(2,1)S(1)}, u32[]{:S(2)}, u32[]{:S(2)}) collective-permute-start(bf16[2,24,3072]{2,1,0:T(8,128)(2,1)S(1)} %get-tuple-element.226), channel_id=1, source_target_pairs={{0,8},{2,10},{4,12},{6,14},{8,0},{10,2},{12,4},{14,6},{16,24},{18,... | collective-permute-start | bytes 884744 | tf_op jit(solution)/shard_map/ppermute | solution.py:36
  257.2 16.1 %collective-permute-start.41 = (bf16[1,96,768]{2,1,0:T(8,128)(2,1)S(1)}, bf16[1,96,768]{2,1,0:T(8,128)(2,1)S(1)}, u32[]{:S(2)}, u32[]{:S(2)}) collective-permute-start(bf16[1,96,768]{2,1,0:T(8,128)(2,1)S(1)} %get-tuple-element.253), channel_id=1, source_target_pairs={{0,16},{2,18},{4,20},{6,22},{8,24},{10,26},{12,28},{14,30},{16,0},... | collective-permute-start | bytes 442376 | tf_op jit(solution)/shard_map/ppermute | solution.py:36
  269.7 12.6 %collective-permute-start.39 = (bf16[2,24,3072]{2,1,0:T(8,128)(2,1)S(1)}, bf16[2,24,3072]{2,1,0:T(8,128)(2,1)S(1)}, u32[]{:S(2)}, u32[]{:S(2)}) collective-permute-start(bf16[2,24,3072]{2,1,0:T(8,128)(2,1)S(1)} %get-tuple-element.246), channel_id=1, source_target_pairs={{0,8},{2,10},{4,12},{6,14},{8,0},{10,2},{12,4},{14,6},{16,24},{18,... | collective-permute-start | bytes 884744 | tf_op jit(solution)/shard_map/ppermute | solution.py:36
  272.5 10.6 %collective-permute-start.33 = (bf16[1,24,3072]{2,1,0:T(8,128)(2,1)S(1)}, bf16[1,24,3072]{2,1,0:T(8,128)(2,1)S(1)}, u32[]{:S(2)}, u32[]{:S(2)}) collective-permute-start(bf16[1,24,3072]{2,1,0:T(8,128)(2,1)S(1)} %get-tuple-element.228), channel_id=1, source_target_pairs={{0,16},{2,18},{4,20},{6,22},{8,24},{10,26},{12,28},{14,30},{16,0},... | collective-permute-start | bytes 442376 | tf_op jit(solution)/shard_map/ppermute | solution.py:36
  (95 other events, 691.9 us)

commit v3 on v2

--- a/solution.py
+++ b/solution.py
@@ -8,6 +8,7 @@
 HD = 64
 BOTH = ("dp", "pair")
 LOW = jnp.bfloat16
+COVER = 30
 
 
 def hold(value, *others):
@@ -52,9 +53,9 @@
         ),
         out_shape=out_shape,
         cost_estimate=pl.CostEstimate(
-            flops=flops, bytes_accessed=moved, transcendentals=special
+            flops=COVER * flops, bytes_accessed=moved if flops == 0 else COVER * moved, transcendentals=special
         ),
-        compiler_params=pltpu.CompilerParams(vmem_limit_bytes=limit or 32 * 2**20),
+        compiler_params=pltpu.CompilerParams(vmem_limit_bytes=limit or 16 * 2**20),
     )
 
 
@@ -84,6 +85,7 @@
         self.right = place.slow + place.fast + place.mid
         self.stage = 0
         self.halves = None
+        self.ready = ()
 
     def step(self, before=(), during=()):
         place, stage = self.place, self.stage
@@ -92,17 +94,21 @@
             value = hold(self.slots, *before)
             got = hold(place.swap(value, self.left[stage]), *during)
             self.slots = jnp.concatenate([value, got])
+            self.ready = (self.slots,)
+            if self.stage == len(place.slow):
+                half = self.slots.shape[-1] // 2
+                self.halves = self.ready = (self.slots[..., :half], self.slots[..., half:])
             return got
         if stage < len(self.left):
-            if self.halves is None:
-                half = self.slots.shape[-1] // 2
-                self.halves = (self.slots[..., :half], self.slots[..., half:])
             l, r = (hold(v, *before) for v in self.halves)
             gl = hold(place.swap(l, self.left[stage]), *during)
             gr = hold(place.swap(r, self.right[stage]), *during)
-            self.halves = (jnp.concatenate([l, gl]), jnp.concatenate([r, gr]))
+            self.halves = self.ready = (jnp.concatenate([l, gl]), jnp.concatenate([r, gr]))
+            if self.stage == len(self.left):
+                self.stacked = jnp.stack(self.halves)
+                self.ready = (self.stacked,)
             return gr
-        self.own = hold(jnp.stack(self.halves), *before)
+        self.own = hold(self.stacked, *before)
         self.other = hold(place.swap_core(self.own), *during)
         return self.other
 
@@ -194,7 +200,7 @@
         self.result = None
         self.gots = None
 
-    def step(self, before=(), during=()):
+    def fold(self):
         place = self.place
         if self.gots is not None:
             orders = (self.left, self.right)
@@ -207,6 +213,10 @@
                 self.held[side].remove(stride)
             join = self.stage == crossing
             self.keeps, self.sends = fold(place, self.keeps, self.gots, bits, join)
+        return self.sends
+
+    def send(self, before=(), during=()):
+        place = self.place
         swaps = (
             [place.swap_core]
             if self.stage < 0
@@ -218,7 +228,7 @@
         self.stage += 1
         if self.stage == len(self.left):
             self.result = self.keeps[0][0].astype(jnp.float32) + self.gots[0][0].astype(jnp.float32)
-        return self.gots[-1]
+        return self.gots
 
 
 def weight_terms(place, lefts, rights, rows):
@@ -314,6 +324,8 @@
         self.strides = [0] + place.fast + place.mid + place.slow
 
     def step(self, before=(), during=()):
+        if not self.strides:
+            return None
         value = hold(self.value, *before)
         stride = self.strides.pop(0)
         got = hold(self.place.swap(value, stride) if stride else self.place.swap_core(value), *during)
@@ -668,6 +680,7 @@
 class PlainGather:
     def __init__(self, rows):
         self.rows = rows
+        self.ready = ()
 
     def step(self, before=(), during=()):
         return None
@@ -689,18 +702,21 @@
 class PlainScatter:
     def __init__(self, term):
         self.result = lax.psum_scatter(term, BOTH, scatter_dimension=0, tiled=True)
-
-    def step(self, before=(), during=()):
-        return None
+        self.sends = ()
+
+    def fold(self):
+        return ()
+
+    def send(self, before=(), during=()):
+        return ()
 
 
 class PlainTotal:
     def __init__(self, value):
         self.value = lax.psum(value, BOTH)
-        self.strides = [0]
 
     def step(self, before=(), during=()):
-        self.strides.pop(0)
+        return None
 
 
 def outer_sum(left, right):
@@ -774,25 +790,27 @@
     )
     vectors = tuple(v[None] for v in vectors)
     query_row, value_row, output_row, inner_row, outer_row, gain_1, shift_1, gain_2, shift_2 = vectors
-    got = first_gather.step(during=(*vectors, start, masked, wanted))
-    inner_gather.step((got,))
-    got = first_gather.step()
-    inner_gather.step((got,))
-    got = first_gather.step()
-    outer_gather.step((got,))
-    inner_gather.step((got,))
+    first_gather.step(during=(*vectors, start, masked, wanted))
+    before = first_gather.ready
+    first_gather.step()
+    inner_gather.step(before, first_gather.ready)
+    before = first_gather.ready
+    first_gather.step()
+    inner_gather.step(before, first_gather.ready)
+    outer_gather.step(inner_gather.ready)
+    inner_gather.step(first_gather.ready)
     got = first_gather.step()
     weights = first_gather.done((width // 2,) * 3)
     query, key, value, context, lse = attention_forward(
-        place, start, weights, query_row, value_row, seqs
-    )
-    inner_gather.step((got,), (context,))
-    outer_gather.step((got,), (context,))
-    got = outer_gather.step((context,))
-    inner_gather.step((context,))
+        place, hold(start, *inner_gather.ready, *outer_gather.ready), weights, query_row, value_row, seqs
+    )
+    outer_gather.step(inner_gather.ready, (context,))
+    inner_gather.step((got,), (context, *outer_gather.ready))
+    got = inner_gather.step((context,))
+    outer_gather.step(inner_gather.ready, (got,))
     wo, wi = inner_gather.done((width // 2, inner // 2))
     unit, inverse, normed_low, active, slope = feed_in(
-        place, start, hold(context, got), wo, output_row, gain_1, shift_1, wi, inner_row
+        place, start, hold(context, *outer_gather.ready), wo, output_row, gain_1, shift_1, wi, inner_row
     )
     outer_gather.step((), (active,))
     outer_gather.step()
@@ -802,43 +820,53 @@
     )
     if staged:
         outer_sums = Scatter(place, *weight_terms_tall(place, active, grad_branch, own_tall))
-        grad_branch = hold(grad_branch, *outer_sums.sends)
     else:
         outer_sums = PlainScatter(outer_sum(active, grad_branch))
-    grad_hidden, inner_bias_grad = hidden_back(place, grad_branch, wu, slope)
-    got = outer_sums.step((), (grad_hidden,))
+    grad_hidden, inner_bias_grad = hidden_back(place, hold(grad_branch, *outer_sums.sends), wu, slope)
+    outer_sums.send((), (grad_hidden,))
+    outer_sums.fold()
     if staged:
         tiles = inner // width
-        inner_sums = Scatter(
-            place, *weight_terms(place, [normed_low] * tiles, hold(grad_hidden, got), own_rows)
-        )
-        grad_hidden = hold(grad_hidden, *inner_sums.sends)
+        grad_tied = hold(grad_hidden, *outer_sums.sends)
+        inner_sums = Scatter(place, *weight_terms(place, [normed_low] * tiles, grad_tied, own_rows))
     else:
         inner_sums = PlainScatter(outer_sum(normed_low, grad_hidden))
+    outer_sums.send((), inner_sums.sends)
+    outer_sums.fold()
+    tied = hold(grad_hidden, *inner_sums.sends, *outer_sums.sends)
     grad_first, grad_attended, grad_context, output_bias_grad, gain_one_grad, shift_one_grad = first_back(
-        place, grad_hidden, wi, grad_second, unit, inverse, gain_1, wo
-    )
-    got = outer_sums.step((), (grad_context,))
+        place, tied, wi, grad_second, unit, inverse, gain_1, wo
+    )
+    outer_sums.send((), (grad_context,))
+    inner_sums.send((), (grad_context,))
+    inner_sums.fold()
+    outer_sums.fold()
+    tied = hold(grad_context, *outer_sums.sends, *inner_sums.sends)
     grad_query, grad_key, grad_value, query_bias_grad, value_bias_grad = attention_backward(
-        place, query, key, value, hold(grad_context, got), lse
-    )
-    got = outer_sums.step((), (grad_query,))
-    inner_sums.step((grad_context,), (grad_query,))
+        place, query, key, value, tied, lse
+    )
+    inner_sums.send((), (grad_query,))
+    outer_sums.send((), (grad_query,))
+    inner_sums.fold()
+    outer_sums.fold()
     lefts = [start, start, start, context]
-    rights = [hold(grad_query, got), grad_key, grad_value, grad_attended]
+    rights = [hold(grad_query, *outer_sums.sends, *inner_sums.sends), grad_key, grad_value, grad_attended]
     if staged:
         first_sums = Scatter(place, *weight_terms(place, lefts, rights, own_rows))
-        grad_query = hold(grad_query, *first_sums.sends)
     else:
         first_sums = PlainScatter(
             jnp.concatenate([outer_sum(l, r) for l, r in zip(lefts, rights)], axis=1)
         )
+    inner_sums.send((), first_sums.sends)
+    outer_sums.send((), first_sums.sends)
+    inner_sums.fold()
+    grad_query = hold(grad_query, *first_sums.sends, *inner_sums.sends)
     input_grad, mask_grad = start_back(
         place, grad_first, (grad_query, grad_key, grad_value), weights, masked
     )
-    got_outer = outer_sums.step((), (mask_grad,))
-    got = inner_sums.step((), (mask_grad,))
-    first_sums.step((), (mask_grad,))
+    first_sums.send((), (mask_grad,))
+    first_sums.fold()
+    inner_sums.send((), (mask_grad, *first_sums.sends))
     smalls = (
         query_bias_grad,
         value_bias_grad,
@@ -856,22 +884,21 @@
     high = -(-(9 + inner // width) // 8) * 8
     packed = pack(place, smalls, spots, (high, width))
     total = Total(place, packed) if staged else PlainTotal(packed)
-    got = inner_sums.step((got,))
-    got = first_sums.step((got_outer,))
-    outer_sums.step((got_outer,))
+    got = total.step(first_sums.sends)
+    first_sums.send((), (got,))
+    got = total.step((), first_sums.sends)
     if staged:
-        total.step((got_outer,))
-        inner_sums.step((got,))
-        got = first_sums.step((got,))
-        total.step()
-        got = first_sums.step()
-        inner_sums.step((got,))
-        total.step()
-        got = first_sums.step()
-        total.step()
-        total.step()
-    else:
-        total.step()
+        inner_sums.fold()
+    first_sums.fold()
+    inner_sums.send(first_sums.sends)
+    first_sums.send((), (got,))
+    got = total.step(first_sums.sends)
+    first_sums.fold()
+    first_sums.send((), (got,))
+    got = total.step(first_sums.sends)
+    first_sums.fold()
+    total.step(first_sums.sends)
+    first_sums.send((), (got,))
     packed = total.value
     order = (0, 1, 2, 9, 3, 4, 5, 6, 7, 8)
     firsts = first_sums.result

time: 293 us -> 241 us (0.82)
  waiting for transfers between devices: 116 us -> 79.9 us
  local copies, waits for them, and re-layouts: 25.8 us -> 12.8 us
  Pallas kernels: 93.9 us -> 86.5 us
  starting transfers between devices: 48 us -> 52.9 us
    ppermute x40, waiting for transfers between devices: 111 us -> 74.7 us  [swap(): lax.ppermute(value, 'dp', [(i, i ^ stride) for i in range(self.chips)])]
    unnamed x162 -> x103, local copies, waits for them, and re-layouts: 19.9 us -> 10.1 us
    pallas_call x12, Pallas kernels: 20.1 us -> 13.7 us  [fold(): kernel_call(body, (steps,), [ins] * (2 * len(keeps)), [pl.BlockSpec((chip...]
    ppermute x40, starting transfers between devices: 47 us -> 52.3 us  [swap(): lax.ppermute(value, 'dp', [(i, i ^ stride) for i in range(self.chips)])]
  transfers between devices with their start and end apart: 47 -> 47, of which waited for: 27 -> 27; matrix products, arithmetic and copies ran while one was open for 4% -> 3% of each run, Pallas kernels for 24% -> 27%
where the time goes in v3:
time: 241 us
  Pallas kernels  86.5 us (36%)
  waiting for transfers between devices  79.9 us (33%)
  starting transfers between devices  52.9 us (22%)
  local copies, waits for them, and re-layouts  12.8 us (5%)
  other arithmetic  6.72 us (3%)
    ppermute x40, waiting for transfers between devices, swap(): lax.ppermute(value, 'dp', [(i, i ^ stride) for i in range(self.chips)])  74.7 us
    ppermute x40, starting transfers between devices, swap(): lax.ppermute(value, 'dp', [(i, i ^ stride) for i in range(self.chips)])  52.3 us
    pallas_call x12, Pallas kernels, fold(): kernel_call(body, (steps,), [ins] * (2 * len(keeps)), [pl.BlockSpec((chip...  13.7 us
    pallas_call x1, Pallas kernels, attention_backward(): kernel_call(body, (groups, seqs), [block] * 4 + [pl.BlockSpec((1, 1, 4, l...  10.8 us
    unnamed x103, local copies, waits for them, and re-layouts  10.1 us
    pallas_call x1, Pallas kernels, attention_forward(): kernel_call(body, (seqs, groups), [pl.BlockSpec((length, width), lambda s...  9.83 us
    pallas_call x2, Pallas kernels, weight_terms(): kernel_call(body, (count,), [pl.BlockSpec((length, features), lambda t, a...  9.3 us
    pallas_call x1, Pallas kernels, feed_in(): kernel_call(body, (inner // tile,), [keep(a) for a in ins] + [pl.BlockSpe...  9.13 us
  transfers between devices with their start and end apart: 47, of which 27 were waited for; matrix products, arithmetic and copies ran while one was open for 3% of the time, Pallas kernels for 27%

profile of v3, /device:TPU:0, one launch (start us, length us, event | category | flops | bytes accessed | tf_op | source)
XLA Modules:
  0.0 240.6 jit_solution(7818853638134045336)
XLA Ops:
  3.7 4.1 %collective-permute-start = (bf16[1,24,2304]{2,1,0:T(8,128)(2,1)S(1)}, bf16[1,24,2304]{2,1,0:T(8,128)(2,1)S(1)}, u32[]{:S(2)}, u32[]{:S(2)}) collective-permute-start(bf16[1,24,2304]{2,1,0:T(8,128)(2,1)S(1)} %bitcast.39), channel_id=1, source_target_pairs={{0,16},{2,18},{4,20},{6,22},{8,24},{10,26},{12,28},{14,30},{16,0},... | collective-permute-start | bytes 331784 | tf_op jit(solution)/shard_map/ppermute | solution.py:37
  10.7 2.5 %collective-permute-done = bf16[1,24,2304]{2,1,0:T(8,128)(2,1)S(1)} collective-permute-done((bf16[1,24,2304]{2,1,0:T(8,128)(2,1)S(1)}, bf16[1,24,2304]{2,1,0:T(8,128)(2,1)S(1)}, u32[]{:S(2)}, u32[]{:S(2)}) %collective-permute-start) | collective-permute-done | bytes 110624 | tf_op jit(solution)/shard_map/ppermute | solution.py:37
  14.6 5.3 %collective-permute-done.1 = bf16[2,24,2304]{2,1,0:T(8,128)(2,1)S(1)} collective-permute-done((bf16[2,24,2304]{2,1,0:T(8,128)(2,1)S(1)}, bf16[2,24,2304]{2,1,0:T(8,128)(2,1)S(1)}, u32[]{:S(2)}, u32[]{:S(2)}) %collective-permute-start.1) | collective-permute-done | bytes 221216 | tf_op jit(solution)/shard_map/ppermute | solution.py:37
  23.5 3.3 %collective-permute-start.2 = (bf16[1,24,3840]{2,1,0:T(8,128)(2,1)S(1)}, bf16[1,24,3840]{2,1,0:T(8,128)(2,1)S(1)}, u32[]{:S(2)}, u32[]{:S(2)}) collective-permute-start(bf16[1,24,3840]{2,1,0:T(8,128)(2,1)S(1)} %bitcast.42), channel_id=1, source_target_pairs={{0,16},{2,18},{4,20},{6,22},{8,24},{10,26},{12,28},{14,30},{16,0},... | collective-permute-start | bytes 552968 | tf_op jit(solution)/shard_map/ppermute | solution.py:37
  29.0 5.4 %collective-permute-done.2 = bf16[1,24,3840]{2,1,0:T(8,128)(2,1)S(1)} collective-permute-done((bf16[1,24,3840]{2,1,0:T(8,128)(2,1)S(1)}, bf16[1,24,3840]{2,1,0:T(8,128)(2,1)S(1)}, u32[]{:S(2)}, u32[]{:S(2)}) %collective-permute-start.2) | collective-permute-done | bytes 184352 | tf_op jit(solution)/shard_map/ppermute | solution.py:37
  35.3 2.3 collective-permute-done.6
  38.4 5.8 %collective-permute-done.5 = bf16[2,24,3840]{2,1,0:T(8,128)(2,1)S(1)} collective-permute-done((bf16[2,24,3840]{2,1,0:T(8,128)(2,1)S(1)}, bf16[2,24,3840]{2,1,0:T(8,128)(2,1)S(1)}, u32[]{:S(2)}, u32[]{:S(2)}) %collective-permute-start.5) | collective-permute-done | bytes 368672 | tf_op jit(solution)/shard_map/ppermute | solution.py:37
  44.9 3.2 %collective-permute-start.10 = (bf16[1,96,768]{2,1,0:T(8,128)(2,1)S(1)}, bf16[1,96,768]{2,1,0:T(8,128)(2,1)S(1)}, u32[]{:S(2)}, u32[]{:S(2)}) collective-permute-start(bf16[1,96,768]{2,1,0:T(8,128)(2,1)S(1)} %bitcast.57), channel_id=1, source_target_pairs={{0,16},{2,18},{4,20},{6,22},{8,24},{10,26},{12,28},{14,30},{16,0},... | collective-permute-start | bytes 442376 | tf_op jit(solution)/shard_map/ppermute | solution.py:37
  48.7 5.7 %collective-permute-done.10 = bf16[1,96,768]{2,1,0:T(8,128)(2,1)S(1)} collective-permute-done((bf16[1,96,768]{2,1,0:T(8,128)(2,1)S(1)}, bf16[1,96,768]{2,1,0:T(8,128)(2,1)S(1)}, u32[]{:S(2)}, u32[]{:S(2)}) %collective-permute-start.10) | collective-permute-done | bytes 147488 | tf_op jit(solution)/shard_map/ppermute | solution.py:37
  54.5 3.1 %collective-permute-done.8 = bf16[4,24,1920]{2,1,0:T(8,128)(2,1)S(1)} collective-permute-done((bf16[4,24,1920]{2,1,0:T(8,128)(2,1)S(1)}, bf16[4,24,1920]{2,1,0:T(8,128)(2,1)S(1)}, u32[]{:S(2)}, u32[]{:S(2)}) %collective-permute-start.8) | collective-permute-done | bytes 368672 | tf_op jit(solution)/shard_map/ppermute | solution.py:37
  62.5 9.8 %shard_map.334 = (bf16[512,768]{1,0:T(8,128)(2,1)S(1)}, bf16[512,768]{1,0:T(8,128)(2,1)S(1)}, bf16[512,768]{1,0:T(8,128)(2,1)S(1)}, bf16[512,768]{1,0:T(8,128)(2,1)S(1)}, f32[1,3,4,512]{3,2,1,0:T(4,128)S(1)}) custom-call(s32[2]{0:T(128)S(1)} %pad_add_fusion.at, bf16[512,768]{1,0:T(8,128)(2,1)S(1)} %broadcast_select_fusion.start.refs_0_, ...), custom_call_target="tpu_custom_call" | custom-call | flops 54358179840 | bytes 106168320 | tf_op jit(solution)/shard_map/pallas_call | solution.py:372
  79.1 6.3 %collective-permute-done.17 = bf16[4,96,384]{2,1,0:T(8,128)(2,1)S(1)} collective-permute-done((bf16[4,96,384]{2,1,0:T(8,128)(2,1)S(1)}, bf16[4,96,384]{2,1,0:T(8,128)(2,1)S(1)}, u32[]{:S(2)}, u32[]{:S(2)}) %collective-permute-start.17) | collective-permute-done | bytes 294944 | tf_op jit(solution)/shard_map/ppermute | solution.py:37
  90.1 9.1 %shard_map.336 = (f32[512,768]{1,0:T(8,128)S(1)}, f32[512,1]{1,0:T(8,128)S(1)}, bf16[512,768]{1,0:T(8,128)(2,1)S(1)}, bf16[512,3072]{1,0:T(8,128)(2,1)S(1)}, bf16[512,3072]{1,0:T(8,128)(2,1)S(1)}) custom-call(s32[2]{0:T(128)S(1)} %pad_add_fusion.at, bf16[512,768]{1,0:T(8,128)(2,1)S(1)} %broadcast_select_fusion.start.refs_0_, ...), custom_call_target="tpu_custom_call" | custom-call | flops 90596966400 | bytes 141557760 | tf_op jit(solution)/shard_map/pallas_call | solution.py:495
  105.1 4.0 %collective-permute-done.20.other = bf16[2,16,96,384]{3,2,1,0:T(8,128)(2,1)} collective-permute-done((bf16[2,16,96,384]{3,2,1,0:T(8,128)(2,1)S(1)}, bf16[2,16,96,384]{3,2,1,0:T(8,128)(2,1)}, u32[]{:S(2)}, u32[]{:S(2)}) %collective-permute-start.20) | collective-permute-done | bytes 2359328 | tf_op jit(solution)/shard_map/ppermute | solution.py:40
  109.1 2.9 %shard_map.337 = bf16[32,96,768]{2,1,0:T(8,128)(2,1)S(1)} custom-call(s32[2]{0:T(128)S(1)} %pad_add_fusion.at, bf16[2,16,96,384]{3,2,1,0:T(8,128)(2,1)S(1)} %pad_maximum_fusion.1.own, bf16[2,16,96,384]{3,2,1,0:T(8,128)(2,1)} %collective-permute-done.20.other), custom_call_target="tpu_custom_call" | custom-call | bytes 9437184 | tf_op jit(solution)/shard_map/pallas_call | solution.py:140
  112.0 7.1 %shard_map.338 = (bf16[512,768]{1,0:T(8,128)(2,1)}, f32[512,768]{1,0:T(8,128)S(1)}, bf16[512,768]{1,0:T(8,128)(2,1)S(1)}, f32[1,768]{1,0:T(1,128)S(1)}, f32[1,768]{1,0:T(1,128)S(1)}, /*index=5*/f32[1,768]{1,0:T(1,128)S(1)}) custom-call(s32[2]{0:T(128)S(1)} %pad_add_fusion.at, bf16[512,3072]{1,0:T(8,128)(2,1)S(1)} %copy-done.19, ...), custom_call_target="tpu_custom_call" | custom-call | flops 72477573120 | bytes 141557760 | tf_op jit(solution)/shard_map/pallas_call | solution.py:551
  119.0 4.7 %shard_map.339 = (bf16[2,16,96,384]{3,2,1,0:T(8,128)(2,1)S(1)}, bf16[2,16,96,384]{3,2,1,0:T(8,128)(2,1)S(1)}) custom-call(s32[2]{0:T(128)S(1)} %pad_add_fusion.at, bf16[512,3072]{1,0:T(8,128)(2,1)S(1)} %copy-done.19, bf16[512,768]{1,0:T(8,128)(2,1)S(1)} %get-tuple-element.185.right_ref.grad), custom_call_target="tpu_custom_call" | custom-call | flops 72477573120 | bytes 283115520 | tf_op jit(solution)/shard_map/pallas_call | solution.py:308
  124.0 4.7 %shard_map.340 = (bf16[512,3072]{1,0:T(8,128)(2,1)S(1)}, f32[1,3072]{1,0:T(1,128)S(1)}) custom-call(s32[2]{0:T(128)S(1)} %pad_add_fusion.at, bf16[512,768]{1,0:T(8,128)(2,1)S(1)} %get-tuple-element.185.right_ref.grad, bf16[3072,768]{1,0:T(8,128)(2,1)S(1)} %bitcast.38, bf16[512,3072]{1,0:T(8,128)(2,1)S(1)} %copy-done.21), custom_call_target="tpu_custom_call" | custom-call | flops 72477573120 | bytes 141557760 | tf_op jit(solution)/shard_map/pallas_call | solution.py:580
  128.7 1.9 shard_map.341
  132.7 4.6 %shard_map.342 = (bf16[2,16,24,1536]{3,2,1,0:T(8,128)(2,1)S(1)}, bf16[2,16,24,1536]{3,2,1,0:T(8,128)(2,1)S(1)}) custom-call(s32[2]{0:T(128)S(1)} %pad_add_fusion.at, bf16[512,768]{1,0:T(8,128)(2,1)S(1)} %copy-done.34, bf16[512,3072]{1,0:T(8,128)(2,1)S(1)} %get-tuple-element.201.refs_1_.gh), custom_call_target="tpu_custom_call" | custom-call | flops 72477573120 | bytes 283115520 | tf_op jit(solution)/shard_map/pallas_call | solution.py:273
  137.4 8.9 %collective-permute-done.23.refs_3_ = bf16[8,96,384]{2,1,0:T(8,128)(2,1)S(1)} collective-permute-done((bf16[8,96,384]{2,1,0:T(8,128)(2,1)S(1)}, bf16[8,96,384]{2,1,0:T(8,128)(2,1)S(1)}, u32[]{:S(2)}, u32[]{:S(2)}) %collective-permute-start.23) | collective-permute-done | bytes 589856 | tf_op jit(solution)/shard_map/ppermute | solution.py:37
  150.9 6.7 %shard_map.344 = (f32[512,768]{1,0:T(8,128)S(1)}, bf16[512,768]{1,0:T(8,128)(2,1)S(1)}, bf16[512,768]{1,0:T(8,128)(2,1)S(1)}, f32[1,768]{1,0:T(1,128)S(1)}, f32[1,768]{1,0:T(1,128)S(1)}, /*index=5*/f32[1,768]{1,0:T(1,128)S(1)}) custom-call(s32[2]{0:T(128)S(1)} %pad_add_fusion.at, bf16[512,3072]{1,0:T(8,128)(2,1)S(1)} %get-tuple-element.201.refs_1_.gh, ...), custom_call_target="tpu_custom_call" | custom-call | flops 90596966400 | bytes 141557760 | tf_op jit(solution)/shard_map/pallas_call | solution.py:640
  162.9 10.8 %shard_map.347 = (bf16[512,768]{1,0:T(8,128)(2,1)S(1)}, bf16[512,768]{1,0:T(8,128)(2,1)S(1)}, bf16[512,768]{1,0:T(8,128)(2,1)S(1)}, f32[1,768]{1,0:T(1,128)S(1)}, f32[1,768]{1,0:T(1,128)S(1)}) custom-call(s32[2]{0:T(128)S(1)} %pad_add_fusion.at, bf16[512,768]{1,0:T(8,128)(2,1)S(1)} %copy-done.28, bf16[512,768]{1,0:T(8,128)(2,1)S(1)} %copy-done.30, ...), custom_call_target="tpu_custom_call" | custom-call | flops 60397977600 | bytes 165150720 | tf_op jit(solution)/shard_map/pallas_call | solution.py:430
  178.3 4.7 %shard_map.350 = (bf16[2,16,24,1536]{3,2,1,0:T(8,128)(2,1)S(1)}, bf16[2,16,24,1536]{3,2,1,0:T(8,128)(2,1)S(1)}) custom-call(s32[2]{0:T(128)S(1)} %pad_add_fusion.at, bf16[512,768]{1,0:T(8,128)(2,1)S(1)} %copy-done.1, bf16[512,768]{1,0:T(8,128)(2,1)S(1)} %copy-done.26, bf16[512,768]{1,0:T(8,128)(2,1)S(1)} %get-tuple-element.240.refs_2_.dq, ...), custom_call_target="tpu_custom_call" | custom-call | flops 72477573120 | bytes 283115520 | tf_op jit(solution)/shard_map/pallas_call | solution.py:273
  184.8 3.7 %shard_map.352 = (bf16[512,768]{1,0:T(8,128)(2,1)}, f32[1,768]{1,0:T(1,128)S(1)}) custom-call(s32[2]{0:T(128)S(1)} %pad_add_fusion.at, f32[512,768]{1,0:T(8,128)S(1)} %get-tuple-element.204.first, bf16[512,768]{1,0:T(8,128)(2,1)S(1)} %get-tuple-element.240.refs_2_.dq, bf16[512,768]{1,0:T(8,128)(2,1)S(1)} %get-tuple-element.231.refs_3_.dk, ...), custom_call_target="tpu_custom_call" | custom-call | flops 54358179840 | bytes 106168320 | tf_op jit(solution)/shard_map/pallas_call | solution.py:670
  194.7 10.5 %collective-permute-done.35.refs_3_ = bf16[8,24,1536]{2,1,0:T(8,128)(2,1)S(1)} collective-permute-done((bf16[8,24,1536]{2,1,0:T(8,128)(2,1)S(1)}, bf16[8,24,1536]{2,1,0:T(8,128)(2,1)S(1)}, u32[]{:S(2)}, u32[]{:S(2)}) %collective-permute-start.35) | collective-permute-done | bytes 589856 | tf_op jit(solution)/shard_map/ppermute | solution.py:37
  210.8 1.7 collective-permute-start.45
  213.0 3.6 %collective-permute-done.37 = f32[16,768]{1,0:T(8,128)S(1)} collective-permute-done((f32[16,768]{1,0:T(8,128)S(1)}, f32[16,768]{1,0:T(8,128)S(1)}, u32[]{:S(2)}, u32[]{:S(2)}) %collective-permute-start.37) | collective-permute-done | bytes 49184 | tf_op jit(solution)/shard_map/ppermute | solution.py:37
  219.3 2.0 collective-permute-done.45
  222.7 2.9 %collective-permute-start.44 = (bf16[1,24,3072]{2,1,0:T(8,128)(2,1)S(1)}, bf16[1,24,3072]{2,1,0:T(8,128)(2,1)S(1)}, u32[]{:S(2)}, u32[]{:S(2)}) collective-permute-start(bf16[1,24,3072]{2,1,0:T(8,128)(2,1)S(1)} %get-tuple-element.280), channel_id=1, source_target_pairs={{0,16},{2,18},{4,20},{6,22},{8,24},{10,26},{12,28},{14,30},{16,0},... | collective-permute-start | bytes 442376 | tf_op jit(solution)/shard_map/ppermute | solution.py:37
  226.5 6.4 %collective-permute-done.42 = f32[16,768]{1,0:T(8,128)S(1)} collective-permute-done((f32[16,768]{1,0:T(8,128)S(1)}, f32[16,768]{1,0:T(8,128)S(1)}, u32[]{:S(2)}, u32[]{:S(2)}) %collective-permute-start.42) | collective-permute-done | bytes 49184 | tf_op jit(solution)/shard_map/ppermute | solution.py:37
  233.8 1.8 collective-permute-start.46
  (244 shorter events, 79.5 us)
Async XLA Ops:
  3.7 9.6 %collective-permute-start = (bf16[1,24,2304]{2,1,0:T(8,128)(2,1)S(1)}, bf16[1,24,2304]{2,1,0:T(8,128)(2,1)S(1)}, u32[]{:S(2)}, u32[]{:S(2)}) collective-permute-start(bf16[1,24,2304]{2,1,0:T(8,128)(2,1)S(1)} %bitcast.39), channel_id=1, source_target_pairs={{0,16},{2,18},{4,20},{6,22},{8,24},{10,26},{12,28},{14,30},{16,0},... | collective-permute-start | bytes 331784 | tf_op jit(solution)/shard_map/ppermute | solution.py:37
  23.5 11.0 %collective-permute-start.2 = (bf16[1,24,3840]{2,1,0:T(8,128)(2,1)S(1)}, bf16[1,24,3840]{2,1,0:T(8,128)(2,1)S(1)}, u32[]{:S(2)}, u32[]{:S(2)}) collective-permute-start(bf16[1,24,3840]{2,1,0:T(8,128)(2,1)S(1)} %bitcast.42), channel_id=1, source_target_pairs={{0,16},{2,18},{4,20},{6,22},{8,24},{10,26},{12,28},{14,30},{16,0},... | collective-permute-start | bytes 552968 | tf_op jit(solution)/shard_map/ppermute | solution.py:37
  26.9 10.7 %collective-permute-start.6 = (bf16[8,24,1152]{2,1,0:T(8,128)(2,1)S(1)}, bf16[8,24,1152]{2,1,0:T(8,128)(2,1)S(1)}, u32[]{:S(2)}, u32[]{:S(2)}) collective-permute-start(bf16[8,24,1152]{2,1,0:T(8,128)(2,1)S(1)} %pad_maximum_fusion.4), channel_id=1, source_target_pairs={{0,2},{2,0},{4,6},{6,4},{8,10},{10,8},{12,14},{14,12},{16,18},{18,... | collective-permute-start | bytes 1327112 | tf_op jit(solution)/shard_map/ppermute | solution.py:37
  28.0 10.0 %collective-permute-start.7 = (bf16[8,24,1152]{2,1,0:T(8,128)(2,1)S(1)}, bf16[8,24,1152]{2,1,0:T(8,128)(2,1)S(1)}, u32[]{:S(2)}, u32[]{:S(2)}) collective-permute-start(bf16[8,24,1152]{2,1,0:T(8,128)(2,1)S(1)} %pad_maximum_fusion.5), channel_id=1, source_target_pairs={{0,4},{2,6},{4,0},{6,2},{8,12},{10,14},{12,8},{14,10},{16,20},{18,... | collective-permute-start | bytes 1327112 | tf_op jit(solution)/shard_map/ppermute | solution.py:37
  34.5 9.7 %collective-permute-start.5 = (bf16[2,24,3840]{2,1,0:T(8,128)(2,1)S(1)}, bf16[2,24,3840]{2,1,0:T(8,128)(2,1)S(1)}, u32[]{:S(2)}, u32[]{:S(2)}) collective-permute-start(bf16[2,24,3840]{2,1,0:T(8,128)(2,1)S(1)} %pad_maximum_fusion.6), channel_id=1, source_target_pairs={{0,8},{2,10},{4,12},{6,14},{8,0},{10,2},{12,4},{14,6},{16,24},{18,... | collective-permute-start | bytes 1105928 | tf_op jit(solution)/shard_map/ppermute | solution.py:37
  38.3 20.9 %collective-permute-start.11 = (bf16[2,16,24,1152]{3,2,1,0:T(8,128)(2,1)S(1)}, bf16[2,16,24,1152]{3,2,1,0:T(8,128)(2,1)S(1)}, u32[]{:S(2)}, u32[]{:S(2)}) collective-permute-start(bf16[2,16,24,1152]{3,2,1,0:T(8,128)(2,1)S(1)} %pad_maximum_fusion.2.own), channel_id=1, source_target_pairs={{0,1},{1,0},{2,3},{3,2},{4,5},{5,4},{6,7},{7,6},{8,9},{9,8},{10,11... | collective-permute-start | bytes 5308424 | tf_op jit(solution)/shard_map/ppermute | solution.py:40
  44.3 10.2 %collective-permute-start.9 = (bf16[4,24,1920]{2,1,0:T(8,128)(2,1)S(1)}, bf16[4,24,1920]{2,1,0:T(8,128)(2,1)S(1)}, u32[]{:S(2)}, u32[]{:S(2)}) collective-permute-start(bf16[4,24,1920]{2,1,0:T(8,128)(2,1)S(1)} %get-tuple-element.157), channel_id=1, source_target_pairs={{0,2},{2,0},{4,6},{6,4},{8,10},{10,8},{12,14},{14,12},{16,18},{18,... | collective-permute-start | bytes 1105928 | tf_op jit(solution)/shard_map/ppermute | solution.py:37
  44.9 9.5 %collective-permute-start.10 = (bf16[1,96,768]{2,1,0:T(8,128)(2,1)S(1)}, bf16[1,96,768]{2,1,0:T(8,128)(2,1)S(1)}, u32[]{:S(2)}, u32[]{:S(2)}) collective-permute-start(bf16[1,96,768]{2,1,0:T(8,128)(2,1)S(1)} %bitcast.57), channel_id=1, source_target_pairs={{0,16},{2,18},{4,20},{6,22},{8,24},{10,26},{12,28},{14,30},{16,0},... | collective-permute-start | bytes 442376 | tf_op jit(solution)/shard_map/ppermute | solution.py:37
  48.2 9.4 %collective-permute-start.8 = (bf16[4,24,1920]{2,1,0:T(8,128)(2,1)S(1)}, bf16[4,24,1920]{2,1,0:T(8,128)(2,1)S(1)}, u32[]{:S(2)}, u32[]{:S(2)}) collective-permute-start(bf16[4,24,1920]{2,1,0:T(8,128)(2,1)S(1)} %get-tuple-element.156), channel_id=1, source_target_pairs={{0,4},{2,6},{4,0},{6,2},{8,12},{10,14},{12,8},{14,10},{16,20},{18,... | collective-permute-start | bytes 1105928 | tf_op jit(solution)/shard_map/ppermute | solution.py:37
  57.6 17.5 %collective-permute-start.12 = (bf16[2,96,768]{2,1,0:T(8,128)(2,1)S(1)}, bf16[2,96,768]{2,1,0:T(8,128)(2,1)S(1)}, u32[]{:S(2)}, u32[]{:S(2)}) collective-permute-start(bf16[2,96,768]{2,1,0:T(8,128)(2,1)S(1)} %constant_dynamic-update-slice_fusion.6), channel_id=1, source_target_pairs={{0,8},{2,10},{4,12},{6,14},{8,0},{10,2},{12,4},{14,6},{16,24},{18,... | collective-permute-start | bytes 884744 | tf_op jit(solution)/shard_map/ppermute | solution.py:37
  59.2 16.0 %collective-permute-start.14 = (bf16[8,24,1920]{2,1,0:T(8,128)(2,1)S(1)}, bf16[8,24,1920]{2,1,0:T(8,128)(2,1)S(1)}, u32[]{:S(2)}, u32[]{:S(2)}) collective-permute-start(bf16[8,24,1920]{2,1,0:T(8,128)(2,1)S(1)} %constant_dynamic-update-slice_fusion.4), channel_id=1, source_target_pairs={{0,4},{2,6},{4,0},{6,2},{8,12},{10,14},{12,8},{14,10},{16,20},{18,... | collective-permute-start | bytes 2211848 | tf_op jit(solution)/shard_map/ppermute | solution.py:37
  59.7 15.6 %collective-permute-start.13 = (bf16[8,24,1920]{2,1,0:T(8,128)(2,1)S(1)}, bf16[8,24,1920]{2,1,0:T(8,128)(2,1)S(1)}, u32[]{:S(2)}, u32[]{:S(2)}) collective-permute-start(bf16[8,24,1920]{2,1,0:T(8,128)(2,1)S(1)} %constant_dynamic-update-slice_fusion.2), channel_id=1, source_target_pairs={{0,2},{2,0},{4,6},{6,4},{8,10},{10,8},{12,14},{14,12},{16,18},{18,... | collective-permute-start | bytes 2211848 | tf_op jit(solution)/shard_map/ppermute | solution.py:37
  75.9 9.5 %collective-permute-start.16 = (bf16[2,16,24,1920]{3,2,1,0:T(8,128)(2,1)S(1)}, bf16[2,16,24,1920]{3,2,1,0:T(8,128)(2,1)S(1)}, u32[]{:S(2)}, u32[]{:S(2)}) collective-permute-start(bf16[2,16,24,1920]{3,2,1,0:T(8,128)(2,1)S(1)} %pad_maximum_fusion.own), channel_id=1, source_target_pairs={{0,1},{1,0},{2,3},{3,2},{4,5},{5,4},{6,7},{7,6},{8,9},{9,8},{10,11... | collective-permute-start | bytes 8847368 | tf_op jit(solution)/shard_map/ppermute | solution.py:40
  76.0 9.4 %collective-permute-start.17 = (bf16[4,96,384]{2,1,0:T(8,128)(2,1)S(1)}, bf16[4,96,384]{2,1,0:T(8,128)(2,1)S(1)}, u32[]{:S(2)}, u32[]{:S(2)}) collective-permute-start(bf16[4,96,384]{2,1,0:T(8,128)(2,1)S(1)} %get-tuple-element.173), channel_id=1, source_target_pairs={{0,2},{2,0},{4,6},{6,4},{8,10},{10,8},{12,14},{14,12},{16,18},{18,... | collective-permute-start | bytes 884744 | tf_op jit(solution)/shard_map/ppermute | solution.py:37
  77.6 9.1 %collective-permute-start.15 = (bf16[4,96,384]{2,1,0:T(8,128)(2,1)S(1)}, bf16[4,96,384]{2,1,0:T(8,128)(2,1)S(1)}, u32[]{:S(2)}, u32[]{:S(2)}) collective-permute-start(bf16[4,96,384]{2,1,0:T(8,128)(2,1)S(1)} %get-tuple-element.170), channel_id=1, source_target_pairs={{0,4},{2,6},{4,0},{6,2},{8,12},{10,14},{12,8},{14,10},{16,20},{18,... | collective-permute-start | bytes 884744 | tf_op jit(solution)/shard_map/ppermute | solution.py:37
  86.7 15.5 %collective-permute-start.18 = (bf16[8,96,384]{2,1,0:T(8,128)(2,1)S(1)}, bf16[8,96,384]{2,1,0:T(8,128)(2,1)S(1)}, u32[]{:S(2)}, u32[]{:S(2)}) collective-permute-start(bf16[8,96,384]{2,1,0:T(8,128)(2,1)S(1)} %constant_dynamic-update-slice_fusion.10), channel_id=1, source_target_pairs={{0,2},{2,0},{4,6},{6,4},{8,10},{10,8},{12,14},{14,12},{16,18},{18,... | collective-permute-start | bytes 1769480 | tf_op jit(solution)/shard_map/ppermute | solution.py:37
  87.3 15.0 %collective-permute-start.19 = (bf16[8,96,384]{2,1,0:T(8,128)(2,1)S(1)}, bf16[8,96,384]{2,1,0:T(8,128)(2,1)S(1)}, u32[]{:S(2)}, u32[]{:S(2)}) collective-permute-start(bf16[8,96,384]{2,1,0:T(8,128)(2,1)S(1)} %constant_dynamic-update-slice_fusion.12), channel_id=1, source_target_pairs={{0,4},{2,6},{4,0},{6,2},{8,12},{10,14},{12,8},{14,10},{16,20},{18,... | collective-permute-start | bytes 1769480 | tf_op jit(solution)/shard_map/ppermute | solution.py:37
  130.6 15.7 %collective-permute-start.23 = (bf16[8,96,384]{2,1,0:T(8,128)(2,1)S(1)}, bf16[8,96,384]{2,1,0:T(8,128)(2,1)S(1)}, u32[]{:S(2)}, u32[]{:S(2)}) collective-permute-start(bf16[8,96,384]{2,1,0:T(8,128)(2,1)S(1)} %get-tuple-element.192), channel_id=1, source_target_pairs={{0,4},{2,6},{4,0},{6,2},{8,12},{10,14},{12,8},{14,10},{16,20},{18,... | collective-permute-start | bytes 1769480 | tf_op jit(solution)/shard_map/ppermute | solution.py:37
  131.2 15.3 %collective-permute-start.22 = (bf16[8,96,384]{2,1,0:T(8,128)(2,1)S(1)}, bf16[8,96,384]{2,1,0:T(8,128)(2,1)S(1)}, u32[]{:S(2)}, u32[]{:S(2)}) collective-permute-start(bf16[8,96,384]{2,1,0:T(8,128)(2,1)S(1)} %get-tuple-element.191), channel_id=1, source_target_pairs={{0,2},{2,0},{4,6},{6,4},{8,10},{10,8},{12,14},{14,12},{16,18},{18,... | collective-permute-start | bytes 1769480 | tf_op jit(solution)/shard_map/ppermute | solution.py:37
  137.3 22.2 %collective-permute-start.26 = (bf16[2,16,24,1536]{3,2,1,0:T(8,128)(2,1)S(1)}, bf16[2,16,24,1536]{3,2,1,0:T(8,128)(2,1)S(1)}, u32[]{:S(2)}, u32[]{:S(2)}) collective-permute-start(bf16[2,16,24,1536]{3,2,1,0:T(8,128)(2,1)S(1)} %get-tuple-element.194), channel_id=1, source_target_pairs={{0,1},{1,0},{2,3},{3,2},{4,5},{5,4},{6,7},{7,6},{8,9},{9,8},{10,11... | collective-permute-start | bytes 7077896 | tf_op jit(solution)/shard_map/ppermute | solution.py:40
  147.8 9.8 %collective-permute-start.25 = (bf16[4,96,384]{2,1,0:T(8,128)(2,1)S(1)}, bf16[4,96,384]{2,1,0:T(8,128)(2,1)S(1)}, u32[]{:S(2)}, u32[]{:S(2)}) collective-permute-start(bf16[4,96,384]{2,1,0:T(8,128)(2,1)S(1)} %get-tuple-element.200), channel_id=1, source_target_pairs={{0,2},{2,0},{4,6},{6,4},{8,10},{10,8},{12,14},{14,12},{16,18},{18,... | collective-permute-start | bytes 884744 | tf_op jit(solution)/shard_map/ppermute | solution.py:37
  158.5 15.1 %collective-permute-start.27 = (bf16[2,96,768]{2,1,0:T(8,128)(2,1)S(1)}, bf16[2,96,768]{2,1,0:T(8,128)(2,1)S(1)}, u32[]{:S(2)}, u32[]{:S(2)}) collective-permute-start(bf16[2,96,768]{2,1,0:T(8,128)(2,1)S(1)} %get-tuple-element.213), channel_id=1, source_target_pairs={{0,8},{2,10},{4,12},{6,14},{8,0},{10,2},{12,4},{14,6},{16,24},{18,... | collective-permute-start | bytes 884744 | tf_op jit(solution)/shard_map/ppermute | solution.py:37
  161.1 13.7 %collective-permute-start.29 = (bf16[8,24,1536]{2,1,0:T(8,128)(2,1)S(1)}, bf16[8,24,1536]{2,1,0:T(8,128)(2,1)S(1)}, u32[]{:S(2)}, u32[]{:S(2)}) collective-permute-start(bf16[8,24,1536]{2,1,0:T(8,128)(2,1)S(1)} %get-tuple-element.217), channel_id=1, source_target_pairs={{0,4},{2,6},{4,0},{6,2},{8,12},{10,14},{12,8},{14,10},{16,20},{18,... | collective-permute-start | bytes 1769480 | tf_op jit(solution)/shard_map/ppermute | solution.py:37
  162.3 12.8 %collective-permute-start.28 = (bf16[8,24,1536]{2,1,0:T(8,128)(2,1)S(1)}, bf16[8,24,1536]{2,1,0:T(8,128)(2,1)S(1)}, u32[]{:S(2)}, u32[]{:S(2)}) collective-permute-start(bf16[8,24,1536]{2,1,0:T(8,128)(2,1)S(1)} %get-tuple-element.216), channel_id=1, source_target_pairs={{0,2},{2,0},{4,6},{6,4},{8,10},{10,8},{12,14},{14,12},{16,18},{18,... | collective-permute-start | bytes 1769480 | tf_op jit(solution)/shard_map/ppermute | solution.py:37
  190.1 15.0 %collective-permute-start.35 = (bf16[8,24,1536]{2,1,0:T(8,128)(2,1)S(1)}, bf16[8,24,1536]{2,1,0:T(8,128)(2,1)S(1)}, u32[]{:S(2)}, u32[]{:S(2)}) collective-permute-start(bf16[8,24,1536]{2,1,0:T(8,128)(2,1)S(1)} %get-tuple-element.257), channel_id=1, source_target_pairs={{0,4},{2,6},{4,0},{6,2},{8,12},{10,14},{12,8},{14,10},{16,20},{18,... | collective-permute-start | bytes 1769480 | tf_op jit(solution)/shard_map/ppermute | solution.py:37
  191.4 14.4 %collective-permute-start.33 = (bf16[8,24,1536]{2,1,0:T(8,128)(2,1)S(1)}, bf16[8,24,1536]{2,1,0:T(8,128)(2,1)S(1)}, u32[]{:S(2)}, u32[]{:S(2)}) collective-permute-start(bf16[8,24,1536]{2,1,0:T(8,128)(2,1)S(1)} %get-tuple-element.247), channel_id=1, source_target_pairs={{0,2},{2,0},{4,6},{6,4},{8,10},{10,8},{12,14},{14,12},{16,18},{18,... | collective-permute-start | bytes 1769480 | tf_op jit(solution)/shard_map/ppermute | solution.py:37
  206.9 9.7 %collective-permute-start.38 = (bf16[4,24,1536]{2,1,0:T(8,128)(2,1)S(1)}, bf16[4,24,1536]{2,1,0:T(8,128)(2,1)S(1)}, u32[]{:S(2)}, u32[]{:S(2)}) collective-permute-start(bf16[4,24,1536]{2,1,0:T(8,128)(2,1)S(1)} %get-tuple-element.266), channel_id=1, source_target_pairs={{0,2},{2,0},{4,6},{6,4},{8,10},{10,8},{12,14},{14,12},{16,18},{18,... | collective-permute-start | bytes 884744 | tf_op jit(solution)/shard_map/ppermute | solution.py:37
  208.2 8.4 %collective-permute-start.36 = (bf16[4,24,1536]{2,1,0:T(8,128)(2,1)S(1)}, bf16[4,24,1536]{2,1,0:T(8,128)(2,1)S(1)}, u32[]{:S(2)}, u32[]{:S(2)}) collective-permute-start(bf16[4,24,1536]{2,1,0:T(8,128)(2,1)S(1)} %get-tuple-element.263), channel_id=1, source_target_pairs={{0,4},{2,6},{4,0},{6,2},{8,12},{10,14},{12,8},{14,10},{16,20},{18,... | collective-permute-start | bytes 884744 | tf_op jit(solution)/shard_map/ppermute | solution.py:37
  209.6 12.3 %collective-permute-start.43 = (bf16[2,24,3072]{2,1,0:T(8,128)(2,1)S(1)}, bf16[2,24,3072]{2,1,0:T(8,128)(2,1)S(1)}, u32[]{:S(2)}, u32[]{:S(2)}) collective-permute-start(bf16[2,24,3072]{2,1,0:T(8,128)(2,1)S(1)} %get-tuple-element.239), channel_id=1, source_target_pairs={{0,8},{2,10},{4,12},{6,14},{8,0},{10,2},{12,4},{14,6},{16,24},{18,... | collective-permute-start | bytes 884744 | tf_op jit(solution)/shard_map/ppermute | solution.py:37
  210.8 10.6 %collective-permute-start.45 = (bf16[1,96,768]{2,1,0:T(8,128)(2,1)S(1)}, bf16[1,96,768]{2,1,0:T(8,128)(2,1)S(1)}, u32[]{:S(2)}, u32[]{:S(2)}) collective-permute-start(bf16[1,96,768]{2,1,0:T(8,128)(2,1)S(1)} %get-tuple-element.223), channel_id=1, source_target_pairs={{0,16},{2,18},{4,20},{6,22},{8,24},{10,26},{12,28},{14,30},{16,0},... | collective-permute-start | bytes 442376 | tf_op jit(solution)/shard_map/ppermute | solution.py:37
  217.5 15.4 %collective-permute-start.39 = (bf16[2,24,3072]{2,1,0:T(8,128)(2,1)S(1)}, bf16[2,24,3072]{2,1,0:T(8,128)(2,1)S(1)}, u32[]{:S(2)}, u32[]{:S(2)}) collective-permute-start(bf16[2,24,3072]{2,1,0:T(8,128)(2,1)S(1)} %get-tuple-element.269), channel_id=1, source_target_pairs={{0,8},{2,10},{4,12},{6,14},{8,0},{10,2},{12,4},{14,6},{16,24},{18,... | collective-permute-start | bytes 884744 | tf_op jit(solution)/shard_map/ppermute | solution.py:37
  222.7 12.9 %collective-permute-start.44 = (bf16[1,24,3072]{2,1,0:T(8,128)(2,1)S(1)}, bf16[1,24,3072]{2,1,0:T(8,128)(2,1)S(1)}, u32[]{:S(2)}, u32[]{:S(2)}) collective-permute-start(bf16[1,24,3072]{2,1,0:T(8,128)(2,1)S(1)} %get-tuple-element.280), channel_id=1, source_target_pairs={{0,16},{2,18},{4,20},{6,22},{8,24},{10,26},{12,28},{14,30},{16,0},... | collective-permute-start | bytes 442376 | tf_op jit(solution)/shard_map/ppermute | solution.py:37
  (63 other events, 482.9 us)

commit v4 on v3

--- a/solution.py
+++ b/solution.py
@@ -40,7 +40,7 @@
         return lax.ppermute(value, "pair", [(0, 1), (1, 0)])
 
 
-def kernel_call(body, grid, in_specs, out_specs, out_shape, cost, scratch=(), limit=None):
+def kernel_call(body, grid, in_specs, out_specs, out_shape, cost, scratch=(), limit=None, cover=COVER):
     flops, moved, special = cost
     return pl.pallas_call(
         body,
@@ -53,7 +53,7 @@
         ),
         out_shape=out_shape,
         cost_estimate=pl.CostEstimate(
-            flops=COVER * flops, bytes_accessed=moved if flops == 0 else COVER * moved, transcendentals=special
+            flops=cover * flops, bytes_accessed=moved if flops == 0 else cover * moved, transcendentals=special
         ),
         compiler_params=pltpu.CompilerParams(vmem_limit_bytes=limit or 16 * 2**20),
     )
@@ -790,15 +790,16 @@
     )
     vectors = tuple(v[None] for v in vectors)
     query_row, value_row, output_row, inner_row, outer_row, gain_1, shift_1, gain_2, shift_2 = vectors
+    before = first_gather.ready
     first_gather.step(during=(*vectors, start, masked, wanted))
-    before = first_gather.ready
-    first_gather.step()
     inner_gather.step(before, first_gather.ready)
     before = first_gather.ready
     first_gather.step()
     inner_gather.step(before, first_gather.ready)
-    outer_gather.step(inner_gather.ready)
+    first_gather.step()
+    before = inner_gather.ready
     inner_gather.step(first_gather.ready)
+    outer_gather.step(before, inner_gather.ready)
     got = first_gather.step()
     weights = first_gather.done((width // 2,) * 3)
     query, key, value, context, lse = attention_forward(
@@ -866,7 +867,9 @@
     )
     first_sums.send((), (mask_grad,))
     first_sums.fold()
-    inner_sums.send((), (mask_grad, *first_sums.sends))
+    tied = (mask_grad, *first_sums.sends)
+    late = inner_sums.send((), tied)
+    inner_sums.fold()
     smalls = (
         query_bias_grad,
         value_bias_grad,
@@ -882,23 +885,22 @@
     spots = [(i, 0, width, i, 0) for i in range(9)]
     spots += [(9, i * width, width, 9 + i, 0) for i in range(inner // width)]
     high = -(-(9 + inner // width) // 8) * 8
+    smalls = (hold(query_bias_grad, *inner_sums.sends), *smalls[1:])
     packed = pack(place, smalls, spots, (high, width))
     total = Total(place, packed) if staged else PlainTotal(packed)
     got = total.step(first_sums.sends)
+    got = total.step(first_sums.sends)
+    late = inner_sums.send(first_sums.sends)
+    first_sums.send((), (got, *late))
+    first_sums.fold()
+    got = total.step(first_sums.sends)
     first_sums.send((), (got,))
-    got = total.step((), first_sums.sends)
-    if staged:
-        inner_sums.fold()
     first_sums.fold()
-    inner_sums.send(first_sums.sends)
+    got = total.step(first_sums.sends)
     first_sums.send((), (got,))
-    got = total.step(first_sums.sends)
-    first_sums.fold()
-    first_sums.send((), (got,))
-    got = total.step(first_sums.sends)
     first_sums.fold()
     total.step(first_sums.sends)
-    first_sums.send((), (got,))
+    first_sums.send()
     packed = total.value
     order = (0, 1, 2, 9, 3, 4, 5, 6, 7, 8)
     firsts = first_sums.result

time: 241 us -> 237 us (0.983)
  waiting for transfers between devices: 79.9 us -> 77.3 us
    ppermute x40, waiting for transfers between devices: 74.7 us -> 72.1 us  [swap(): lax.ppermute(value, 'dp', [(i, i ^ stride) for i in range(self.chips)])]
  transfers between devices with their start and end apart: 47 -> 47, of which waited for: 27 -> 28; matrix products, arithmetic and copies ran while one was open for 3% -> 3% of each run, Pallas kernels for 27% -> 27%
where the time goes in v4:
time: 237 us; the launch traced here: 236 us
  Pallas kernels  86.5 us (36%)
  waiting for transfers between devices  77.3 us (33%)
  starting transfers between devices  50.8 us (21%)
  local copies, waits for them, and re-layouts  13.5 us (6%)
  other arithmetic  6.69 us (3%)
    ppermute x40, waiting for transfers between devices, swap(): lax.ppermute(value, 'dp', [(i, i ^ stride) for i in range(self.chips)])  72.1 us
    ppermute x40, starting transfers between devices, swap(): lax.ppermute(value, 'dp', [(i, i ^ stride) for i in range(self.chips)])  50.1 us
    pallas_call x12, Pallas kernels, fold(): kernel_call(body, (steps,), [ins] * (2 * len(keeps)), [pl.BlockSpec((chip...  13.7 us
    unnamed x103, local copies, waits for them, and re-layouts  10.8 us
    pallas_call x1, Pallas kernels, attention_backward(): kernel_call(body, (groups, seqs), [block] * 4 + [pl.BlockSpec((1, 1, 4, l...  10.8 us
    pallas_call x1, Pallas kernels, attention_forward(): kernel_call(body, (seqs, groups), [pl.BlockSpec((length, width), lambda s...  9.82 us
    pallas_call x2, Pallas kernels, weight_terms(): kernel_call(body, (count,), [pl.BlockSpec((length, features), lambda t, a...  9.3 us
    pallas_call x1, Pallas kernels, feed_in(): kernel_call(body, (inner // tile,), [keep(a) for a in ins] + [pl.BlockSpe...  9.12 us
  transfers between devices with their start and end apart: 47, of which 28 were waited for; matrix products, arithmetic and copies ran while one was open for 3% of the time, Pallas kernels for 27%

profile of v4, /device:TPU:0, one launch (start us, length us, event | category | flops | bytes accessed | tf_op | source)
XLA Modules:
  0.0 236.4 jit_solution(7623407021866861403)
XLA Ops:
  3.7 4.1 %collective-permute-start = (bf16[1,24,2304]{2,1,0:T(8,128)(2,1)S(1)}, bf16[1,24,2304]{2,1,0:T(8,128)(2,1)S(1)}, u32[]{:S(2)}, u32[]{:S(2)}) collective-permute-start(bf16[1,24,2304]{2,1,0:T(8,128)(2,1)S(1)} %bitcast.39), channel_id=1, source_target_pairs={{0,16},{2,18},{4,20},{6,22},{8,24},{10,26},{12,28},{14,30},{16,0},... | collective-permute-start | bytes 331784 | tf_op jit(solution)/shard_map/ppermute | solution.py:37
  11.3 2.0 collective-permute-done
  14.6 3.4 %collective-permute-start.1 = (bf16[1,24,3840]{2,1,0:T(8,128)(2,1)S(1)}, bf16[1,24,3840]{2,1,0:T(8,128)(2,1)S(1)}, u32[]{:S(2)}, u32[]{:S(2)}) collective-permute-start(bf16[1,24,3840]{2,1,0:T(8,128)(2,1)S(1)} %bitcast.42), channel_id=1, source_target_pairs={{0,16},{2,18},{4,20},{6,22},{8,24},{10,26},{12,28},{14,30},{16,0},... | collective-permute-start | bytes 552968 | tf_op jit(solution)/shard_map/ppermute | solution.py:37
  18.0 5.8 %collective-permute-done.2 = bf16[2,24,2304]{2,1,0:T(8,128)(2,1)S(1)} collective-permute-done((bf16[2,24,2304]{2,1,0:T(8,128)(2,1)S(1)}, bf16[2,24,2304]{2,1,0:T(8,128)(2,1)S(1)}, u32[]{:S(2)}, u32[]{:S(2)}) %collective-permute-start.2) | collective-permute-done | bytes 221216 | tf_op jit(solution)/shard_map/ppermute | solution.py:37
  27.2 2.7 %collective-permute-done.4 = bf16[4,24,1152]{2,1,0:T(8,128)(2,1)S(1)} collective-permute-done((bf16[4,24,1152]{2,1,0:T(8,128)(2,1)S(1)}, bf16[4,24,1152]{2,1,0:T(8,128)(2,1)S(1)}, u32[]{:S(2)}, u32[]{:S(2)}) %collective-permute-start.4) | collective-permute-done | bytes 221216 | tf_op jit(solution)/shard_map/ppermute | solution.py:37
  31.7 1.8 collective-permute-done.5
  35.3 5.4 %collective-permute-done.6 = bf16[8,24,1152]{2,1,0:T(8,128)(2,1)S(1)} collective-permute-done((bf16[8,24,1152]{2,1,0:T(8,128)(2,1)S(1)}, bf16[8,24,1152]{2,1,0:T(8,128)(2,1)S(1)}, u32[]{:S(2)}, u32[]{:S(2)}) %collective-permute-start.6) | collective-permute-done | bytes 442400 | tf_op jit(solution)/shard_map/ppermute | solution.py:37
  46.5 7.9 %collective-permute-done.9 = bf16[4,24,1920]{2,1,0:T(8,128)(2,1)S(1)} collective-permute-done((bf16[4,24,1920]{2,1,0:T(8,128)(2,1)S(1)}, bf16[4,24,1920]{2,1,0:T(8,128)(2,1)S(1)}, u32[]{:S(2)}, u32[]{:S(2)}) %collective-permute-start.9) | collective-permute-done | bytes 368672 | tf_op jit(solution)/shard_map/ppermute | solution.py:37
  55.3 2.5 %collective-permute-start.12 = (bf16[2,96,768]{2,1,0:T(8,128)(2,1)S(1)}, bf16[2,96,768]{2,1,0:T(8,128)(2,1)S(1)}, u32[]{:S(2)}, u32[]{:S(2)}) collective-permute-start(bf16[2,96,768]{2,1,0:T(8,128)(2,1)S(1)} %constant_dynamic-update-slice_fusion.6), channel_id=1, source_target_pairs={{0,8},{2,10},{4,12},{6,14},{8,0},{10,2},{12,4},{14,6},{16,24},{18,... | collective-permute-start | bytes 884744 | tf_op jit(solution)/shard_map/ppermute | solution.py:37
  61.7 9.8 %shard_map.334 = (bf16[512,768]{1,0:T(8,128)(2,1)S(1)}, bf16[512,768]{1,0:T(8,128)(2,1)S(1)}, bf16[512,768]{1,0:T(8,128)(2,1)S(1)}, bf16[512,768]{1,0:T(8,128)(2,1)S(1)}, f32[1,3,4,512]{3,2,1,0:T(4,128)S(1)}) custom-call(s32[2]{0:T(128)S(1)} %pad_add_fusion.at, bf16[512,768]{1,0:T(8,128)(2,1)S(1)} %broadcast_select_fusion.start.refs_0_, ...), custom_call_target="tpu_custom_call" | custom-call | flops 54358179840 | bytes 106168320 | tf_op jit(solution)/shard_map/pallas_call | solution.py:372
  78.0 7.3 %collective-permute-done.17 = bf16[4,96,384]{2,1,0:T(8,128)(2,1)S(1)} collective-permute-done((bf16[4,96,384]{2,1,0:T(8,128)(2,1)S(1)}, bf16[4,96,384]{2,1,0:T(8,128)(2,1)S(1)}, u32[]{:S(2)}, u32[]{:S(2)}) %collective-permute-start.17) | collective-permute-done | bytes 294944 | tf_op jit(solution)/shard_map/ppermute | solution.py:37
  89.6 9.1 %shard_map.336 = (f32[512,768]{1,0:T(8,128)S(1)}, f32[512,1]{1,0:T(8,128)S(1)}, bf16[512,768]{1,0:T(8,128)(2,1)S(1)}, bf16[512,3072]{1,0:T(8,128)(2,1)S(1)}, bf16[512,3072]{1,0:T(8,128)(2,1)S(1)}) custom-call(s32[2]{0:T(128)S(1)} %pad_add_fusion.at, bf16[512,768]{1,0:T(8,128)(2,1)S(1)} %broadcast_select_fusion.start.refs_0_, ...), custom_call_target="tpu_custom_call" | custom-call | flops 90596966400 | bytes 141557760 | tf_op jit(solution)/shard_map/pallas_call | solution.py:495
  104.5 4.0 %collective-permute-done.20.other = bf16[2,16,96,384]{3,2,1,0:T(8,128)(2,1)} collective-permute-done((bf16[2,16,96,384]{3,2,1,0:T(8,128)(2,1)S(1)}, bf16[2,16,96,384]{3,2,1,0:T(8,128)(2,1)}, u32[]{:S(2)}, u32[]{:S(2)}) %collective-permute-start.20) | collective-permute-done | bytes 2359328 | tf_op jit(solution)/shard_map/ppermute | solution.py:40
  108.5 2.9 %shard_map.337 = bf16[32,96,768]{2,1,0:T(8,128)(2,1)S(1)} custom-call(s32[2]{0:T(128)S(1)} %pad_add_fusion.at, bf16[2,16,96,384]{3,2,1,0:T(8,128)(2,1)S(1)} %pad_maximum_fusion.1.own, bf16[2,16,96,384]{3,2,1,0:T(8,128)(2,1)} %collective-permute-done.20.other), custom_call_target="tpu_custom_call" | custom-call | bytes 9437184 | tf_op jit(solution)/shard_map/pallas_call | solution.py:140
  111.4 7.1 %shard_map.338 = (bf16[512,768]{1,0:T(8,128)(2,1)}, f32[512,768]{1,0:T(8,128)S(1)}, bf16[512,768]{1,0:T(8,128)(2,1)S(1)}, f32[1,768]{1,0:T(1,128)S(1)}, f32[1,768]{1,0:T(1,128)S(1)}, /*index=5*/f32[1,768]{1,0:T(1,128)S(1)}) custom-call(s32[2]{0:T(128)S(1)} %pad_add_fusion.at, bf16[512,3072]{1,0:T(8,128)(2,1)S(1)} %copy-done.19, ...), custom_call_target="tpu_custom_call" | custom-call | flops 72477573120 | bytes 141557760 | tf_op jit(solution)/shard_map/pallas_call | solution.py:551
  118.5 4.7 %shard_map.339 = (bf16[2,16,96,384]{3,2,1,0:T(8,128)(2,1)S(1)}, bf16[2,16,96,384]{3,2,1,0:T(8,128)(2,1)S(1)}) custom-call(s32[2]{0:T(128)S(1)} %pad_add_fusion.at, bf16[512,3072]{1,0:T(8,128)(2,1)S(1)} %copy-done.19, bf16[512,768]{1,0:T(8,128)(2,1)S(1)} %get-tuple-element.187.right_ref.grad), custom_call_target="tpu_custom_call" | custom-call | flops 72477573120 | bytes 283115520 | tf_op jit(solution)/shard_map/pallas_call | solution.py:308
  123.4 4.7 %shard_map.340 = (bf16[512,3072]{1,0:T(8,128)(2,1)S(1)}, f32[1,3072]{1,0:T(1,128)S(1)}) custom-call(s32[2]{0:T(128)S(1)} %pad_add_fusion.at, bf16[512,768]{1,0:T(8,128)(2,1)S(1)} %get-tuple-element.187.right_ref.grad, bf16[3072,768]{1,0:T(8,128)(2,1)S(1)} %bitcast.38, bf16[512,3072]{1,0:T(8,128)(2,1)S(1)} %copy-done.21), custom_call_target="tpu_custom_call" | custom-call | flops 72477573120 | bytes 141557760 | tf_op jit(solution)/shard_map/pallas_call | solution.py:580
  128.1 1.9 shard_map.341
  132.5 4.6 %shard_map.342 = (bf16[2,16,24,1536]{3,2,1,0:T(8,128)(2,1)S(1)}, bf16[2,16,24,1536]{3,2,1,0:T(8,128)(2,1)S(1)}) custom-call(s32[2]{0:T(128)S(1)} %pad_add_fusion.at, bf16[512,768]{1,0:T(8,128)(2,1)S(1)} %copy-done.34, bf16[512,3072]{1,0:T(8,128)(2,1)S(1)} %get-tuple-element.203.refs_1_.gh), custom_call_target="tpu_custom_call" | custom-call | flops 72477573120 | bytes 283115520 | tf_op jit(solution)/shard_map/pallas_call | solution.py:273
  137.2 8.4 %collective-permute-done.23.refs_3_ = bf16[8,96,384]{2,1,0:T(8,128)(2,1)S(1)} collective-permute-done((bf16[8,96,384]{2,1,0:T(8,128)(2,1)S(1)}, bf16[8,96,384]{2,1,0:T(8,128)(2,1)S(1)}, u32[]{:S(2)}, u32[]{:S(2)}) %collective-permute-start.23) | collective-permute-done | bytes 589856 | tf_op jit(solution)/shard_map/ppermute | solution.py:37
  149.7 6.7 %shard_map.344 = (f32[512,768]{1,0:T(8,128)S(1)}, bf16[512,768]{1,0:T(8,128)(2,1)S(1)}, bf16[512,768]{1,0:T(8,128)(2,1)S(1)}, f32[1,768]{1,0:T(1,128)S(1)}, f32[1,768]{1,0:T(1,128)S(1)}, /*index=5*/f32[1,768]{1,0:T(1,128)S(1)}) custom-call(s32[2]{0:T(128)S(1)} %pad_add_fusion.at, bf16[512,3072]{1,0:T(8,128)(2,1)S(1)} %get-tuple-element.203.refs_1_.gh, ...), custom_call_target="tpu_custom_call" | custom-call | flops 90596966400 | bytes 141557760 | tf_op jit(solution)/shard_map/pallas_call | solution.py:640
  161.7 10.8 %shard_map.347 = (bf16[512,768]{1,0:T(8,128)(2,1)S(1)}, bf16[512,768]{1,0:T(8,128)(2,1)S(1)}, bf16[512,768]{1,0:T(8,128)(2,1)S(1)}, f32[1,768]{1,0:T(1,128)S(1)}, f32[1,768]{1,0:T(1,128)S(1)}) custom-call(s32[2]{0:T(128)S(1)} %pad_add_fusion.at, bf16[512,768]{1,0:T(8,128)(2,1)S(1)} %copy-done.28, bf16[512,768]{1,0:T(8,128)(2,1)S(1)} %copy-done.30, ...), custom_call_target="tpu_custom_call" | custom-call | flops 60397977600 | bytes 165150720 | tf_op jit(solution)/shard_map/pallas_call | solution.py:430
  177.2 4.7 %shard_map.350 = (bf16[2,16,24,1536]{3,2,1,0:T(8,128)(2,1)S(1)}, bf16[2,16,24,1536]{3,2,1,0:T(8,128)(2,1)S(1)}) custom-call(s32[2]{0:T(128)S(1)} %pad_add_fusion.at, bf16[512,768]{1,0:T(8,128)(2,1)S(1)} %copy-done.1, bf16[512,768]{1,0:T(8,128)(2,1)S(1)} %copy-done.26, bf16[512,768]{1,0:T(8,128)(2,1)S(1)} %get-tuple-element.242.refs_2_.dq, ...), custom_call_target="tpu_custom_call" | custom-call | flops 72477573120 | bytes 283115520 | tf_op jit(solution)/shard_map/pallas_call | solution.py:273
  183.9 3.7 %shard_map.352 = (bf16[512,768]{1,0:T(8,128)(2,1)}, f32[1,768]{1,0:T(1,128)S(1)}) custom-call(s32[2]{0:T(128)S(1)} %pad_add_fusion.at, f32[512,768]{1,0:T(8,128)S(1)} %get-tuple-element.206.first, bf16[512,768]{1,0:T(8,128)(2,1)S(1)} %get-tuple-element.242.refs_2_.dq, bf16[512,768]{1,0:T(8,128)(2,1)S(1)} %get-tuple-element.233.refs_3_.dk, ...), custom_call_target="tpu_custom_call" | custom-call | flops 54358179840 | bytes 106168320 | tf_op jit(solution)/shard_map/pallas_call | solution.py:670
  192.9 6.7 %collective-permute-done.34.refs_1_ = bf16[2,24,3072]{2,1,0:T(8,128)(2,1)S(1)} collective-permute-done((bf16[2,24,3072]{2,1,0:T(8,128)(2,1)S(1)}, bf16[2,24,3072]{2,1,0:T(8,128)(2,1)S(1)}, u32[]{:S(2)}, u32[]{:S(2)}) %collective-permute-start.34) | collective-permute-done | bytes 294944 | tf_op jit(solution)/shard_map/ppermute | solution.py:37
  203.9 3.2 %collective-permute-done.36 = f32[16,768]{1,0:T(8,128)S(1)} collective-permute-done((f32[16,768]{1,0:T(8,128)S(1)}, f32[16,768]{1,0:T(8,128)S(1)}, u32[]{:S(2)}, u32[]{:S(2)}) %collective-permute-start.36) | collective-permute-done | bytes 49184 | tf_op jit(solution)/shard_map/ppermute | solution.py:37
  207.0 1.8 collective-permute-done.37
  213.3 4.9 %collective-permute-done.40 = f32[16,768]{1,0:T(8,128)S(1)} collective-permute-done((f32[16,768]{1,0:T(8,128)S(1)}, f32[16,768]{1,0:T(8,128)S(1)}, u32[]{:S(2)}, u32[]{:S(2)}) %collective-permute-start.40) | collective-permute-done | bytes 49184 | tf_op jit(solution)/shard_map/ppermute | solution.py:37
  220.5 2.4 %collective-permute-start.43 = (f32[16,768]{1,0:T(8,128)S(1)}, f32[16,768]{1,0:T(8,128)S(1)}, u32[]{:S(2)}, u32[]{:S(2)}) collective-permute-start(f32[16,768]{1,0:T(8,128)S(1)} %add.50), channel_id=1, source_target_pairs={{0,16},{2,18},{4,20},{6,22},{8,24},{10,26},{12,28},{14,30},{16,0},... | collective-permute-start | bytes 147464 | tf_op jit(solution)/shard_map/ppermute | solution.py:37
  223.7 2.5 %collective-permute-done.43 = f32[16,768]{1,0:T(8,128)S(1)} collective-permute-done((f32[16,768]{1,0:T(8,128)S(1)}, f32[16,768]{1,0:T(8,128)S(1)}, u32[]{:S(2)}, u32[]{:S(2)}) %collective-permute-start.43) | collective-permute-done | bytes 49184 | tf_op jit(solution)/shard_map/ppermute | solution.py:37
  227.6 2.7 %collective-permute-start.44 = (bf16[1,24,3072]{2,1,0:T(8,128)(2,1)S(1)}, bf16[1,24,3072]{2,1,0:T(8,128)(2,1)S(1)}, u32[]{:S(2)}, u32[]{:S(2)}) collective-permute-start(bf16[1,24,3072]{2,1,0:T(8,128)(2,1)S(1)} %get-tuple-element.281), channel_id=1, source_target_pairs={{0,16},{2,18},{4,20},{6,22},{8,24},{10,26},{12,28},{14,30},{16,0},... | collective-permute-start | bytes 442376 | tf_op jit(solution)/shard_map/ppermute | solution.py:37
  232.5 1.9 collective-permute-done.46
  (244 shorter events, 82.5 us)
Async XLA Ops:
  3.7 9.6 %collective-permute-start = (bf16[1,24,2304]{2,1,0:T(8,128)(2,1)S(1)}, bf16[1,24,2304]{2,1,0:T(8,128)(2,1)S(1)}, u32[]{:S(2)}, u32[]{:S(2)}) collective-permute-start(bf16[1,24,2304]{2,1,0:T(8,128)(2,1)S(1)} %bitcast.39), channel_id=1, source_target_pairs={{0,16},{2,18},{4,20},{6,22},{8,24},{10,26},{12,28},{14,30},{16,0},... | collective-permute-start | bytes 331784 | tf_op jit(solution)/shard_map/ppermute | solution.py:37
  13.3 10.6 %collective-permute-start.2 = (bf16[2,24,2304]{2,1,0:T(8,128)(2,1)S(1)}, bf16[2,24,2304]{2,1,0:T(8,128)(2,1)S(1)}, u32[]{:S(2)}, u32[]{:S(2)}) collective-permute-start(bf16[2,24,2304]{2,1,0:T(8,128)(2,1)S(1)} %pad_maximum_fusion.7), channel_id=1, source_target_pairs={{0,8},{2,10},{4,12},{6,14},{8,0},{10,2},{12,4},{14,6},{16,24},{18,... | collective-permute-start | bytes 663560 | tf_op jit(solution)/shard_map/ppermute | solution.py:37
  14.6 12.2 %collective-permute-start.1 = (bf16[1,24,3840]{2,1,0:T(8,128)(2,1)S(1)}, bf16[1,24,3840]{2,1,0:T(8,128)(2,1)S(1)}, u32[]{:S(2)}, u32[]{:S(2)}) collective-permute-start(bf16[1,24,3840]{2,1,0:T(8,128)(2,1)S(1)} %bitcast.42), channel_id=1, source_target_pairs={{0,16},{2,18},{4,20},{6,22},{8,24},{10,26},{12,28},{14,30},{16,0},... | collective-permute-start | bytes 552968 | tf_op jit(solution)/shard_map/ppermute | solution.py:37
  25.3 8.2 %collective-permute-start.5 = (bf16[4,24,1152]{2,1,0:T(8,128)(2,1)S(1)}, bf16[4,24,1152]{2,1,0:T(8,128)(2,1)S(1)}, u32[]{:S(2)}, u32[]{:S(2)}) collective-permute-start(bf16[4,24,1152]{2,1,0:T(8,128)(2,1)S(1)} %get-tuple-element.301), channel_id=1, source_target_pairs={{0,2},{2,0},{4,6},{6,4},{8,10},{10,8},{12,14},{14,12},{16,18},{18,... | collective-permute-start | bytes 663560 | tf_op jit(solution)/shard_map/ppermute | solution.py:37
  26.9 8.5 %collective-permute-start.3 = (bf16[2,24,3840]{2,1,0:T(8,128)(2,1)S(1)}, bf16[2,24,3840]{2,1,0:T(8,128)(2,1)S(1)}, u32[]{:S(2)}, u32[]{:S(2)}) collective-permute-start(bf16[2,24,3840]{2,1,0:T(8,128)(2,1)S(1)} %pad_maximum_fusion.6), channel_id=1, source_target_pairs={{0,8},{2,10},{4,12},{6,14},{8,0},{10,2},{12,4},{14,6},{16,24},{18,... | collective-permute-start | bytes 1105928 | tf_op jit(solution)/shard_map/ppermute | solution.py:37
  30.0 10.7 %collective-permute-start.6 = (bf16[8,24,1152]{2,1,0:T(8,128)(2,1)S(1)}, bf16[8,24,1152]{2,1,0:T(8,128)(2,1)S(1)}, u32[]{:S(2)}, u32[]{:S(2)}) collective-permute-start(bf16[8,24,1152]{2,1,0:T(8,128)(2,1)S(1)} %pad_maximum_fusion.4), channel_id=1, source_target_pairs={{0,2},{2,0},{4,6},{6,4},{8,10},{10,8},{12,14},{14,12},{16,18},{18,... | collective-permute-start | bytes 1327112 | tf_op jit(solution)/shard_map/ppermute | solution.py:37
  33.5 8.4 %collective-permute-start.7 = (bf16[8,24,1152]{2,1,0:T(8,128)(2,1)S(1)}, bf16[8,24,1152]{2,1,0:T(8,128)(2,1)S(1)}, u32[]{:S(2)}, u32[]{:S(2)}) collective-permute-start(bf16[8,24,1152]{2,1,0:T(8,128)(2,1)S(1)} %pad_maximum_fusion.5), channel_id=1, source_target_pairs={{0,4},{2,6},{4,0},{6,2},{8,12},{10,14},{12,8},{14,10},{16,20},{18,... | collective-permute-start | bytes 1327112 | tf_op jit(solution)/shard_map/ppermute | solution.py:37
  42.2 15.7 %collective-permute-start.11 = (bf16[2,16,24,1152]{3,2,1,0:T(8,128)(2,1)S(1)}, bf16[2,16,24,1152]{3,2,1,0:T(8,128)(2,1)S(1)}, u32[]{:S(2)}, u32[]{:S(2)}) collective-permute-start(bf16[2,16,24,1152]{3,2,1,0:T(8,128)(2,1)S(1)} %pad_maximum_fusion.2.own), channel_id=1, source_target_pairs={{0,1},{1,0},{2,3},{3,2},{4,5},{5,4},{6,7},{7,6},{8,9},{9,8},{10,11... | collective-permute-start | bytes 5308424 | tf_op jit(solution)/shard_map/ppermute | solution.py:40
  43.1 12.2 %collective-permute-start.10 = (bf16[1,96,768]{2,1,0:T(8,128)(2,1)S(1)}, bf16[1,96,768]{2,1,0:T(8,128)(2,1)S(1)}, u32[]{:S(2)}, u32[]{:S(2)}) collective-permute-start(bf16[1,96,768]{2,1,0:T(8,128)(2,1)S(1)} %bitcast.57), channel_id=1, source_target_pairs={{0,16},{2,18},{4,20},{6,22},{8,24},{10,26},{12,28},{14,30},{16,0},... | collective-permute-start | bytes 442376 | tf_op jit(solution)/shard_map/ppermute | solution.py:37
  44.3 10.1 %collective-permute-start.9 = (bf16[4,24,1920]{2,1,0:T(8,128)(2,1)S(1)}, bf16[4,24,1920]{2,1,0:T(8,128)(2,1)S(1)}, u32[]{:S(2)}, u32[]{:S(2)}) collective-permute-start(bf16[4,24,1920]{2,1,0:T(8,128)(2,1)S(1)} %get-tuple-element.158), channel_id=1, source_target_pairs={{0,2},{2,0},{4,6},{6,4},{8,10},{10,8},{12,14},{14,12},{16,18},{18,... | collective-permute-start | bytes 1105928 | tf_op jit(solution)/shard_map/ppermute | solution.py:37
  45.5 9.8 %collective-permute-start.8 = (bf16[4,24,1920]{2,1,0:T(8,128)(2,1)S(1)}, bf16[4,24,1920]{2,1,0:T(8,128)(2,1)S(1)}, u32[]{:S(2)}, u32[]{:S(2)}) collective-permute-start(bf16[4,24,1920]{2,1,0:T(8,128)(2,1)S(1)} %get-tuple-element.157), channel_id=1, source_target_pairs={{0,4},{2,6},{4,0},{6,2},{8,12},{10,14},{12,8},{14,10},{16,20},{18,... | collective-permute-start | bytes 1105928 | tf_op jit(solution)/shard_map/ppermute | solution.py:37
  55.3 18.9 %collective-permute-start.12 = (bf16[2,96,768]{2,1,0:T(8,128)(2,1)S(1)}, bf16[2,96,768]{2,1,0:T(8,128)(2,1)S(1)}, u32[]{:S(2)}, u32[]{:S(2)}) collective-permute-start(bf16[2,96,768]{2,1,0:T(8,128)(2,1)S(1)} %constant_dynamic-update-slice_fusion.6), channel_id=1, source_target_pairs={{0,8},{2,10},{4,12},{6,14},{8,0},{10,2},{12,4},{14,6},{16,24},{18,... | collective-permute-start | bytes 884744 | tf_op jit(solution)/shard_map/ppermute | solution.py:37
  57.9 16.6 %collective-permute-start.14 = (bf16[8,24,1920]{2,1,0:T(8,128)(2,1)S(1)}, bf16[8,24,1920]{2,1,0:T(8,128)(2,1)S(1)}, u32[]{:S(2)}, u32[]{:S(2)}) collective-permute-start(bf16[8,24,1920]{2,1,0:T(8,128)(2,1)S(1)} %constant_dynamic-update-slice_fusion.4), channel_id=1, source_target_pairs={{0,4},{2,6},{4,0},{6,2},{8,12},{10,14},{12,8},{14,10},{16,20},{18,... | collective-permute-start | bytes 2211848 | tf_op jit(solution)/shard_map/ppermute | solution.py:37
  58.9 16.3 %collective-permute-start.13 = (bf16[8,24,1920]{2,1,0:T(8,128)(2,1)S(1)}, bf16[8,24,1920]{2,1,0:T(8,128)(2,1)S(1)}, u32[]{:S(2)}, u32[]{:S(2)}) collective-permute-start(bf16[8,24,1920]{2,1,0:T(8,128)(2,1)S(1)} %constant_dynamic-update-slice_fusion.2), channel_id=1, source_target_pairs={{0,2},{2,0},{4,6},{6,4},{8,10},{10,8},{12,14},{14,12},{16,18},{18,... | collective-permute-start | bytes 2211848 | tf_op jit(solution)/shard_map/ppermute | solution.py:37
  75.8 9.5 %collective-permute-start.16 = (bf16[2,16,24,1920]{3,2,1,0:T(8,128)(2,1)S(1)}, bf16[2,16,24,1920]{3,2,1,0:T(8,128)(2,1)S(1)}, u32[]{:S(2)}, u32[]{:S(2)}) collective-permute-start(bf16[2,16,24,1920]{3,2,1,0:T(8,128)(2,1)S(1)} %pad_maximum_fusion.own), channel_id=1, source_target_pairs={{0,1},{1,0},{2,3},{3,2},{4,5},{5,4},{6,7},{7,6},{8,9},{9,8},{10,11... | collective-permute-start | bytes 8847368 | tf_op jit(solution)/shard_map/ppermute | solution.py:40
  75.9 9.4 %collective-permute-start.17 = (bf16[4,96,384]{2,1,0:T(8,128)(2,1)S(1)}, bf16[4,96,384]{2,1,0:T(8,128)(2,1)S(1)}, u32[]{:S(2)}, u32[]{:S(2)}) collective-permute-start(bf16[4,96,384]{2,1,0:T(8,128)(2,1)S(1)} %get-tuple-element.175), channel_id=1, source_target_pairs={{0,2},{2,0},{4,6},{6,4},{8,10},{10,8},{12,14},{14,12},{16,18},{18,... | collective-permute-start | bytes 884744 | tf_op jit(solution)/shard_map/ppermute | solution.py:37
  77.4 9.1 %collective-permute-start.15 = (bf16[4,96,384]{2,1,0:T(8,128)(2,1)S(1)}, bf16[4,96,384]{2,1,0:T(8,128)(2,1)S(1)}, u32[]{:S(2)}, u32[]{:S(2)}) collective-permute-start(bf16[4,96,384]{2,1,0:T(8,128)(2,1)S(1)} %get-tuple-element.172), channel_id=1, source_target_pairs={{0,4},{2,6},{4,0},{6,2},{8,12},{10,14},{12,8},{14,10},{16,20},{18,... | collective-permute-start | bytes 884744 | tf_op jit(solution)/shard_map/ppermute | solution.py:37
  86.5 15.1 %collective-permute-start.18 = (bf16[8,96,384]{2,1,0:T(8,128)(2,1)S(1)}, bf16[8,96,384]{2,1,0:T(8,128)(2,1)S(1)}, u32[]{:S(2)}, u32[]{:S(2)}) collective-permute-start(bf16[8,96,384]{2,1,0:T(8,128)(2,1)S(1)} %constant_dynamic-update-slice_fusion.10), channel_id=1, source_target_pairs={{0,2},{2,0},{4,6},{6,4},{8,10},{10,8},{12,14},{14,12},{16,18},{18,... | collective-permute-start | bytes 1769480 | tf_op jit(solution)/shard_map/ppermute | solution.py:37
  87.3 14.5 %collective-permute-start.19 = (bf16[8,96,384]{2,1,0:T(8,128)(2,1)S(1)}, bf16[8,96,384]{2,1,0:T(8,128)(2,1)S(1)}, u32[]{:S(2)}, u32[]{:S(2)}) collective-permute-start(bf16[8,96,384]{2,1,0:T(8,128)(2,1)S(1)} %constant_dynamic-update-slice_fusion.12), channel_id=1, source_target_pairs={{0,4},{2,6},{4,0},{6,2},{8,12},{10,14},{12,8},{14,10},{16,20},{18,... | collective-permute-start | bytes 1769480 | tf_op jit(solution)/shard_map/ppermute | solution.py:37
  130.0 15.7 %collective-permute-start.23 = (bf16[8,96,384]{2,1,0:T(8,128)(2,1)S(1)}, bf16[8,96,384]{2,1,0:T(8,128)(2,1)S(1)}, u32[]{:S(2)}, u32[]{:S(2)}) collective-permute-start(bf16[8,96,384]{2,1,0:T(8,128)(2,1)S(1)} %get-tuple-element.194), channel_id=1, source_target_pairs={{0,4},{2,6},{4,0},{6,2},{8,12},{10,14},{12,8},{14,10},{16,20},{18,... | collective-permute-start | bytes 1769480 | tf_op jit(solution)/shard_map/ppermute | solution.py:37
  131.1 15.3 %collective-permute-start.22 = (bf16[8,96,384]{2,1,0:T(8,128)(2,1)S(1)}, bf16[8,96,384]{2,1,0:T(8,128)(2,1)S(1)}, u32[]{:S(2)}, u32[]{:S(2)}) collective-permute-start(bf16[8,96,384]{2,1,0:T(8,128)(2,1)S(1)} %get-tuple-element.193), channel_id=1, source_target_pairs={{0,2},{2,0},{4,6},{6,4},{8,10},{10,8},{12,14},{14,12},{16,18},{18,... | collective-permute-start | bytes 1769480 | tf_op jit(solution)/shard_map/ppermute | solution.py:37
  137.1 21.2 %collective-permute-start.26 = (bf16[2,16,24,1536]{3,2,1,0:T(8,128)(2,1)S(1)}, bf16[2,16,24,1536]{3,2,1,0:T(8,128)(2,1)S(1)}, u32[]{:S(2)}, u32[]{:S(2)}) collective-permute-start(bf16[2,16,24,1536]{3,2,1,0:T(8,128)(2,1)S(1)} %get-tuple-element.196), channel_id=1, source_target_pairs={{0,1},{1,0},{2,3},{3,2},{4,5},{5,4},{6,7},{7,6},{8,9},{9,8},{10,11... | collective-permute-start | bytes 7077896 | tf_op jit(solution)/shard_map/ppermute | solution.py:40
  147.7 8.7 %collective-permute-start.25 = (bf16[4,96,384]{2,1,0:T(8,128)(2,1)S(1)}, bf16[4,96,384]{2,1,0:T(8,128)(2,1)S(1)}, u32[]{:S(2)}, u32[]{:S(2)}) collective-permute-start(bf16[4,96,384]{2,1,0:T(8,128)(2,1)S(1)} %get-tuple-element.202), channel_id=1, source_target_pairs={{0,2},{2,0},{4,6},{6,4},{8,10},{10,8},{12,14},{14,12},{16,18},{18,... | collective-permute-start | bytes 884744 | tf_op jit(solution)/shard_map/ppermute | solution.py:37
  158.0 14.5 %collective-permute-start.27 = (bf16[2,96,768]{2,1,0:T(8,128)(2,1)S(1)}, bf16[2,96,768]{2,1,0:T(8,128)(2,1)S(1)}, u32[]{:S(2)}, u32[]{:S(2)}) collective-permute-start(bf16[2,96,768]{2,1,0:T(8,128)(2,1)S(1)} %get-tuple-element.215), channel_id=1, source_target_pairs={{0,8},{2,10},{4,12},{6,14},{8,0},{10,2},{12,4},{14,6},{16,24},{18,... | collective-permute-start | bytes 884744 | tf_op jit(solution)/shard_map/ppermute | solution.py:37
  160.0 13.3 %collective-permute-start.29 = (bf16[8,24,1536]{2,1,0:T(8,128)(2,1)S(1)}, bf16[8,24,1536]{2,1,0:T(8,128)(2,1)S(1)}, u32[]{:S(2)}, u32[]{:S(2)}) collective-permute-start(bf16[8,24,1536]{2,1,0:T(8,128)(2,1)S(1)} %get-tuple-element.219), channel_id=1, source_target_pairs={{0,4},{2,6},{4,0},{6,2},{8,12},{10,14},{12,8},{14,10},{16,20},{18,... | collective-permute-start | bytes 1769480 | tf_op jit(solution)/shard_map/ppermute | solution.py:37
  161.0 13.4 %collective-permute-start.28 = (bf16[8,24,1536]{2,1,0:T(8,128)(2,1)S(1)}, bf16[8,24,1536]{2,1,0:T(8,128)(2,1)S(1)}, u32[]{:S(2)}, u32[]{:S(2)}) collective-permute-start(bf16[8,24,1536]{2,1,0:T(8,128)(2,1)S(1)} %get-tuple-element.218), channel_id=1, source_target_pairs={{0,2},{2,0},{4,6},{6,4},{8,10},{10,8},{12,14},{14,12},{16,18},{18,... | collective-permute-start | bytes 1769480 | tf_op jit(solution)/shard_map/ppermute | solution.py:37
  189.2 19.7 %collective-permute-start.38 = (bf16[8,24,1536]{2,1,0:T(8,128)(2,1)S(1)}, bf16[8,24,1536]{2,1,0:T(8,128)(2,1)S(1)}, u32[]{:S(2)}, u32[]{:S(2)}) collective-permute-start(bf16[8,24,1536]{2,1,0:T(8,128)(2,1)S(1)} %get-tuple-element.252), channel_id=1, source_target_pairs={{0,4},{2,6},{4,0},{6,2},{8,12},{10,14},{12,8},{14,10},{16,20},{18,... | collective-permute-start | bytes 1769480 | tf_op jit(solution)/shard_map/ppermute | solution.py:37
  190.3 18.6 %collective-permute-start.33 = (bf16[8,24,1536]{2,1,0:T(8,128)(2,1)S(1)}, bf16[8,24,1536]{2,1,0:T(8,128)(2,1)S(1)}, u32[]{:S(2)}, u32[]{:S(2)}) collective-permute-start(bf16[8,24,1536]{2,1,0:T(8,128)(2,1)S(1)} %get-tuple-element.249), channel_id=1, source_target_pairs={{0,2},{2,0},{4,6},{6,4},{8,10},{10,8},{12,14},{14,12},{16,18},{18,... | collective-permute-start | bytes 1769480 | tf_op jit(solution)/shard_map/ppermute | solution.py:37
  191.2 8.4 %collective-permute-start.34 = (bf16[2,24,3072]{2,1,0:T(8,128)(2,1)S(1)}, bf16[2,24,3072]{2,1,0:T(8,128)(2,1)S(1)}, u32[]{:S(2)}, u32[]{:S(2)}) collective-permute-start(bf16[2,24,3072]{2,1,0:T(8,128)(2,1)S(1)} %get-tuple-element.241), channel_id=1, source_target_pairs={{0,8},{2,10},{4,12},{6,14},{8,0},{10,2},{12,4},{14,6},{16,24},{18,... | collective-permute-start | bytes 884744 | tf_op jit(solution)/shard_map/ppermute | solution.py:37
  200.4 8.5 %collective-permute-start.37 = (bf16[1,24,3072]{2,1,0:T(8,128)(2,1)S(1)}, bf16[1,24,3072]{2,1,0:T(8,128)(2,1)S(1)}, u32[]{:S(2)}, u32[]{:S(2)}) collective-permute-start(bf16[1,24,3072]{2,1,0:T(8,128)(2,1)S(1)} %get-tuple-element.266), channel_id=1, source_target_pairs={{0,16},{2,18},{4,20},{6,22},{8,24},{10,26},{12,28},{14,30},{16,0},... | collective-permute-start | bytes 442376 | tf_op jit(solution)/shard_map/ppermute | solution.py:37
  210.0 8.1 %collective-permute-start.41 = (bf16[4,24,1536]{2,1,0:T(8,128)(2,1)S(1)}, bf16[4,24,1536]{2,1,0:T(8,128)(2,1)S(1)}, u32[]{:S(2)}, u32[]{:S(2)}) collective-permute-start(bf16[4,24,1536]{2,1,0:T(8,128)(2,1)S(1)} %get-tuple-element.272), channel_id=1, source_target_pairs={{0,2},{2,0},{4,6},{6,4},{8,10},{10,8},{12,14},{14,12},{16,18},{18,... | collective-permute-start | bytes 884744 | tf_op jit(solution)/shard_map/ppermute | solution.py:37
  211.3 9.2 %collective-permute-start.45 = (bf16[1,96,768]{2,1,0:T(8,128)(2,1)S(1)}, bf16[1,96,768]{2,1,0:T(8,128)(2,1)S(1)}, u32[]{:S(2)}, u32[]{:S(2)}) collective-permute-start(bf16[1,96,768]{2,1,0:T(8,128)(2,1)S(1)} %get-tuple-element.225), channel_id=1, source_target_pairs={{0,16},{2,18},{4,20},{6,22},{8,24},{10,26},{12,28},{14,30},{16,0},... | collective-permute-start | bytes 442376 | tf_op jit(solution)/shard_map/ppermute | solution.py:37
  (63 other events, 459.6 us)

commit v5 on v4

--- a/solution.py
+++ b/solution.py
@@ -374,7 +374,7 @@
         (seqs, groups),
         [pl.BlockSpec((length, width), lambda s, g, at: (s, 0)), weight, weight, weight, bias, bias],
         [block] * 4 + [pl.BlockSpec((1, 1, 4, length), lambda s, g, at: (s, g, 0, 0))],
-        [table] * 4 + [jax.ShapeDtypeStruct((seqs, groups, 4, length), jnp.float32)],
+        [pltpu.HBM(table.shape, LOW)] * 3 + [table, jax.ShapeDtypeStruct((seqs, groups, 4, length), jnp.float32)],
         (6 * rows * width * width, 6 * width * width, seqs * groups * 4 * length * length),
     )(place.where, start, *weights, query_bias, value_bias)
 

time: 237 us -> 237 us (level)
  local copies, waits for them, and re-layouts: 13.5 us -> 10.8 us
    unnamed x103 -> x97, local copies, waits for them, and re-layouts: 10.8 us -> 8.15 us
  transfers between devices with their start and end apart: 47 -> 47, of which waited for: 28 -> 28; matrix products, arithmetic and copies ran while one was open for 3% -> 3% of each run, Pallas kernels for 27% -> 28%
where the time goes in v5:
time: 237 us; the launch traced here: 236 us
  Pallas kernels  87.1 us (37%)
  waiting for transfers between devices  79.4 us (34%)
  starting transfers between devices  50.7 us (21%)
  local copies, waits for them, and re-layouts  10.8 us (5%)
  other arithmetic  6.69 us (3%)
    ppermute x40, waiting for transfers between devices, swap(): lax.ppermute(value, 'dp', [(i, i ^ stride) for i in range(self.chips)])  74.2 us
    ppermute x40, starting transfers between devices, swap(): lax.ppermute(value, 'dp', [(i, i ^ stride) for i in range(self.chips)])  50.1 us
    pallas_call x12, Pallas kernels, fold(): kernel_call(body, (steps,), [ins] * (2 * len(keeps)), [pl.BlockSpec((chip...  13.7 us
    pallas_call x1, Pallas kernels, attention_backward(): kernel_call(body, (groups, seqs), [block] * 4 + [pl.BlockSpec((1, 1, 4, l...  10.8 us
    pallas_call x1, Pallas kernels, attention_forward(): kernel_call(body, (seqs, groups), [pl.BlockSpec((length, width), lambda s...  10.4 us
    pallas_call x2, Pallas kernels, weight_terms(): kernel_call(body, (count,), [pl.BlockSpec((length, features), lambda t, a...  9.3 us
    pallas_call x1, Pallas kernels, feed_in(): kernel_call(body, (inner // tile,), [keep(a) for a in ins] + [pl.BlockSpe...  9.12 us
    unnamed x97, local copies, waits for them, and re-layouts  8.15 us
  transfers between devices with their start and end apart: 47, of which 28 were waited for; matrix products, arithmetic and copies ran while one was open for 3% of the time, Pallas kernels for 28%

profile of v5, /device:TPU:0, one launch (start us, length us, event | category | flops | bytes accessed | tf_op | source)
XLA Modules:
  0.0 236.5 jit_solution(17286312499509758430)
XLA Ops:
  3.7 4.1 %collective-permute-start = (bf16[1,24,2304]{2,1,0:T(8,128)(2,1)S(1)}, bf16[1,24,2304]{2,1,0:T(8,128)(2,1)S(1)}, u32[]{:S(2)}, u32[]{:S(2)}) collective-permute-start(bf16[1,24,2304]{2,1,0:T(8,128)(2,1)S(1)} %bitcast.39), channel_id=1, source_target_pairs={{0,16},{2,18},{4,20},{6,22},{8,24},{10,26},{12,28},{14,30},{16,0},... | collective-permute-start | bytes 331784 | tf_op jit(solution)/shard_map/ppermute | solution.py:37
  11.3 2.0 collective-permute-done
  14.6 3.4 %collective-permute-start.1 = (bf16[1,24,3840]{2,1,0:T(8,128)(2,1)S(1)}, bf16[1,24,3840]{2,1,0:T(8,128)(2,1)S(1)}, u32[]{:S(2)}, u32[]{:S(2)}) collective-permute-start(bf16[1,24,3840]{2,1,0:T(8,128)(2,1)S(1)} %bitcast.42), channel_id=1, source_target_pairs={{0,16},{2,18},{4,20},{6,22},{8,24},{10,26},{12,28},{14,30},{16,0},... | collective-permute-start | bytes 552968 | tf_op jit(solution)/shard_map/ppermute | solution.py:37
  18.0 5.8 %collective-permute-done.2 = bf16[2,24,2304]{2,1,0:T(8,128)(2,1)S(1)} collective-permute-done((bf16[2,24,2304]{2,1,0:T(8,128)(2,1)S(1)}, bf16[2,24,2304]{2,1,0:T(8,128)(2,1)S(1)}, u32[]{:S(2)}, u32[]{:S(2)}) %collective-permute-start.2) | collective-permute-done | bytes 221216 | tf_op jit(solution)/shard_map/ppermute | solution.py:37
  27.2 2.7 %collective-permute-done.4 = bf16[4,24,1152]{2,1,0:T(8,128)(2,1)S(1)} collective-permute-done((bf16[4,24,1152]{2,1,0:T(8,128)(2,1)S(1)}, bf16[4,24,1152]{2,1,0:T(8,128)(2,1)S(1)}, u32[]{:S(2)}, u32[]{:S(2)}) %collective-permute-start.4) | collective-permute-done | bytes 221216 | tf_op jit(solution)/shard_map/ppermute | solution.py:37
  35.3 5.4 %collective-permute-done.6 = bf16[8,24,1152]{2,1,0:T(8,128)(2,1)S(1)} collective-permute-done((bf16[8,24,1152]{2,1,0:T(8,128)(2,1)S(1)}, bf16[8,24,1152]{2,1,0:T(8,128)(2,1)S(1)}, u32[]{:S(2)}, u32[]{:S(2)}) %collective-permute-start.6) | collective-permute-done | bytes 442400 | tf_op jit(solution)/shard_map/ppermute | solution.py:37
  46.5 7.9 %collective-permute-done.9 = bf16[4,24,1920]{2,1,0:T(8,128)(2,1)S(1)} collective-permute-done((bf16[4,24,1920]{2,1,0:T(8,128)(2,1)S(1)}, bf16[4,24,1920]{2,1,0:T(8,128)(2,1)S(1)}, u32[]{:S(2)}, u32[]{:S(2)}) %collective-permute-start.9) | collective-permute-done | bytes 368672 | tf_op jit(solution)/shard_map/ppermute | solution.py:37
  55.3 2.5 %collective-permute-start.12 = (bf16[2,96,768]{2,1,0:T(8,128)(2,1)S(1)}, bf16[2,96,768]{2,1,0:T(8,128)(2,1)S(1)}, u32[]{:S(2)}, u32[]{:S(2)}) collective-permute-start(bf16[2,96,768]{2,1,0:T(8,128)(2,1)S(1)} %constant_dynamic-update-slice_fusion.6), channel_id=1, source_target_pairs={{0,8},{2,10},{4,12},{6,14},{8,0},{10,2},{12,4},{14,6},{16,24},{18,... | collective-permute-start | bytes 884744 | tf_op jit(solution)/shard_map/ppermute | solution.py:37
  61.7 10.4 %shard_map.334 = (bf16[512,768]{1,0:T(8,128)(2,1)}, bf16[512,768]{1,0:T(8,128)(2,1)}, bf16[512,768]{1,0:T(8,128)(2,1)}, bf16[512,768]{1,0:T(8,128)(2,1)S(1)}, f32[1,3,4,512]{3,2,1,0:T(4,128)S(1)}) custom-call(s32[2]{0:T(128)S(1)} %pad_add_fusion.at, bf16[512,768]{1,0:T(8,128)(2,1)S(1)} %broadcast_select_fusion.start.refs_0_, bf16[768,768]{1,0:T(8,128)(2,1)S(1)} %bitcast.48, ...), custom_call_target="tpu_custom_call" | custom-call | flops 54358179840 | bytes 106168320 | tf_op jit(solution)/shard_map/pallas_call | solution.py:372
  72.2 2.3 collective-permute-done.14
  78.0 7.3 %collective-permute-done.17 = bf16[4,96,384]{2,1,0:T(8,128)(2,1)S(1)} collective-permute-done((bf16[4,96,384]{2,1,0:T(8,128)(2,1)S(1)}, bf16[4,96,384]{2,1,0:T(8,128)(2,1)S(1)}, u32[]{:S(2)}, u32[]{:S(2)}) %collective-permute-start.17) | collective-permute-done | bytes 294944 | tf_op jit(solution)/shard_map/ppermute | solution.py:37
  89.6 9.1 %shard_map.336 = (f32[512,768]{1,0:T(8,128)S(1)}, f32[512,1]{1,0:T(8,128)S(1)}, bf16[512,768]{1,0:T(8,128)(2,1)S(1)}, bf16[512,3072]{1,0:T(8,128)(2,1)S(1)}, bf16[512,3072]{1,0:T(8,128)(2,1)S(1)}) custom-call(s32[2]{0:T(128)S(1)} %pad_add_fusion.at, bf16[512,768]{1,0:T(8,128)(2,1)S(1)} %broadcast_select_fusion.start.refs_0_, ...), custom_call_target="tpu_custom_call" | custom-call | flops 90596966400 | bytes 141557760 | tf_op jit(solution)/shard_map/pallas_call | solution.py:495
  104.5 4.0 %collective-permute-done.20.other = bf16[2,16,96,384]{3,2,1,0:T(8,128)(2,1)} collective-permute-done((bf16[2,16,96,384]{3,2,1,0:T(8,128)(2,1)S(1)}, bf16[2,16,96,384]{3,2,1,0:T(8,128)(2,1)}, u32[]{:S(2)}, u32[]{:S(2)}) %collective-permute-start.20) | collective-permute-done | bytes 2359328 | tf_op jit(solution)/shard_map/ppermute | solution.py:40
  108.5 2.9 %shard_map.337 = bf16[32,96,768]{2,1,0:T(8,128)(2,1)S(1)} custom-call(s32[2]{0:T(128)S(1)} %pad_add_fusion.at, bf16[2,16,96,384]{3,2,1,0:T(8,128)(2,1)S(1)} %pad_maximum_fusion.1.own, bf16[2,16,96,384]{3,2,1,0:T(8,128)(2,1)} %collective-permute-done.20.other), custom_call_target="tpu_custom_call" | custom-call | bytes 9437184 | tf_op jit(solution)/shard_map/pallas_call | solution.py:140
  111.4 7.1 %shard_map.338 = (bf16[512,768]{1,0:T(8,128)(2,1)}, f32[512,768]{1,0:T(8,128)S(1)}, bf16[512,768]{1,0:T(8,128)(2,1)S(1)}, f32[1,768]{1,0:T(1,128)S(1)}, f32[1,768]{1,0:T(1,128)S(1)}, /*index=5*/f32[1,768]{1,0:T(1,128)S(1)}) custom-call(s32[2]{0:T(128)S(1)} %pad_add_fusion.at, bf16[512,3072]{1,0:T(8,128)(2,1)S(1)} %copy-done.19, ...), custom_call_target="tpu_custom_call" | custom-call | flops 72477573120 | bytes 141557760 | tf_op jit(solution)/shard_map/pallas_call | solution.py:551
  118.5 4.7 %shard_map.339 = (bf16[2,16,96,384]{3,2,1,0:T(8,128)(2,1)S(1)}, bf16[2,16,96,384]{3,2,1,0:T(8,128)(2,1)S(1)}) custom-call(s32[2]{0:T(128)S(1)} %pad_add_fusion.at, bf16[512,3072]{1,0:T(8,128)(2,1)S(1)} %copy-done.19, bf16[512,768]{1,0:T(8,128)(2,1)S(1)} %get-tuple-element.187.right_ref.grad), custom_call_target="tpu_custom_call" | custom-call | flops 72477573120 | bytes 283115520 | tf_op jit(solution)/shard_map/pallas_call | solution.py:308
  123.4 4.7 %shard_map.340 = (bf16[512,3072]{1,0:T(8,128)(2,1)S(1)}, f32[1,3072]{1,0:T(1,128)S(1)}) custom-call(s32[2]{0:T(128)S(1)} %pad_add_fusion.at, bf16[512,768]{1,0:T(8,128)(2,1)S(1)} %get-tuple-element.187.right_ref.grad, bf16[3072,768]{1,0:T(8,128)(2,1)S(1)} %bitcast.38, bf16[512,3072]{1,0:T(8,128)(2,1)S(1)} %copy-done.21), custom_call_target="tpu_custom_call" | custom-call | flops 72477573120 | bytes 141557760 | tf_op jit(solution)/shard_map/pallas_call | solution.py:580
  128.1 1.9 shard_map.341
  132.5 4.6 %shard_map.342 = (bf16[2,16,24,1536]{3,2,1,0:T(8,128)(2,1)S(1)}, bf16[2,16,24,1536]{3,2,1,0:T(8,128)(2,1)S(1)}) custom-call(s32[2]{0:T(128)S(1)} %pad_add_fusion.at, bf16[512,768]{1,0:T(8,128)(2,1)S(1)} %copy-done.31, bf16[512,3072]{1,0:T(8,128)(2,1)S(1)} %get-tuple-element.203.refs_1_.gh), custom_call_target="tpu_custom_call" | custom-call | flops 72477573120 | bytes 283115520 | tf_op jit(solution)/shard_map/pallas_call | solution.py:273
  137.2 8.5 %collective-permute-done.23.refs_3_ = bf16[8,96,384]{2,1,0:T(8,128)(2,1)S(1)} collective-permute-done((bf16[8,96,384]{2,1,0:T(8,128)(2,1)S(1)}, bf16[8,96,384]{2,1,0:T(8,128)(2,1)S(1)}, u32[]{:S(2)}, u32[]{:S(2)}) %collective-permute-start.23) | collective-permute-done | bytes 589856 | tf_op jit(solution)/shard_map/ppermute | solution.py:37
  149.7 6.7 %shard_map.344 = (f32[512,768]{1,0:T(8,128)S(1)}, bf16[512,768]{1,0:T(8,128)(2,1)S(1)}, bf16[512,768]{1,0:T(8,128)(2,1)S(1)}, f32[1,768]{1,0:T(1,128)S(1)}, f32[1,768]{1,0:T(1,128)S(1)}, /*index=5*/f32[1,768]{1,0:T(1,128)S(1)}) custom-call(s32[2]{0:T(128)S(1)} %pad_add_fusion.at, bf16[512,3072]{1,0:T(8,128)(2,1)S(1)} %get-tuple-element.203.refs_1_.gh, ...), custom_call_target="tpu_custom_call" | custom-call | flops 90596966400 | bytes 141557760 | tf_op jit(solution)/shard_map/pallas_call | solution.py:640
  161.7 10.8 %shard_map.347 = (bf16[512,768]{1,0:T(8,128)(2,1)S(1)}, bf16[512,768]{1,0:T(8,128)(2,1)S(1)}, bf16[512,768]{1,0:T(8,128)(2,1)S(1)}, f32[1,768]{1,0:T(1,128)S(1)}, f32[1,768]{1,0:T(1,128)S(1)}) custom-call(s32[2]{0:T(128)S(1)} %pad_add_fusion.at, bf16[512,768]{1,0:T(8,128)(2,1)S(1)} %copy-done.27, bf16[512,768]{1,0:T(8,128)(2,1)S(1)} %copy-done.28, ...), custom_call_target="tpu_custom_call" | custom-call | flops 60397977600 | bytes 165150720 | tf_op jit(solution)/shard_map/pallas_call | solution.py:430
  177.3 4.7 %shard_map.350 = (bf16[2,16,24,1536]{3,2,1,0:T(8,128)(2,1)S(1)}, bf16[2,16,24,1536]{3,2,1,0:T(8,128)(2,1)S(1)}) custom-call(s32[2]{0:T(128)S(1)} %pad_add_fusion.at, bf16[512,768]{1,0:T(8,128)(2,1)S(1)} %copy-done.1, bf16[512,768]{1,0:T(8,128)(2,1)S(1)} %copy-done.26, bf16[512,768]{1,0:T(8,128)(2,1)S(1)} %get-tuple-element.242.refs_2_.dq, ...), custom_call_target="tpu_custom_call" | custom-call | flops 72477573120 | bytes 283115520 | tf_op jit(solution)/shard_map/pallas_call | solution.py:273
  183.9 3.7 %shard_map.352 = (bf16[512,768]{1,0:T(8,128)(2,1)}, f32[1,768]{1,0:T(1,128)S(1)}) custom-call(s32[2]{0:T(128)S(1)} %pad_add_fusion.at, f32[512,768]{1,0:T(8,128)S(1)} %get-tuple-element.206.first, bf16[512,768]{1,0:T(8,128)(2,1)S(1)} %get-tuple-element.242.refs_2_.dq, bf16[512,768]{1,0:T(8,128)(2,1)S(1)} %get-tuple-element.233.refs_3_.dk, ...), custom_call_target="tpu_custom_call" | custom-call | flops 54358179840 | bytes 106168320 | tf_op jit(solution)/shard_map/pallas_call | solution.py:670
  193.0 6.7 %collective-permute-done.34.refs_1_ = bf16[2,24,3072]{2,1,0:T(8,128)(2,1)S(1)} collective-permute-done((bf16[2,24,3072]{2,1,0:T(8,128)(2,1)S(1)}, bf16[2,24,3072]{2,1,0:T(8,128)(2,1)S(1)}, u32[]{:S(2)}, u32[]{:S(2)}) %collective-permute-start.34) | collective-permute-done | bytes 294944 | tf_op jit(solution)/shard_map/ppermute | solution.py:37
  203.9 3.2 %collective-permute-done.36 = f32[16,768]{1,0:T(8,128)S(1)} collective-permute-done((f32[16,768]{1,0:T(8,128)S(1)}, f32[16,768]{1,0:T(8,128)S(1)}, u32[]{:S(2)}, u32[]{:S(2)}) %collective-permute-start.36) | collective-permute-done | bytes 49184 | tf_op jit(solution)/shard_map/ppermute | solution.py:37
  207.1 1.8 collective-permute-done.37
  213.3 4.9 %collective-permute-done.40 = f32[16,768]{1,0:T(8,128)S(1)} collective-permute-done((f32[16,768]{1,0:T(8,128)S(1)}, f32[16,768]{1,0:T(8,128)S(1)}, u32[]{:S(2)}, u32[]{:S(2)}) %collective-permute-start.40) | collective-permute-done | bytes 49184 | tf_op jit(solution)/shard_map/ppermute | solution.py:37
  220.5 2.4 %collective-permute-start.43 = (f32[16,768]{1,0:T(8,128)S(1)}, f32[16,768]{1,0:T(8,128)S(1)}, u32[]{:S(2)}, u32[]{:S(2)}) collective-permute-start(f32[16,768]{1,0:T(8,128)S(1)} %add.50), channel_id=1, source_target_pairs={{0,16},{2,18},{4,20},{6,22},{8,24},{10,26},{12,28},{14,30},{16,0},... | collective-permute-start | bytes 147464 | tf_op jit(solution)/shard_map/ppermute | solution.py:37
  223.7 2.5 %collective-permute-done.43 = f32[16,768]{1,0:T(8,128)S(1)} collective-permute-done((f32[16,768]{1,0:T(8,128)S(1)}, f32[16,768]{1,0:T(8,128)S(1)}, u32[]{:S(2)}, u32[]{:S(2)}) %collective-permute-start.43) | collective-permute-done | bytes 49184 | tf_op jit(solution)/shard_map/ppermute | solution.py:37
  227.6 2.7 %collective-permute-start.44 = (bf16[1,24,3072]{2,1,0:T(8,128)(2,1)S(1)}, bf16[1,24,3072]{2,1,0:T(8,128)(2,1)S(1)}, u32[]{:S(2)}, u32[]{:S(2)}) collective-permute-start(bf16[1,24,3072]{2,1,0:T(8,128)(2,1)S(1)} %get-tuple-element.281), channel_id=1, source_target_pairs={{0,16},{2,18},{4,20},{6,22},{8,24},{10,26},{12,28},{14,30},{16,0},... | collective-permute-start | bytes 442376 | tf_op jit(solution)/shard_map/ppermute | solution.py:37
  232.5 1.9 collective-permute-done.46
  (238 shorter events, 81.5 us)
Async XLA Ops:
  3.7 9.6 %collective-permute-start = (bf16[1,24,2304]{2,1,0:T(8,128)(2,1)S(1)}, bf16[1,24,2304]{2,1,0:T(8,128)(2,1)S(1)}, u32[]{:S(2)}, u32[]{:S(2)}) collective-permute-start(bf16[1,24,2304]{2,1,0:T(8,128)(2,1)S(1)} %bitcast.39), channel_id=1, source_target_pairs={{0,16},{2,18},{4,20},{6,22},{8,24},{10,26},{12,28},{14,30},{16,0},... | collective-permute-start | bytes 331784 | tf_op jit(solution)/shard_map/ppermute | solution.py:37
  13.3 10.6 %collective-permute-start.2 = (bf16[2,24,2304]{2,1,0:T(8,128)(2,1)S(1)}, bf16[2,24,2304]{2,1,0:T(8,128)(2,1)S(1)}, u32[]{:S(2)}, u32[]{:S(2)}) collective-permute-start(bf16[2,24,2304]{2,1,0:T(8,128)(2,1)S(1)} %pad_maximum_fusion.7), channel_id=1, source_target_pairs={{0,8},{2,10},{4,12},{6,14},{8,0},{10,2},{12,4},{14,6},{16,24},{18,... | collective-permute-start | bytes 663560 | tf_op jit(solution)/shard_map/ppermute | solution.py:37
  14.6 12.2 %collective-permute-start.1 = (bf16[1,24,3840]{2,1,0:T(8,128)(2,1)S(1)}, bf16[1,24,3840]{2,1,0:T(8,128)(2,1)S(1)}, u32[]{:S(2)}, u32[]{:S(2)}) collective-permute-start(bf16[1,24,3840]{2,1,0:T(8,128)(2,1)S(1)} %bitcast.42), channel_id=1, source_target_pairs={{0,16},{2,18},{4,20},{6,22},{8,24},{10,26},{12,28},{14,30},{16,0},... | collective-permute-start | bytes 552968 | tf_op jit(solution)/shard_map/ppermute | solution.py:37
  25.3 8.2 %collective-permute-start.5 = (bf16[4,24,1152]{2,1,0:T(8,128)(2,1)S(1)}, bf16[4,24,1152]{2,1,0:T(8,128)(2,1)S(1)}, u32[]{:S(2)}, u32[]{:S(2)}) collective-permute-start(bf16[4,24,1152]{2,1,0:T(8,128)(2,1)S(1)} %get-tuple-element.301), channel_id=1, source_target_pairs={{0,2},{2,0},{4,6},{6,4},{8,10},{10,8},{12,14},{14,12},{16,18},{18,... | collective-permute-start | bytes 663560 | tf_op jit(solution)/shard_map/ppermute | solution.py:37
  26.9 8.5 %collective-permute-start.3 = (bf16[2,24,3840]{2,1,0:T(8,128)(2,1)S(1)}, bf16[2,24,3840]{2,1,0:T(8,128)(2,1)S(1)}, u32[]{:S(2)}, u32[]{:S(2)}) collective-permute-start(bf16[2,24,3840]{2,1,0:T(8,128)(2,1)S(1)} %pad_maximum_fusion.6), channel_id=1, source_target_pairs={{0,8},{2,10},{4,12},{6,14},{8,0},{10,2},{12,4},{14,6},{16,24},{18,... | collective-permute-start | bytes 1105928 | tf_op jit(solution)/shard_map/ppermute | solution.py:37
  30.0 10.7 %collective-permute-start.6 = (bf16[8,24,1152]{2,1,0:T(8,128)(2,1)S(1)}, bf16[8,24,1152]{2,1,0:T(8,128)(2,1)S(1)}, u32[]{:S(2)}, u32[]{:S(2)}) collective-permute-start(bf16[8,24,1152]{2,1,0:T(8,128)(2,1)S(1)} %pad_maximum_fusion.4), channel_id=1, source_target_pairs={{0,2},{2,0},{4,6},{6,4},{8,10},{10,8},{12,14},{14,12},{16,18},{18,... | collective-permute-start | bytes 1327112 | tf_op jit(solution)/shard_map/ppermute | solution.py:37
  33.5 8.4 %collective-permute-start.7 = (bf16[8,24,1152]{2,1,0:T(8,128)(2,1)S(1)}, bf16[8,24,1152]{2,1,0:T(8,128)(2,1)S(1)}, u32[]{:S(2)}, u32[]{:S(2)}) collective-permute-start(bf16[8,24,1152]{2,1,0:T(8,128)(2,1)S(1)} %pad_maximum_fusion.5), channel_id=1, source_target_pairs={{0,4},{2,6},{4,0},{6,2},{8,12},{10,14},{12,8},{14,10},{16,20},{18,... | collective-permute-start | bytes 1327112 | tf_op jit(solution)/shard_map/ppermute | solution.py:37
  42.2 15.7 %collective-permute-start.11 = (bf16[2,16,24,1152]{3,2,1,0:T(8,128)(2,1)S(1)}, bf16[2,16,24,1152]{3,2,1,0:T(8,128)(2,1)S(1)}, u32[]{:S(2)}, u32[]{:S(2)}) collective-permute-start(bf16[2,16,24,1152]{3,2,1,0:T(8,128)(2,1)S(1)} %pad_maximum_fusion.2.own), channel_id=1, source_target_pairs={{0,1},{1,0},{2,3},{3,2},{4,5},{5,4},{6,7},{7,6},{8,9},{9,8},{10,11... | collective-permute-start | bytes 5308424 | tf_op jit(solution)/shard_map/ppermute | solution.py:40
  43.1 12.2 %collective-permute-start.10 = (bf16[1,96,768]{2,1,0:T(8,128)(2,1)S(1)}, bf16[1,96,768]{2,1,0:T(8,128)(2,1)S(1)}, u32[]{:S(2)}, u32[]{:S(2)}) collective-permute-start(bf16[1,96,768]{2,1,0:T(8,128)(2,1)S(1)} %bitcast.57), channel_id=1, source_target_pairs={{0,16},{2,18},{4,20},{6,22},{8,24},{10,26},{12,28},{14,30},{16,0},... | collective-permute-start | bytes 442376 | tf_op jit(solution)/shard_map/ppermute | solution.py:37
  44.3 10.1 %collective-permute-start.9 = (bf16[4,24,1920]{2,1,0:T(8,128)(2,1)S(1)}, bf16[4,24,1920]{2,1,0:T(8,128)(2,1)S(1)}, u32[]{:S(2)}, u32[]{:S(2)}) collective-permute-start(bf16[4,24,1920]{2,1,0:T(8,128)(2,1)S(1)} %get-tuple-element.158), channel_id=1, source_target_pairs={{0,2},{2,0},{4,6},{6,4},{8,10},{10,8},{12,14},{14,12},{16,18},{18,... | collective-permute-start | bytes 1105928 | tf_op jit(solution)/shard_map/ppermute | solution.py:37
  45.5 9.8 %collective-permute-start.8 = (bf16[4,24,1920]{2,1,0:T(8,128)(2,1)S(1)}, bf16[4,24,1920]{2,1,0:T(8,128)(2,1)S(1)}, u32[]{:S(2)}, u32[]{:S(2)}) collective-permute-start(bf16[4,24,1920]{2,1,0:T(8,128)(2,1)S(1)} %get-tuple-element.157), channel_id=1, source_target_pairs={{0,4},{2,6},{4,0},{6,2},{8,12},{10,14},{12,8},{14,10},{16,20},{18,... | collective-permute-start | bytes 1105928 | tf_op jit(solution)/shard_map/ppermute | solution.py:37
  55.3 16.8 %collective-permute-start.12 = (bf16[2,96,768]{2,1,0:T(8,128)(2,1)S(1)}, bf16[2,96,768]{2,1,0:T(8,128)(2,1)S(1)}, u32[]{:S(2)}, u32[]{:S(2)}) collective-permute-start(bf16[2,96,768]{2,1,0:T(8,128)(2,1)S(1)} %constant_dynamic-update-slice_fusion.6), channel_id=1, source_target_pairs={{0,8},{2,10},{4,12},{6,14},{8,0},{10,2},{12,4},{14,6},{16,24},{18,... | collective-permute-start | bytes 884744 | tf_op jit(solution)/shard_map/ppermute | solution.py:37
  57.9 16.6 %collective-permute-start.14 = (bf16[8,24,1920]{2,1,0:T(8,128)(2,1)S(1)}, bf16[8,24,1920]{2,1,0:T(8,128)(2,1)S(1)}, u32[]{:S(2)}, u32[]{:S(2)}) collective-permute-start(bf16[8,24,1920]{2,1,0:T(8,128)(2,1)S(1)} %constant_dynamic-update-slice_fusion.4), channel_id=1, source_target_pairs={{0,4},{2,6},{4,0},{6,2},{8,12},{10,14},{12,8},{14,10},{16,20},{18,... | collective-permute-start | bytes 2211848 | tf_op jit(solution)/shard_map/ppermute | solution.py:37
  58.9 16.3 %collective-permute-start.13 = (bf16[8,24,1920]{2,1,0:T(8,128)(2,1)S(1)}, bf16[8,24,1920]{2,1,0:T(8,128)(2,1)S(1)}, u32[]{:S(2)}, u32[]{:S(2)}) collective-permute-start(bf16[8,24,1920]{2,1,0:T(8,128)(2,1)S(1)} %constant_dynamic-update-slice_fusion.2), channel_id=1, source_target_pairs={{0,2},{2,0},{4,6},{6,4},{8,10},{10,8},{12,14},{14,12},{16,18},{18,... | collective-permute-start | bytes 2211848 | tf_op jit(solution)/shard_map/ppermute | solution.py:37
  75.8 9.5 %collective-permute-start.16 = (bf16[2,16,24,1920]{3,2,1,0:T(8,128)(2,1)S(1)}, bf16[2,16,24,1920]{3,2,1,0:T(8,128)(2,1)S(1)}, u32[]{:S(2)}, u32[]{:S(2)}) collective-permute-start(bf16[2,16,24,1920]{3,2,1,0:T(8,128)(2,1)S(1)} %pad_maximum_fusion.own), channel_id=1, source_target_pairs={{0,1},{1,0},{2,3},{3,2},{4,5},{5,4},{6,7},{7,6},{8,9},{9,8},{10,11... | collective-permute-start | bytes 8847368 | tf_op jit(solution)/shard_map/ppermute | solution.py:40
  75.9 9.4 %collective-permute-start.17 = (bf16[4,96,384]{2,1,0:T(8,128)(2,1)S(1)}, bf16[4,96,384]{2,1,0:T(8,128)(2,1)S(1)}, u32[]{:S(2)}, u32[]{:S(2)}) collective-permute-start(bf16[4,96,384]{2,1,0:T(8,128)(2,1)S(1)} %get-tuple-element.175), channel_id=1, source_target_pairs={{0,2},{2,0},{4,6},{6,4},{8,10},{10,8},{12,14},{14,12},{16,18},{18,... | collective-permute-start | bytes 884744 | tf_op jit(solution)/shard_map/ppermute | solution.py:37
  77.4 9.1 %collective-permute-start.15 = (bf16[4,96,384]{2,1,0:T(8,128)(2,1)S(1)}, bf16[4,96,384]{2,1,0:T(8,128)(2,1)S(1)}, u32[]{:S(2)}, u32[]{:S(2)}) collective-permute-start(bf16[4,96,384]{2,1,0:T(8,128)(2,1)S(1)} %get-tuple-element.172), channel_id=1, source_target_pairs={{0,4},{2,6},{4,0},{6,2},{8,12},{10,14},{12,8},{14,10},{16,20},{18,... | collective-permute-start | bytes 884744 | tf_op jit(solution)/shard_map/ppermute | solution.py:37
  86.5 15.1 %collective-permute-start.18 = (bf16[8,96,384]{2,1,0:T(8,128)(2,1)S(1)}, bf16[8,96,384]{2,1,0:T(8,128)(2,1)S(1)}, u32[]{:S(2)}, u32[]{:S(2)}) collective-permute-start(bf16[8,96,384]{2,1,0:T(8,128)(2,1)S(1)} %constant_dynamic-update-slice_fusion.10), channel_id=1, source_target_pairs={{0,2},{2,0},{4,6},{6,4},{8,10},{10,8},{12,14},{14,12},{16,18},{18,... | collective-permute-start | bytes 1769480 | tf_op jit(solution)/shard_map/ppermute | solution.py:37
  87.3 14.5 %collective-permute-start.19 = (bf16[8,96,384]{2,1,0:T(8,128)(2,1)S(1)}, bf16[8,96,384]{2,1,0:T(8,128)(2,1)S(1)}, u32[]{:S(2)}, u32[]{:S(2)}) collective-permute-start(bf16[8,96,384]{2,1,0:T(8,128)(2,1)S(1)} %constant_dynamic-update-slice_fusion.12), channel_id=1, source_target_pairs={{0,4},{2,6},{4,0},{6,2},{8,12},{10,14},{12,8},{14,10},{16,20},{18,... | collective-permute-start | bytes 1769480 | tf_op jit(solution)/shard_map/ppermute | solution.py:37
  130.0 15.7 %collective-permute-start.23 = (bf16[8,96,384]{2,1,0:T(8,128)(2,1)S(1)}, bf16[8,96,384]{2,1,0:T(8,128)(2,1)S(1)}, u32[]{:S(2)}, u32[]{:S(2)}) collective-permute-start(bf16[8,96,384]{2,1,0:T(8,128)(2,1)S(1)} %get-tuple-element.194), channel_id=1, source_target_pairs={{0,4},{2,6},{4,0},{6,2},{8,12},{10,14},{12,8},{14,10},{16,20},{18,... | collective-permute-start | bytes 1769480 | tf_op jit(solution)/shard_map/ppermute | solution.py:37
  131.1 15.3 %collective-permute-start.22 = (bf16[8,96,384]{2,1,0:T(8,128)(2,1)S(1)}, bf16[8,96,384]{2,1,0:T(8,128)(2,1)S(1)}, u32[]{:S(2)}, u32[]{:S(2)}) collective-permute-start(bf16[8,96,384]{2,1,0:T(8,128)(2,1)S(1)} %get-tuple-element.193), channel_id=1, source_target_pairs={{0,2},{2,0},{4,6},{6,4},{8,10},{10,8},{12,14},{14,12},{16,18},{18,... | collective-permute-start | bytes 1769480 | tf_op jit(solution)/shard_map/ppermute | solution.py:37
  137.2 21.2 %collective-permute-start.26 = (bf16[2,16,24,1536]{3,2,1,0:T(8,128)(2,1)S(1)}, bf16[2,16,24,1536]{3,2,1,0:T(8,128)(2,1)S(1)}, u32[]{:S(2)}, u32[]{:S(2)}) collective-permute-start(bf16[2,16,24,1536]{3,2,1,0:T(8,128)(2,1)S(1)} %get-tuple-element.196), channel_id=1, source_target_pairs={{0,1},{1,0},{2,3},{3,2},{4,5},{5,4},{6,7},{7,6},{8,9},{9,8},{10,11... | collective-permute-start | bytes 7077896 | tf_op jit(solution)/shard_map/ppermute | solution.py:40
  147.7 8.7 %collective-permute-start.25 = (bf16[4,96,384]{2,1,0:T(8,128)(2,1)S(1)}, bf16[4,96,384]{2,1,0:T(8,128)(2,1)S(1)}, u32[]{:S(2)}, u32[]{:S(2)}) collective-permute-start(bf16[4,96,384]{2,1,0:T(8,128)(2,1)S(1)} %get-tuple-element.202), channel_id=1, source_target_pairs={{0,2},{2,0},{4,6},{6,4},{8,10},{10,8},{12,14},{14,12},{16,18},{18,... | collective-permute-start | bytes 884744 | tf_op jit(solution)/shard_map/ppermute | solution.py:37
  158.0 14.5 %collective-permute-start.27 = (bf16[2,96,768]{2,1,0:T(8,128)(2,1)S(1)}, bf16[2,96,768]{2,1,0:T(8,128)(2,1)S(1)}, u32[]{:S(2)}, u32[]{:S(2)}) collective-permute-start(bf16[2,96,768]{2,1,0:T(8,128)(2,1)S(1)} %get-tuple-element.215), channel_id=1, source_target_pairs={{0,8},{2,10},{4,12},{6,14},{8,0},{10,2},{12,4},{14,6},{16,24},{18,... | collective-permute-start | bytes 884744 | tf_op jit(solution)/shard_map/ppermute | solution.py:37
  160.0 13.3 %collective-permute-start.29 = (bf16[8,24,1536]{2,1,0:T(8,128)(2,1)S(1)}, bf16[8,24,1536]{2,1,0:T(8,128)(2,1)S(1)}, u32[]{:S(2)}, u32[]{:S(2)}) collective-permute-start(bf16[8,24,1536]{2,1,0:T(8,128)(2,1)S(1)} %get-tuple-element.219), channel_id=1, source_target_pairs={{0,4},{2,6},{4,0},{6,2},{8,12},{10,14},{12,8},{14,10},{16,20},{18,... | collective-permute-start | bytes 1769480 | tf_op jit(solution)/shard_map/ppermute | solution.py:37
  161.0 13.4 %collective-permute-start.28 = (bf16[8,24,1536]{2,1,0:T(8,128)(2,1)S(1)}, bf16[8,24,1536]{2,1,0:T(8,128)(2,1)S(1)}, u32[]{:S(2)}, u32[]{:S(2)}) collective-permute-start(bf16[8,24,1536]{2,1,0:T(8,128)(2,1)S(1)} %get-tuple-element.218), channel_id=1, source_target_pairs={{0,2},{2,0},{4,6},{6,4},{8,10},{10,8},{12,14},{14,12},{16,18},{18,... | collective-permute-start | bytes 1769480 | tf_op jit(solution)/shard_map/ppermute | solution.py:37
  189.2 19.7 %collective-permute-start.38 = (bf16[8,24,1536]{2,1,0:T(8,128)(2,1)S(1)}, bf16[8,24,1536]{2,1,0:T(8,128)(2,1)S(1)}, u32[]{:S(2)}, u32[]{:S(2)}) collective-permute-start(bf16[8,24,1536]{2,1,0:T(8,128)(2,1)S(1)} %get-tuple-element.252), channel_id=1, source_target_pairs={{0,4},{2,6},{4,0},{6,2},{8,12},{10,14},{12,8},{14,10},{16,20},{18,... | collective-permute-start | bytes 1769480 | tf_op jit(solution)/shard_map/ppermute | solution.py:37
  190.3 18.6 %collective-permute-start.33 = (bf16[8,24,1536]{2,1,0:T(8,128)(2,1)S(1)}, bf16[8,24,1536]{2,1,0:T(8,128)(2,1)S(1)}, u32[]{:S(2)}, u32[]{:S(2)}) collective-permute-start(bf16[8,24,1536]{2,1,0:T(8,128)(2,1)S(1)} %get-tuple-element.249), channel_id=1, source_target_pairs={{0,2},{2,0},{4,6},{6,4},{8,10},{10,8},{12,14},{14,12},{16,18},{18,... | collective-permute-start | bytes 1769480 | tf_op jit(solution)/shard_map/ppermute | solution.py:37
  191.3 8.4 %collective-permute-start.34 = (bf16[2,24,3072]{2,1,0:T(8,128)(2,1)S(1)}, bf16[2,24,3072]{2,1,0:T(8,128)(2,1)S(1)}, u32[]{:S(2)}, u32[]{:S(2)}) collective-permute-start(bf16[2,24,3072]{2,1,0:T(8,128)(2,1)S(1)} %get-tuple-element.241), channel_id=1, source_target_pairs={{0,8},{2,10},{4,12},{6,14},{8,0},{10,2},{12,4},{14,6},{16,24},{18,... | collective-permute-start | bytes 884744 | tf_op jit(solution)/shard_map/ppermute | solution.py:37
  200.4 8.5 %collective-permute-start.37 = (bf16[1,24,3072]{2,1,0:T(8,128)(2,1)S(1)}, bf16[1,24,3072]{2,1,0:T(8,128)(2,1)S(1)}, u32[]{:S(2)}, u32[]{:S(2)}) collective-permute-start(bf16[1,24,3072]{2,1,0:T(8,128)(2,1)S(1)} %get-tuple-element.266), channel_id=1, source_target_pairs={{0,16},{2,18},{4,20},{6,22},{8,24},{10,26},{12,28},{14,30},{16,0},... | collective-permute-start | bytes 442376 | tf_op jit(solution)/shard_map/ppermute | solution.py:37
  211.3 9.2 %collective-permute-start.45 = (bf16[1,96,768]{2,1,0:T(8,128)(2,1)S(1)}, bf16[1,96,768]{2,1,0:T(8,128)(2,1)S(1)}, u32[]{:S(2)}, u32[]{:S(2)}) collective-permute-start(bf16[1,96,768]{2,1,0:T(8,128)(2,1)S(1)} %get-tuple-element.225), channel_id=1, source_target_pairs={{0,16},{2,18},{4,20},{6,22},{8,24},{10,26},{12,28},{14,30},{16,0},... | collective-permute-start | bytes 442376 | tf_op jit(solution)/shard_map/ppermute | solution.py:37
  227.6 8.1 %collective-permute-start.44 = (bf16[1,24,3072]{2,1,0:T(8,128)(2,1)S(1)}, bf16[1,24,3072]{2,1,0:T(8,128)(2,1)S(1)}, u32[]{:S(2)}, u32[]{:S(2)}) collective-permute-start(bf16[1,24,3072]{2,1,0:T(8,128)(2,1)S(1)} %get-tuple-element.281), channel_id=1, source_target_pairs={{0,16},{2,18},{4,20},{6,22},{8,24},{10,26},{12,28},{14,30},{16,0},... | collective-permute-start | bytes 442376 | tf_op jit(solution)/shard_map/ppermute | solution.py:37
  (60 other events, 460.6 us)
